TPU v7x, 32 devices: a whole 2x2x4 slice. The times are simulated.
32 devices in a mesh: shots: 2 (over x), blk: 16 (over z, y, core).
Axes of the slice: x: 2, y: 2, z: 4, core: 2. Of those that a mesh axis runs over, the one named last changes fastest.
Arguments:
- source_prev: float32 [32, 8, 64, 256], P(('shots', 'blk')), parts along dimension 0, may hold values from -8 to 8
- source_cur: float32 [32, 8, 64, 256], P(('shots', 'blk')), parts along dimension 0, may hold values from -8 to 8
- receiver_prev: float32 [32, 8, 64, 256], P(('shots', 'blk')), parts along dimension 0, may hold values from -8 to 8
- receiver_cur: float32 [32, 8, 64, 256], P(('shots', 'blk')), parts along dimension 0, may hold values from -8 to 8
- coef_horiz: float32 [16, 8, 64, 256], P('blk'), may hold values from 0.08 to 0.2
- coef_vert: float32 [16, 8, 64, 256], P('blk'), may hold values from 0.04 to 0.1
- coef_mixed: float32 [16, 8, 64, 256], P('blk'), may hold values from -0.05 to 0.05
- live_depth: int32 [16, 8, 64], P('blk'), may hold values from 1 to 256
- offsets: int32 [9], replicated, may hold values from 0 to 8, each once
- image_in: float32 [9, 32, 8, 64, 256], P(None, ('shots', 'blk')), parts along dimension 1, may hold values from -6 to 6
Outputs:
- image_out: float32 [9, 32, 8, 64, 256], P(None, ('shots', 'blk')), parts along dimension 1
- source_last: float32 [32, 8, 64, 256], P(('shots', 'blk')), parts along dimension 0
- receiver_last: float32 [32, 8, 64, 256], P(('shots', 'blk')), parts along dimension 0
There are 2 independent parts, one for each index of `shots`. A program takes and returns all parts, laid end to end along the dimension named above; an argument that names none is the same for every part. Nothing has to cross between parts.
Inputs may be any that keep to these rules, and one draw needn't show every extreme that they name: offsets holds every value from 0 to 8 once.
All inputs are finite; a program needn't handle non-finite values.
Results may differ from a plain program's by a relative error of at most 0.0003.
Values sent between devices are 32-bit elements; how exact they have to be, the bound alone decides.
No kernel may reach another device: no remote copies, remote signals or barrier semaphores. Data moves between devices by JAX's collectives and lax.ppermute only.
A program may use at most 64 MiB of HBM per device.

v0:
```python
import jax
import jax.numpy as jnp
from jax import lax
from jax.sharding import PartitionSpec as P

STEPS = 4
RAD = 4
HMAX = 4
NOFF = 9


second_w = (-205.0 / 72.0, 8.0 / 5.0, -1.0 / 5.0, 8.0 / 315.0, -1.0 / 560.0)
first_w = (4.0 / 5.0, -1.0 / 5.0, 4.0 / 105.0, -1.0 / 280.0)


def from_behind(value, axis, steps):
    count = lax.axis_size(axis)
    first, last = (max(0, -steps), min(count, count - steps))
    return lax.ppermute(value, axis, [(source, source + steps) for source in range(first, last)])


def stencil(padded_xy, coef_horiz, coef_vert, coef_mixed):
    count_x = padded_xy.shape[0] - 8
    count_y = padded_xy.shape[1] - 8
    depth = padded_xy.shape[2]
    padded = jnp.pad(padded_xy, ((0, 0), (0, 0), (4, 4)))

    def take(a, b, c):
        return padded[4 + a : 4 + a + count_x, 4 + b : 4 + b + count_y, 4 + c : 4 + c + depth]

    center = take(0, 0, 0)
    horiz = 2.0 * second_w[0] * center
    vert = second_w[0] * center
    deriv_z = jnp.zeros((count_x + 8, count_y, depth), jnp.float32)
    for k in range(1, 5):
        horiz = horiz + second_w[k] * (
            take(k, 0, 0) + take(-k, 0, 0) + take(0, k, 0) + take(0, -k, 0)
        )
        vert = vert + second_w[k] * (take(0, 0, k) + take(0, 0, -k))
        deriv_z = deriv_z + first_w[k - 1] * (
            padded[:, 4 : 4 + count_y, 4 + k : 4 + k + depth]
            - padded[:, 4 : 4 + count_y, 4 - k : 4 - k + depth]
        )
    mixed = jnp.zeros((count_x, count_y, depth), jnp.float32)
    for k in range(1, 5):
        mixed = mixed + first_w[k - 1] * (
            deriv_z[4 + k : 4 + k + count_x] - deriv_z[4 - k : 4 - k + count_x]
        )
    return coef_horiz * horiz + coef_vert * vert + coef_mixed * mixed


def image_terms(src_pad, rec_pad, width, offsets, mute):
    count = mute.shape[0]
    terms = []
    for slot in range(NOFF):
        shift = offsets[slot] - HMAX
        left = lax.dynamic_slice_in_dim(src_pad, width - shift, count, 0)
        right = lax.dynamic_slice_in_dim(rec_pad, width + shift, count, 0)
        terms.append(mute * left * right)
    return jnp.stack(terms)


def wave_rims(field, xdim):
    ydim = xdim + 1
    size_x = field.shape[xdim]
    from_below = from_behind(lax.slice_in_dim(field, size_x - RAD, size_x, axis=xdim), "blk", 1)
    from_above = from_behind(lax.slice_in_dim(field, 0, RAD, axis=xdim), "blk", -1)
    joined = jnp.concatenate([from_below, field, from_above], xdim)
    widths = [(0, 0)] * field.ndim
    widths[ydim] = (RAD, RAD)
    return jnp.pad(joined, widths)


def snap_rims(snaps):
    size_x = snaps.shape[1]
    from_below = from_behind(snaps[:, size_x - HMAX :], "blk", 1)
    from_above = from_behind(snaps[:, :HMAX], "blk", -1)
    return jnp.concatenate([from_below, snaps, from_above], 1)


def wave_pads(source_cur, receiver_cur):
    return (wave_rims(source_cur, 0), wave_rims(receiver_cur, 0))


def per_device(
    source_prev,
    source_cur,
    receiver_prev,
    receiver_cur,
    coef_horiz,
    coef_vert,
    coef_mixed,
    live_depth,
    offsets,
    image_in,
):
    source_prev = source_prev[0]
    source_cur = source_cur[0]
    receiver_prev = receiver_prev[0]
    receiver_cur = receiver_cur[0]
    coef_horiz = coef_horiz[0]
    coef_vert = coef_vert[0]
    coef_mixed = coef_mixed[0]
    span_y = source_cur.shape[1]
    depth_ids = lax.broadcasted_iota(jnp.int32, source_cur.shape, 2)
    mute = (depth_ids < live_depth[0][:, :, None]).astype(jnp.float32)
    image = image_in[:, 0]
    half_steps = STEPS // 2
    for step in range(STEPS):
        src_pad, rec_pad = wave_pads(source_cur, receiver_cur)
        if step > 0 and step % half_steps == 0:
            image = image + image_terms(
                src_pad[:, RAD : RAD + span_y], rec_pad[:, RAD : RAD + span_y], RAD, offsets, mute
            )
        src_new = (
            2.0 * source_cur - source_prev + stencil(src_pad, coef_horiz, coef_vert, coef_mixed)
        )
        rec_new = (
            2.0 * receiver_cur - receiver_prev + stencil(rec_pad, coef_horiz, coef_vert, coef_mixed)
        )
        source_prev, source_cur = (source_cur, src_new)
        receiver_prev, receiver_cur = (receiver_cur, rec_new)
        if (step + 1) % half_steps == 0:
            if step + 1 == STEPS:
                snap_pad = snap_rims(jnp.stack([source_cur, receiver_cur]))
                image = image + image_terms(snap_pad[0], snap_pad[1], HMAX, offsets, mute)
    return (image[:, None], source_cur[None], receiver_cur[None])


def solution(mesh):
    in_specs = (
        P(("shots", "blk"), None, None, None),
        P(("shots", "blk"), None, None, None),
        P(("shots", "blk"), None, None, None),
        P(("shots", "blk"), None, None, None),
        P("blk", None, None, None),
        P("blk", None, None, None),
        P("blk", None, None, None),
        P("blk", None, None),
        P(),
        P(None, ("shots", "blk"), None, None, None),
    )
    out_specs = (
        P(None, ("shots", "blk"), None, None, None),
        P(("shots", "blk"), None, None, None),
        P(("shots", "blk"), None, None, None),
    )
    return jax.shard_map(
        per_device, mesh=mesh, in_specs=in_specs, out_specs=out_specs, check_vma=False
    )
```

profile of v0, /device:TPU:1, one launch (start us, length us, event | category | flops | bytes accessed | tf_op | source)
XLA Modules:
  0.0 127.1 jit_solution(8926772650504436230)
XLA Ops:
  0.7 1.2 slice_bitcast_fusion.1
  1.8 2.0 %collective-permute-start.6 = (f32[4,64,256]{2,1,0:T(8,128)S(1)}, f32[4,64,256]{2,1,0:T(8,128)S(1)}, u32[]{:S(2)}, u32[]{:S(2)}) collective-permute-start(f32[4,64,256]{2,1,0:T(8,128)S(1)} %get-tuple-element.21), channel_id=1, source_target_pairs={{1,0},{2,1},{3,2},{4,3},{5,4},{6,5},{7,6},{8,7},{9,8},{10,9},{11,1... | collective-permute-start | bytes 786440 | tf_op jit(solution)/shard_map/ppermute | solution.py:19
  3.8 4.5 %collective-permute-start.7 = (f32[4,64,256]{2,1,0:T(8,128)S(1)}, f32[4,64,256]{2,1,0:T(8,128)S(1)}, u32[]{:S(2)}, u32[]{:S(2)}) collective-permute-start(f32[4,64,256]{2,1,0:T(8,128)S(1)} %get-tuple-element.22), channel_id=1, source_target_pairs={{0,1},{1,2},{2,3},{3,4},{4,5},{5,6},{6,7},{7,8},{8,9},{9,10},{10,1... | collective-permute-start | bytes 786440 | tf_op jit(solution)/shard_map/ppermute | solution.py:19
  8.3 1.9 %collective-permute-start = (f32[4,64,256]{2,1,0:T(8,128)S(1)}, f32[4,64,256]{2,1,0:T(8,128)S(1)}, u32[]{:S(2)}, u32[]{:S(2)}) collective-permute-start(f32[4,64,256]{2,1,0:T(8,128)S(1)} %get-tuple-element.13), channel_id=1, source_target_pairs={{1,0},{2,1},{3,2},{4,3},{5,4},{6,5},{7,6},{8,7},{9,8},{10,9},{11,1... | collective-permute-start | bytes 786440 | tf_op jit(solution)/shard_map/ppermute | solution.py:19
  10.3 3.6 %collective-permute-start.1 = (f32[4,64,256]{2,1,0:T(8,128)S(1)}, f32[4,64,256]{2,1,0:T(8,128)S(1)}, u32[]{:S(2)}, u32[]{:S(2)}) collective-permute-start(f32[4,64,256]{2,1,0:T(8,128)S(1)} %get-tuple-element.14), channel_id=1, source_target_pairs={{0,1},{1,2},{2,3},{3,4},{4,5},{5,6},{6,7},{7,8},{8,9},{9,10},{10,1... | collective-permute-start | bytes 786440 | tf_op jit(solution)/shard_map/ppermute | solution.py:19
  14.0 0.1 select_maximum_fusion.6
  14.1 2.3 %fusion.27 = f32[16,64,256]{2,1,0:T(8,128)S(1)} fusion(f32[16,72,256]{2,1,0:T(8,128)S(1)} %select_maximum_fusion.6), kind=kLoop, calls=%fused_computation.219 | loop fusion | flops 2883584 | bytes 2228224 | tf_op jit(solution)/shard_map/add | solution.py:40
  16.5 1.8 %fusion.231 = f32[8,64,256]{2,1,0:T(8,128)S(1)} fusion(f32[8,64,256]{2,1,0:T(8,128)S(1)} %bitcast.98, f32[4,64,256]{2,1,0:T(8,128)S(1)} %collective-permute-done.7, f32[4,64,256]{2,1,0:T(8,128)S(1)} %collective-permute-done.6, f32[16,72,256]{2,1,0:T(8,128)S(1)} %select_maximum_fusion.6, f32[16,64,256]{2,1,0:T(8,128)S(1)} %fusion.27, ...), kind=kLoop, calls=%fused_computation.475 | loop fusion | flops 7995392 | bytes 13238272 | tf_op jit(solution)/shard_map/add | solution.py:119
  18.3 1.9 %collective-permute-start.8 = (f32[4,64,256]{2,1,0:T(8,128)S(1)}, f32[4,64,256]{2,1,0:T(8,128)S(1)}, u32[]{:S(2)}, u32[]{:S(2)}) collective-permute-start(f32[4,64,256]{2,1,0:T(8,128)S(1)} %get-tuple-element.19), channel_id=1, source_target_pairs={{1,0},{2,1},{3,2},{4,3},{5,4},{6,5},{7,6},{8,7},{9,8},{10,9},{11,1... | collective-permute-start | bytes 786440 | tf_op jit(solution)/shard_map/ppermute | solution.py:19
  20.2 3.8 %collective-permute-start.9 = (f32[4,64,256]{2,1,0:T(8,128)S(1)}, f32[4,64,256]{2,1,0:T(8,128)S(1)}, u32[]{:S(2)}, u32[]{:S(2)}) collective-permute-start(f32[4,64,256]{2,1,0:T(8,128)S(1)} %get-tuple-element.20), channel_id=1, source_target_pairs={{0,1},{1,2},{2,3},{3,4},{4,5},{5,6},{6,7},{7,8},{8,9},{9,10},{10,1... | collective-permute-start | bytes 786440 | tf_op jit(solution)/shard_map/ppermute | solution.py:19
  24.1 0.1 select_maximum_fusion.10
  24.2 2.3 %fusion.5 = f32[16,64,256]{2,1,0:T(8,128)S(1)} fusion(f32[16,72,256]{2,1,0:T(8,128)S(1)} %select_maximum_fusion.10), kind=kLoop, calls=%fused_computation.197 | loop fusion | flops 2883584 | bytes 2228224 | tf_op jit(solution)/shard_map/add | solution.py:40
  26.5 1.8 %fusion.283 = f32[8,64,256]{2,1,0:T(8,128)S(1)} fusion(f32[8,64,256]{2,1,0:T(8,128)S(1)} %bitcast.100, f32[4,64,256]{2,1,0:T(8,128)S(1)} %collective-permute-done.1, f32[4,64,256]{2,1,0:T(8,128)S(1)} %collective-permute-done, f32[16,72,256]{2,1,0:T(8,128)S(1)} %select_maximum_fusion.10, f32[16,64,256]{2,1,0:T(8,128)S(1)} %fusion.5, ...), kind=kLoop, calls=%fused_computation.527 | loop fusion | flops 7995392 | bytes 13238272 | tf_op jit(solution)/shard_map/add | solution.py:116
  28.3 1.9 %collective-permute-start.2 = (f32[4,64,256]{2,1,0:T(8,128)S(1)}, f32[4,64,256]{2,1,0:T(8,128)S(1)}, u32[]{:S(2)}, u32[]{:S(2)}) collective-permute-start(f32[4,64,256]{2,1,0:T(8,128)S(1)} %get-tuple-element.11), channel_id=1, source_target_pairs={{1,0},{2,1},{3,2},{4,3},{5,4},{6,5},{7,6},{8,7},{9,8},{10,9},{11,1... | collective-permute-start | bytes 786440 | tf_op jit(solution)/shard_map/ppermute | solution.py:19
  30.2 3.6 %collective-permute-start.3 = (f32[4,64,256]{2,1,0:T(8,128)S(1)}, f32[4,64,256]{2,1,0:T(8,128)S(1)}, u32[]{:S(2)}, u32[]{:S(2)}) collective-permute-start(f32[4,64,256]{2,1,0:T(8,128)S(1)} %get-tuple-element.12), channel_id=1, source_target_pairs={{0,1},{1,2},{2,3},{3,4},{4,5},{5,6},{6,7},{7,8},{8,9},{9,10},{10,1... | collective-permute-start | bytes 786440 | tf_op jit(solution)/shard_map/ppermute | solution.py:19
  33.9 0.1 select_maximum_fusion.4
  34.0 2.3 %fusion.38 = f32[16,64,256]{2,1,0:T(8,128)S(1)} fusion(f32[16,72,256]{2,1,0:T(8,128)S(1)} %select_maximum_fusion.4), kind=kLoop, calls=%fused_computation.230 | loop fusion | flops 2883584 | bytes 2228224 | tf_op jit(solution)/shard_map/add | solution.py:40
  36.3 1.8 %fusion.205 = f32[8,64,256]{2,1,0:T(8,128)S(1)} fusion(f32[8,64,256]{2,1,0:T(8,128)S(1)} %fusion.231, f32[4,64,256]{2,1,0:T(8,128)S(1)} %collective-permute-done.9, f32[4,64,256]{2,1,0:T(8,128)S(1)} %collective-permute-done.8, f32[16,72,256]{2,1,0:T(8,128)S(1)} %select_maximum_fusion.4, f32[16,64,256]{2,1,0:T(8,128)S(1)} %fusion.38, ...), kind=kLoop, calls=%fused_computation.449 | loop fusion | flops 7995392 | bytes 13238272 | tf_op jit(solution)/shard_map/add | solution.py:119
  38.1 4.3 %collective-permute-start.10 = (f32[4,64,256]{2,1,0:T(8,128)S(1)}, f32[4,64,256]{2,1,0:T(8,128)S(1)}, u32[]{:S(2)}, u32[]{:S(2)}) collective-permute-start(f32[4,64,256]{2,1,0:T(8,128)S(1)} %get-tuple-element.18), channel_id=1, source_target_pairs={{0,1},{1,2},{2,3},{3,4},{4,5},{5,6},{6,7},{7,8},{8,9},{9,10},{10,1... | collective-permute-start | bytes 786440 | tf_op jit(solution)/shard_map/ppermute | solution.py:19
  42.4 2.1 %collective-permute-start.11 = (f32[4,64,256]{2,1,0:T(8,128)S(1)}, f32[4,64,256]{2,1,0:T(8,128)S(1)}, u32[]{:S(2)}, u32[]{:S(2)}) collective-permute-start(f32[4,64,256]{2,1,0:T(8,128)S(1)} %get-tuple-element.17), channel_id=1, source_target_pairs={{1,0},{2,1},{3,2},{4,3},{5,4},{6,5},{7,6},{8,7},{9,8},{10,9},{11,1... | collective-permute-start | bytes 786440 | tf_op jit(solution)/shard_map/ppermute | solution.py:19
  44.5 0.1 select_maximum_fusion.8
  44.7 2.3 %fusion.16 = f32[16,64,256]{2,1,0:T(8,128)S(1)} fusion(f32[16,72,256]{2,1,0:T(8,128)S(1)} %select_maximum_fusion.8), kind=kLoop, calls=%fused_computation.208 | loop fusion | flops 2883584 | bytes 2228224 | tf_op jit(solution)/shard_map/add | solution.py:40
  47.0 1.8 %fusion.257 = f32[8,64,256]{2,1,0:T(8,128)S(1)} fusion(f32[8,64,256]{2,1,0:T(8,128)S(1)} %fusion.283, f32[4,64,256]{2,1,0:T(8,128)S(1)} %collective-permute-done.3, f32[4,64,256]{2,1,0:T(8,128)S(1)} %collective-permute-done.2, f32[16,72,256]{2,1,0:T(8,128)S(1)} %select_maximum_fusion.8, f32[16,64,256]{2,1,0:T(8,128)S(1)} %fusion.16, ...), kind=kLoop, calls=%fused_computation.501 | loop fusion | flops 7995392 | bytes 13238272 | tf_op jit(solution)/shard_map/add | solution.py:116
  48.8 4.5 %collective-permute-start.4 = (f32[4,64,256]{2,1,0:T(8,128)S(1)}, f32[4,64,256]{2,1,0:T(8,128)S(1)}, u32[]{:S(2)}, u32[]{:S(2)}) collective-permute-start(f32[4,64,256]{2,1,0:T(8,128)S(1)} %get-tuple-element.10), channel_id=1, source_target_pairs={{0,1},{1,2},{2,3},{3,4},{4,5},{5,6},{6,7},{7,8},{8,9},{9,10},{10,1... | collective-permute-start | bytes 786440 | tf_op jit(solution)/shard_map/ppermute | solution.py:19
  53.3 1.9 %collective-permute-start.5 = (f32[4,64,256]{2,1,0:T(8,128)S(1)}, f32[4,64,256]{2,1,0:T(8,128)S(1)}, u32[]{:S(2)}, u32[]{:S(2)}) collective-permute-start(f32[4,64,256]{2,1,0:T(8,128)S(1)} %get-tuple-element.9), channel_id=1, source_target_pairs={{1,0},{2,1},{3,2},{4,3},{5,4},{6,5},{7,6},{8,7},{9,8},{10,9},{11,1... | collective-permute-start | bytes 786440 | tf_op jit(solution)/shard_map/ppermute | solution.py:19
  55.3 0.1 pad_maximum_fusion.2
  55.4 0.1 pad.62
  55.5 2.3 %fusion.71 = f32[16,64,256]{2,1,0:T(8,128)S(1)} fusion(f32[16,72,256]{2,1,0:T(8,128)S(1)} %pad.62), kind=kLoop, calls=%fused_computation.263 | loop fusion | flops 2883584 | bytes 2228224 | tf_op jit(solution)/shard_map/add | solution.py:40
  57.8 1.8 %fusion.126 = f32[8,64,256]{2,1,0:T(8,128)S(1)} fusion(f32[8,64,256]{2,1,0:T(8,128)S(1)} %fusion.205, f32[4,64,256]{2,1,0:T(8,128)S(1)} %collective-permute-done.10, f32[4,64,256]{2,1,0:T(8,128)S(1)} %collective-permute-done.11, f32[16,72,256]{2,1,0:T(8,128)S(1)} %pad.62, f32[16,64,256]{2,1,0:T(8,128)S(1)} %fusion.71, f32[1,8,64,256]{3,2,1,0:T(8,128)S(1)} %copy-done, ...), kind=kLoop, calls=%fused_computation.370 | loop fusion | flops 7995392 | bytes 13238272 | tf_op jit(solution)/shard_map/add | solution.py:119
  59.6 1.9 %collective-permute-start.14 = (f32[4,64,256]{2,1,0:T(8,128)S(1)}, f32[4,64,256]{2,1,0:T(8,128)S(1)}, u32[]{:S(2)}, u32[]{:S(2)}) collective-permute-start(f32[4,64,256]{2,1,0:T(8,128)S(1)} %get-tuple-element.15), channel_id=1, source_target_pairs={{1,0},{2,1},{3,2},{4,3},{5,4},{6,5},{7,6},{8,7},{9,8},{10,9},{11,1... | collective-permute-start | bytes 786440 | tf_op jit(solution)/shard_map/ppermute | solution.py:19
  61.5 3.6 %collective-permute-start.15 = (f32[4,64,256]{2,1,0:T(8,128)S(1)}, f32[4,64,256]{2,1,0:T(8,128)S(1)}, u32[]{:S(2)}, u32[]{:S(2)}) collective-permute-start(f32[4,64,256]{2,1,0:T(8,128)S(1)} %get-tuple-element.16), channel_id=1, source_target_pairs={{0,1},{1,2},{2,3},{3,4},{4,5},{5,6},{6,7},{7,8},{8,9},{9,10},{10,1... | collective-permute-start | bytes 786440 | tf_op jit(solution)/shard_map/ppermute | solution.py:19
  65.2 0.1 pad_maximum_fusion.1
  65.3 0.1 pad.58
  65.4 2.3 %fusion.49 = f32[16,64,256]{2,1,0:T(8,128)S(1)} fusion(f32[16,72,256]{2,1,0:T(8,128)S(1)} %pad.58), kind=kLoop, calls=%fused_computation.241 | loop fusion | flops 2883584 | bytes 2228224 | tf_op jit(solution)/shard_map/add | solution.py:40
  67.7 1.8 %fusion.179 = f32[8,64,256]{2,1,0:T(8,128)S(1)} fusion(f32[8,64,256]{2,1,0:T(8,128)S(1)} %fusion.257, f32[4,64,256]{2,1,0:T(8,128)S(1)} %collective-permute-done.4, f32[4,64,256]{2,1,0:T(8,128)S(1)} %collective-permute-done.5, f32[16,72,256]{2,1,0:T(8,128)S(1)} %pad.58, f32[16,64,256]{2,1,0:T(8,128)S(1)} %fusion.49, f32[1,8,64,256]{3,2,1,0:T(8,128)S(1)} %copy-done, ...), kind=kLoop, calls=%fused_computation.423 | loop fusion | flops 7995392 | bytes 13238272 | tf_op jit(solution)/shard_map/add | solution.py:116
  69.5 1.9 %collective-permute-start.12 = (f32[4,64,256]{2,1,0:T(8,128)S(1)}, f32[4,64,256]{2,1,0:T(8,128)S(1)}, u32[]{:S(2)}, u32[]{:S(2)}) collective-permute-start(f32[4,64,256]{2,1,0:T(8,128)S(1)} %get-tuple-element.7), channel_id=1, source_target_pairs={{1,0},{2,1},{3,2},{4,3},{5,4},{6,5},{7,6},{8,7},{9,8},{10,9},{11,1... | collective-permute-start | bytes 786440 | tf_op jit(solution)/shard_map/ppermute | solution.py:19
  71.4 3.9 %collective-permute-start.13 = (f32[4,64,256]{2,1,0:T(8,128)S(1)}, f32[4,64,256]{2,1,0:T(8,128)S(1)}, u32[]{:S(2)}, u32[]{:S(2)}) collective-permute-start(f32[4,64,256]{2,1,0:T(8,128)S(1)} %get-tuple-element.8), channel_id=1, source_target_pairs={{0,1},{1,2},{2,3},{3,4},{4,5},{5,6},{6,7},{7,8},{8,9},{9,10},{10,1... | collective-permute-start | bytes 786440 | tf_op jit(solution)/shard_map/ppermute | solution.py:19
  75.3 0.1 select_maximum_fusion
  75.5 2.3 %fusion.82 = f32[16,64,256]{2,1,0:T(8,128)S(1)} fusion(f32[16,72,256]{2,1,0:T(8,128)S(1)} %select_maximum_fusion), kind=kLoop, calls=%fused_computation.274 | loop fusion | flops 2883584 | bytes 2228224 | tf_op jit(solution)/shard_map/add | solution.py:40
  77.8 3.4 %collective-permute-done.13 = f32[4,64,256]{2,1,0:T(8,128)S(1)} collective-permute-done((f32[4,64,256]{2,1,0:T(8,128)S(1)}, f32[4,64,256]{2,1,0:T(8,128)S(1)}, u32[]{:S(2)}, u32[]{:S(2)}) %collective-permute-start.13) | collective-permute-done | bytes 262176 | tf_op jit(solution)/shard_map/ppermute | solution.py:19
  81.2 0.1 select_maximum_fusion.2
  81.3 2.3 %fusion.60 = f32[16,64,256]{2,1,0:T(8,128)S(1)} fusion(f32[16,72,256]{2,1,0:T(8,128)S(1)} %select_maximum_fusion.2), kind=kLoop, calls=%fused_computation.252 | loop fusion | flops 2883584 | bytes 2228224 | tf_op jit(solution)/shard_map/add | solution.py:40
  83.6 1.8 %fusion.100 = f32[1,8,64,256]{3,2,1,0:T(8,128)S(1)} fusion(f32[8,64,256]{2,1,0:T(8,128)S(1)} %fusion.126, f32[4,64,256]{2,1,0:T(8,128)S(1)} %collective-permute-done.15, f32[4,64,256]{2,1,0:T(8,128)S(1)} %collective-permute-done.14, f32[16,72,256]{2,1,0:T(8,128)S(1)} %select_maximum_fusion, f32[16,64,256]{2,1,0:T(8,128)S(1)} %fusion.82, ...), kind=kLoop, calls=%fused_computation.344 | loop fusion | flops 7995392 | bytes 13238272 | tf_op jit(solution)/shard_map/stack | solution.py:125
  85.4 1.8 %fusion.153 = f32[1,8,64,256]{3,2,1,0:T(8,128)S(1)} fusion(f32[8,64,256]{2,1,0:T(8,128)S(1)} %fusion.179, f32[4,64,256]{2,1,0:T(8,128)S(1)} %collective-permute-done.13, f32[4,64,256]{2,1,0:T(8,128)S(1)} %collective-permute-done.12, f32[16,72,256]{2,1,0:T(8,128)S(1)} %select_maximum_fusion.2, f32[16,64,256]{2,1,0:T(8,128)S(1)} %fusion.60, ...), kind=kLoop, calls=%fused_computation.397 | loop fusion | flops 7995392 | bytes 13238272 | tf_op jit(solution)/shard_map/stack | solution.py:125
  87.2 1.1 fusion.299
  88.3 4.4 %collective-permute-start.16 = (f32[2,4,64,256]{3,2,1,0:T(8,128)}, f32[2,4,64,256]{3,2,1,0:T(8,128)}, u32[]{:S(2)}, u32[]{:S(2)}) collective-permute-start(f32[2,4,64,256]{3,2,1,0:T(8,128)} %get-tuple-element.5), channel_id=1, source_target_pairs={{0,1},{1,2},{2,3},{3,4},{4,5},{5,6},{6,7},{7,8},{8,9},{9,10},{10,1... | collective-permute-start | bytes 1572872 | tf_op jit(solution)/shard_map/ppermute | solution.py:19
  92.7 1.9 %collective-permute-start.17 = (f32[2,4,64,256]{3,2,1,0:T(8,128)}, f32[2,4,64,256]{3,2,1,0:T(8,128)}, u32[]{:S(2)}, u32[]{:S(2)}) collective-permute-start(f32[2,4,64,256]{3,2,1,0:T(8,128)} %get-tuple-element.6), channel_id=1, source_target_pairs={{1,0},{2,1},{3,2},{4,3},{5,4},{6,5},{7,6},{8,7},{9,8},{10,9},{11,1... | collective-permute-start | bytes 1572872 | tf_op jit(solution)/shard_map/ppermute | solution.py:19
  94.6 0.7 fusion.495
  118.1 0.1 bitcast_dynamic-update-slice_fusion.17
  118.3 1.4 %pad_maximum_fusion = f32[2,16,64,256]{3,2,1,0:T(8,128)S(1)} fusion(f32[2,4,64,256]{3,2,1,0:T(8,128)} %collective-permute-done.17, f32[1,8,64,256]{3,2,1,0:T(8,128)S(1)} %fusion.100, f32[1,8,64,256]{3,2,1,0:T(8,128)S(1)} %fusion.153, f32[2,4,64,256]{3,2,1,0:T(8,128)} %collective-permute-done.16), kind=kLoop, calls=%fused_computation.129 | loop fusion | flops 1572864 | bytes 4194304 | tf_op jit(solution)/shard_map/concatenate | solution.py:78
  119.7 0.1 fusion.488
  119.8 0.2 bitcast_dynamic-update-slice_fusion.16
  120.1 0.2 bitcast_dynamic-update-slice_fusion.15
  120.3 0.2 bitcast_dynamic-update-slice_fusion.14
  120.5 0.2 bitcast_dynamic-update-slice_fusion.13
  120.8 0.2 bitcast_dynamic-update-slice_fusion.12
  121.0 0.2 bitcast_dynamic-update-slice_fusion.11
  121.3 0.0 slice-start.1
  121.3 0.2 bitcast_dynamic-update-slice_fusion.10
  121.5 0.2 bitcast_dynamic-update-slice_fusion.9
  121.8 0.1 bitcast_dynamic-update-slice_fusion
  121.9 1.3 %slice-done = s8[4194304]{0:T(1024)(128)(4,1)S(1)} async-done(((s8[4718592]{0:T(1024)(128)(4,1)}), s8[4194304]{0:T(1024)(128)(4,1)S(1)}, s32[]{:S(2)}) %slice-start) | async-done | bytes 4194328
  123.2 0.2 slice-done.1
  123.4 3.7 %add_add_fusion = f32[9,1,8,64,256]{4,3,2,1,0:T(8,128)} fusion(f32[9,1,8,64,256]{4,3,2,1,0:T(8,128)S(1)} %bitcast_dynamic-update-slice_fusion, f32[9,1,8,64,256]{4,3,2,1,0:T(8,128)S(1)} %bitcast.102, f32[9,1,8,64,256]{4,3,2,1,0:T(8,128)S(1)} %get-tuple-element.23), kind=kLoop, calls=%fused_computation | loop fusion | flops 2359296 | bytes 18874368 | tf_op jit(solution)/shard_map/add | solution.py:126
  (48 shorter events, 0.4 us)
Async XLA Ops:
  0.6 13.3 %copy-start.3 = (f32[1,8,64,256]{3,2,1,0:T(8,128)S(1)}, f32[1,8,64,256]{3,2,1,0:T(8,128)}, u32[]{:S(2)}) copy-start(f32[1,8,64,256]{3,2,1,0:T(8,128)} %param.13) | copy-start | bytes 1572868
  0.6 7.7 %copy-start.4 = (f32[1,8,64,256]{3,2,1,0:T(8,128)S(1)}, f32[1,8,64,256]{3,2,1,0:T(8,128)}, u32[]{:S(2)}) copy-start(f32[1,8,64,256]{3,2,1,0:T(8,128)} %param.11) | copy-start | bytes 1572868
  1.8 12.1 %collective-permute-start.6 = (f32[4,64,256]{2,1,0:T(8,128)S(1)}, f32[4,64,256]{2,1,0:T(8,128)S(1)}, u32[]{:S(2)}, u32[]{:S(2)}) collective-permute-start(f32[4,64,256]{2,1,0:T(8,128)S(1)} %get-tuple-element.21), channel_id=1, source_target_pairs={{1,0},{2,1},{3,2},{4,3},{5,4},{6,5},{7,6},{8,7},{9,8},{10,9},{11,1... | collective-permute-start | bytes 786440 | tf_op jit(solution)/shard_map/ppermute | solution.py:19
  3.8 10.1 %collective-permute-start.7 = (f32[4,64,256]{2,1,0:T(8,128)S(1)}, f32[4,64,256]{2,1,0:T(8,128)S(1)}, u32[]{:S(2)}, u32[]{:S(2)}) collective-permute-start(f32[4,64,256]{2,1,0:T(8,128)S(1)} %get-tuple-element.22), channel_id=1, source_target_pairs={{0,1},{1,2},{2,3},{3,4},{4,5},{5,6},{6,7},{7,8},{8,9},{9,10},{10,1... | collective-permute-start | bytes 786440 | tf_op jit(solution)/shard_map/ppermute | solution.py:19
  8.3 15.7 %collective-permute-start = (f32[4,64,256]{2,1,0:T(8,128)S(1)}, f32[4,64,256]{2,1,0:T(8,128)S(1)}, u32[]{:S(2)}, u32[]{:S(2)}) collective-permute-start(f32[4,64,256]{2,1,0:T(8,128)S(1)} %get-tuple-element.13), channel_id=1, source_target_pairs={{1,0},{2,1},{3,2},{4,3},{5,4},{6,5},{7,6},{8,7},{9,8},{10,9},{11,1... | collective-permute-start | bytes 786440 | tf_op jit(solution)/shard_map/ppermute | solution.py:19
  10.3 13.8 %collective-permute-start.1 = (f32[4,64,256]{2,1,0:T(8,128)S(1)}, f32[4,64,256]{2,1,0:T(8,128)S(1)}, u32[]{:S(2)}, u32[]{:S(2)}) collective-permute-start(f32[4,64,256]{2,1,0:T(8,128)S(1)} %get-tuple-element.14), channel_id=1, source_target_pairs={{0,1},{1,2},{2,3},{3,4},{4,5},{5,6},{6,7},{7,8},{8,9},{9,10},{10,1... | collective-permute-start | bytes 786440 | tf_op jit(solution)/shard_map/ppermute | solution.py:19
  14.1 2.3 %copy-start = (f32[1,8,64,256]{3,2,1,0:T(8,128)S(1)}, f32[1,8,64,256]{3,2,1,0:T(8,128)}, u32[]{:S(2)}) copy-start(f32[1,8,64,256]{3,2,1,0:T(8,128)} %param.16) | copy-start | bytes 1572868
  14.1 2.3 %copy-start.1 = (f32[1,8,64,256]{3,2,1,0:T(8,128)S(1)}, f32[1,8,64,256]{3,2,1,0:T(8,128)}, u32[]{:S(2)}) copy-start(f32[1,8,64,256]{3,2,1,0:T(8,128)} %param.15) | copy-start | bytes 1572868
  14.1 2.3 %copy-start.2 = (f32[1,8,64,256]{3,2,1,0:T(8,128)S(1)}, f32[1,8,64,256]{3,2,1,0:T(8,128)}, u32[]{:S(2)}) copy-start(f32[1,8,64,256]{3,2,1,0:T(8,128)} %param.14) | copy-start | bytes 1572868
  14.1 2.3 %copy-start.8 = (f32[1,8,64,256]{3,2,1,0:T(8,128)S(1)}, f32[1,8,64,256]{3,2,1,0:T(8,128)}, u32[]{:S(2)}) copy-start(f32[1,8,64,256]{3,2,1,0:T(8,128)} %param.12) | copy-start | bytes 1572868
  18.3 15.6 %collective-permute-start.8 = (f32[4,64,256]{2,1,0:T(8,128)S(1)}, f32[4,64,256]{2,1,0:T(8,128)S(1)}, u32[]{:S(2)}, u32[]{:S(2)}) collective-permute-start(f32[4,64,256]{2,1,0:T(8,128)S(1)} %get-tuple-element.19), channel_id=1, source_target_pairs={{1,0},{2,1},{3,2},{4,3},{5,4},{6,5},{7,6},{8,7},{9,8},{10,9},{11,1... | collective-permute-start | bytes 786440 | tf_op jit(solution)/shard_map/ppermute | solution.py:19
  20.2 13.7 %collective-permute-start.9 = (f32[4,64,256]{2,1,0:T(8,128)S(1)}, f32[4,64,256]{2,1,0:T(8,128)S(1)}, u32[]{:S(2)}, u32[]{:S(2)}) collective-permute-start(f32[4,64,256]{2,1,0:T(8,128)S(1)} %get-tuple-element.20), channel_id=1, source_target_pairs={{0,1},{1,2},{2,3},{3,4},{4,5},{5,6},{6,7},{7,8},{8,9},{9,10},{10,1... | collective-permute-start | bytes 786440 | tf_op jit(solution)/shard_map/ppermute | solution.py:19
  24.2 2.3 %copy-start.9 = (f32[1,8,64,256]{3,2,1,0:T(8,128)S(1)}, f32[1,8,64,256]{3,2,1,0:T(8,128)}, u32[]{:S(2)}) copy-start(f32[1,8,64,256]{3,2,1,0:T(8,128)} %param.10) | copy-start | bytes 1572868
  28.3 16.2 %collective-permute-start.2 = (f32[4,64,256]{2,1,0:T(8,128)S(1)}, f32[4,64,256]{2,1,0:T(8,128)S(1)}, u32[]{:S(2)}, u32[]{:S(2)}) collective-permute-start(f32[4,64,256]{2,1,0:T(8,128)S(1)} %get-tuple-element.11), channel_id=1, source_target_pairs={{1,0},{2,1},{3,2},{4,3},{5,4},{6,5},{7,6},{8,7},{9,8},{10,9},{11,1... | collective-permute-start | bytes 786440 | tf_op jit(solution)/shard_map/ppermute | solution.py:19
  30.2 14.3 %collective-permute-start.3 = (f32[4,64,256]{2,1,0:T(8,128)S(1)}, f32[4,64,256]{2,1,0:T(8,128)S(1)}, u32[]{:S(2)}, u32[]{:S(2)}) collective-permute-start(f32[4,64,256]{2,1,0:T(8,128)S(1)} %get-tuple-element.12), channel_id=1, source_target_pairs={{0,1},{1,2},{2,3},{3,4},{4,5},{5,6},{6,7},{7,8},{8,9},{9,10},{10,1... | collective-permute-start | bytes 786440 | tf_op jit(solution)/shard_map/ppermute | solution.py:19
  38.1 17.1 %collective-permute-start.10 = (f32[4,64,256]{2,1,0:T(8,128)S(1)}, f32[4,64,256]{2,1,0:T(8,128)S(1)}, u32[]{:S(2)}, u32[]{:S(2)}) collective-permute-start(f32[4,64,256]{2,1,0:T(8,128)S(1)} %get-tuple-element.18), channel_id=1, source_target_pairs={{0,1},{1,2},{2,3},{3,4},{4,5},{5,6},{6,7},{7,8},{8,9},{9,10},{10,1... | collective-permute-start | bytes 786440 | tf_op jit(solution)/shard_map/ppermute | solution.py:19
  42.4 12.9 %collective-permute-start.11 = (f32[4,64,256]{2,1,0:T(8,128)S(1)}, f32[4,64,256]{2,1,0:T(8,128)S(1)}, u32[]{:S(2)}, u32[]{:S(2)}) collective-permute-start(f32[4,64,256]{2,1,0:T(8,128)S(1)} %get-tuple-element.17), channel_id=1, source_target_pairs={{1,0},{2,1},{3,2},{4,3},{5,4},{6,5},{7,6},{8,7},{9,8},{10,9},{11,1... | collective-permute-start | bytes 786440 | tf_op jit(solution)/shard_map/ppermute | solution.py:19
  48.8 16.4 %collective-permute-start.4 = (f32[4,64,256]{2,1,0:T(8,128)S(1)}, f32[4,64,256]{2,1,0:T(8,128)S(1)}, u32[]{:S(2)}, u32[]{:S(2)}) collective-permute-start(f32[4,64,256]{2,1,0:T(8,128)S(1)} %get-tuple-element.10), channel_id=1, source_target_pairs={{0,1},{1,2},{2,3},{3,4},{4,5},{5,6},{6,7},{7,8},{8,9},{9,10},{10,1... | collective-permute-start | bytes 786440 | tf_op jit(solution)/shard_map/ppermute | solution.py:19
  53.3 11.8 %collective-permute-start.5 = (f32[4,64,256]{2,1,0:T(8,128)S(1)}, f32[4,64,256]{2,1,0:T(8,128)S(1)}, u32[]{:S(2)}, u32[]{:S(2)}) collective-permute-start(f32[4,64,256]{2,1,0:T(8,128)S(1)} %get-tuple-element.9), channel_id=1, source_target_pairs={{1,0},{2,1},{3,2},{4,3},{5,4},{6,5},{7,6},{8,7},{9,8},{10,9},{11,1... | collective-permute-start | bytes 786440 | tf_op jit(solution)/shard_map/ppermute | solution.py:19
  59.6 15.7 %collective-permute-start.14 = (f32[4,64,256]{2,1,0:T(8,128)S(1)}, f32[4,64,256]{2,1,0:T(8,128)S(1)}, u32[]{:S(2)}, u32[]{:S(2)}) collective-permute-start(f32[4,64,256]{2,1,0:T(8,128)S(1)} %get-tuple-element.15), channel_id=1, source_target_pairs={{1,0},{2,1},{3,2},{4,3},{5,4},{6,5},{7,6},{8,7},{9,8},{10,9},{11,1... | collective-permute-start | bytes 786440 | tf_op jit(solution)/shard_map/ppermute | solution.py:19
  61.5 13.8 %collective-permute-start.15 = (f32[4,64,256]{2,1,0:T(8,128)S(1)}, f32[4,64,256]{2,1,0:T(8,128)S(1)}, u32[]{:S(2)}, u32[]{:S(2)}) collective-permute-start(f32[4,64,256]{2,1,0:T(8,128)S(1)} %get-tuple-element.16), channel_id=1, source_target_pairs={{0,1},{1,2},{2,3},{3,4},{4,5},{5,6},{6,7},{7,8},{8,9},{9,10},{10,1... | collective-permute-start | bytes 786440 | tf_op jit(solution)/shard_map/ppermute | solution.py:19
  69.5 8.2 %collective-permute-start.12 = (f32[4,64,256]{2,1,0:T(8,128)S(1)}, f32[4,64,256]{2,1,0:T(8,128)S(1)}, u32[]{:S(2)}, u32[]{:S(2)}) collective-permute-start(f32[4,64,256]{2,1,0:T(8,128)S(1)} %get-tuple-element.7), channel_id=1, source_target_pairs={{1,0},{2,1},{3,2},{4,3},{5,4},{6,5},{7,6},{8,7},{9,8},{10,9},{11,1... | collective-permute-start | bytes 786440 | tf_op jit(solution)/shard_map/ppermute | solution.py:19
  71.4 9.8 %collective-permute-start.13 = (f32[4,64,256]{2,1,0:T(8,128)S(1)}, f32[4,64,256]{2,1,0:T(8,128)S(1)}, u32[]{:S(2)}, u32[]{:S(2)}) collective-permute-start(f32[4,64,256]{2,1,0:T(8,128)S(1)} %get-tuple-element.8), channel_id=1, source_target_pairs={{0,1},{1,2},{2,3},{3,4},{4,5},{5,6},{6,7},{7,8},{8,9},{9,10},{10,1... | collective-permute-start | bytes 786440 | tf_op jit(solution)/shard_map/ppermute | solution.py:19
  85.4 32.9 %copy-start.5 = (f32[1,8,64,256]{3,2,1,0:T(8,128)}, f32[1,8,64,256]{3,2,1,0:T(8,128)S(1)}, u32[]{:S(2)}) copy-start(f32[1,8,64,256]{3,2,1,0:T(8,128)S(1)} %fusion.100) | copy-start | bytes 1572868
  87.2 31.1 %copy-start.6 = (f32[1,8,64,256]{3,2,1,0:T(8,128)}, f32[1,8,64,256]{3,2,1,0:T(8,128)S(1)}, u32[]{:S(2)}) copy-start(f32[1,8,64,256]{3,2,1,0:T(8,128)S(1)} %fusion.153) | copy-start | bytes 1572868
  87.2 7.5 %copy-start.10 = (s32[9]{0:T(128)S(1)}, s32[9]{0:T(128)}, u32[]{:S(2)}) copy-start(s32[9]{0:T(128)} %param.18) | copy-start | bytes 112
  87.2 30.9 %copy-start.7 = (s32[1,8,64]{2,1,0:T(8,128)S(1)}, s32[1,8,64]{2,1,0:T(8,128)}, u32[]{:S(2)}) copy-start(s32[1,8,64]{2,1,0:T(8,128)} %param.17) | copy-start | bytes 6148
  88.3 29.9 %collective-permute-start.16 = (f32[2,4,64,256]{3,2,1,0:T(8,128)}, f32[2,4,64,256]{3,2,1,0:T(8,128)}, u32[]{:S(2)}, u32[]{:S(2)}) collective-permute-start(f32[2,4,64,256]{3,2,1,0:T(8,128)} %get-tuple-element.5), channel_id=1, source_target_pairs={{0,1},{1,2},{2,3},{3,4},{4,5},{5,6},{6,7},{7,8},{8,9},{9,10},{10,1... | collective-permute-start | bytes 1572872 | tf_op jit(solution)/shard_map/ppermute | solution.py:19
  92.7 25.5 %collective-permute-start.17 = (f32[2,4,64,256]{3,2,1,0:T(8,128)}, f32[2,4,64,256]{3,2,1,0:T(8,128)}, u32[]{:S(2)}, u32[]{:S(2)}) collective-permute-start(f32[2,4,64,256]{3,2,1,0:T(8,128)} %get-tuple-element.6), channel_id=1, source_target_pairs={{1,0},{2,1},{3,2},{4,3},{5,4},{6,5},{7,6},{8,7},{9,8},{10,9},{11,1... | collective-permute-start | bytes 1572872 | tf_op jit(solution)/shard_map/ppermute | solution.py:19
  121.0 2.2 %slice-start = ((s8[4718592]{0:T(1024)(128)(4,1)}), s8[4194304]{0:T(1024)(128)(4,1)S(1)}, s32[]{:S(2)}) async-start(s8[4718592]{0:T(1024)(128)(4,1)} %bitcast.101), calls=%async_computation | async-start | bytes 8388608
  121.3 2.1 %slice-start.1 = ((s8[4718592]{0:T(1024)(128)(4,1)}), s8[524288]{0:T(1024)(128)(4,1)S(1)}, s32[]{:S(2)}) async-start(s8[4718592]{0:T(1024)(128)(4,1)} %bitcast.101), calls=%async_computation.1 | async-start | bytes 1048576
where the time goes:
time: 129 us; the launch traced here: 127 us
  starting transfers between devices  53.8 us (42%)
  other arithmetic  41.7 us (32%)
  between operations  24.2 us (19%)
  local copies, waits for them, and re-layouts  3.98 us (3%)
  waiting for transfers between devices  3.47 us (3%)
    ppermute x18, starting transfers between devices, from_behind(): lax.ppermute(value, axis, [(source, source + steps) for source in range(f...  53.8 us
    add x8, other arithmetic, stencil(): deriv_z + first_w[k - 1] * (padded[:, 4:4 + count_y, 4 + k:4 + k + depth]...  18.2 us
    add x3, other arithmetic, per_device(): 2.0 * receiver_cur - receiver_prev  5.29 us
    add x3, other arithmetic, per_device(): 2.0 * source_cur - source_prev  5.29 us
    another operation x3, other arithmetic, per_device(): snap_pad = snap_rims(jnp.stack([source_cur, receiver_cur]))  4.64 us
    add x1, other arithmetic, per_device(): image = image + image_terms(snap_pad[0], snap_pad[1], HMAX, offsets, mute)  3.71 us
    ppermute x18, waiting for transfers between devices, from_behind(): lax.ppermute(value, axis, [(source, source + steps) for source in range(f...  3.47 us
  transfers between devices with their start and end apart: 18, of which 1 were waited for; matrix products, arithmetic and copies ran while one was open for 23% of the time, Pallas kernels for 0%

commit v1 on v0

v1 whole, which is shorter than its diff:
```python
import functools

import jax
import jax.numpy as jnp
import numpy as np
from jax import lax
from jax.experimental import pallas as pl
from jax.experimental.pallas import tpu as pltpu
from jax.sharding import PartitionSpec as P

STEPS = 4
RAD = 4
HMAX = 4
NOFF = 9

second_w = (-205.0 / 72.0, 8.0 / 5.0, -1.0 / 5.0, 8.0 / 315.0, -1.0 / 560.0)
first_w = (4.0 / 5.0, -1.0 / 5.0, 4.0 / 105.0, -1.0 / 280.0)

VMEM = pl.BlockSpec(memory_space=pltpu.VMEM)
SMEM = pl.BlockSpec(memory_space=pltpu.SMEM)
ANY = pl.BlockSpec(memory_space=pl.ANY)
MIB = 1 << 20


def parity():
    return lax.rem(lax.axis_index("blk"), 2)


def is_flipped(inner):
    odd = parity()
    return 1 - odd if inner else odd


def natural(plane, flipped):
    return plane + flipped * (7 - 2 * plane)


def at(half, other, halo, field, position):
    if position < 0:
        return halo.at[field, -1 - position]
    if position < 4:
        return half.at[field, position]
    return other.at[field, 7 - position]


def bands(depth, rows):
    d = np.arange(depth)[None, :] - np.arange(depth)[:, None]
    dzz = np.zeros((depth, depth))
    dz = np.zeros((depth, depth))
    r = np.arange(4 * rows)
    dr = np.where(r[None, :] // rows == r[:, None] // rows, r[None, :] - r[:, None], 99)
    dyy = np.zeros((4 * rows, 4 * rows))
    dzz[d == 0] = second_w[0]
    for k in range(1, 5):
        dzz[np.abs(d) == k] = second_w[k]
        dyy[np.abs(dr) == k] = second_w[k]
        dz[d == -k] = first_w[k - 1]
        dz[d == k] = -first_w[k - 1]

    def pair(m):
        m = m.astype(np.float32)
        high = m.astype(jnp.bfloat16)
        low = (m - high.astype(np.float32)).astype(jnp.bfloat16)
        return [high, low]

    return jnp.asarray(np.stack(pair(dzz) + pair(dz))), jnp.asarray(np.stack(pair(dyy)))


def gather_kernel(plan, n_in, *refs):
    ins, outs, sem = refs[:n_in], refs[n_in:-1], refs[-1]
    copies = []
    for out_id, inner, sources in plan:
        flip = is_flipped(inner)
        for i, src in enumerate(sources):
            for m in range(4):
                copies.append(
                    pltpu.make_async_copy(
                        ins[src].at[natural(m, flip)], outs[out_id].at[i, m], sem.at[len(copies)]
                    )
                )
    for c in copies:
        c.start()
    for c in copies:
        c.wait()


def gather(arrays, plan):
    shape = arrays[0].shape[1:]
    return pl.pallas_call(
        functools.partial(gather_kernel, plan, len(arrays)),
        out_shape=[jax.ShapeDtypeStruct((len(s), 4) + shape, jnp.float32) for _, _, s in plan],
        in_specs=[ANY] * len(arrays),
        out_specs=[VMEM] * len(plan),
        scratch_shapes=[pltpu.SemaphoreType.DMA((sum(4 * len(s) for _, _, s in plan),))],
        compiler_params=pltpu.CompilerParams(vmem_limit_bytes=8 * MIB),
        name="gather",
    )(*arrays)


CHUNK = 16


def step_kernel(inner, half, other, halo, prev, coef, wz, wy, out, v_hi, v_lo, x_hi, x_lo, horiz):
    rows = half.shape[2]
    sign = (1 - 2 * is_flipped(inner)).astype(jnp.float32)
    w1 = [sign * w for w in first_w]

    def first(i, carry):
        r = pl.multiple_of(i * CHUNK, CHUNK)
        span = pl.ds(r, CHUNK)
        for f in range(2):
            line = [at(half, other, halo, f, q)[span] for q in range(-4, 8)]
            for m in range(4):
                center = line[m + 4]
                hx = (2.0 * second_w[0]) * center
                dx = None
                for k in range(1, 5):
                    up, down = line[m + 4 + k], line[m + 4 - k]
                    hx = hx + second_w[k] * (up + down)
                    t = w1[k - 1] * (up - down)
                    dx = t if dx is None else dx + t
                horiz[f, m, span] = hx
                at_row = pl.ds(pl.multiple_of((f * 4 + m) * rows + r, CHUNK), CHUNK)
                high = center.astype(jnp.bfloat16)
                v_hi[at_row] = high
                v_lo[at_row] = (center - high.astype(jnp.float32)).astype(jnp.bfloat16)
                high = dx.astype(jnp.bfloat16)
                x_hi[at_row] = high
                x_lo[at_row] = (dx - high.astype(jnp.float32)).astype(jnp.bfloat16)
        return carry

    lax.fori_loop(0, rows // CHUNK, first, 0)
    dot = functools.partial(jnp.dot, preferred_element_type=jnp.float32)
    for f in range(2):
        part = pl.ds(f * 4 * rows, 4 * rows)
        vh, vl, xh, xl = v_hi[part], v_lo[part], x_hi[part], x_lo[part]
        zz = dot(vh, wz[0]) + (dot(vl, wz[0]) + dot(vh, wz[1]))
        zx = dot(xh, wz[2]) + (dot(xl, wz[2]) + dot(xh, wz[3]))
        yy = dot(wy[0], vh) + (dot(wy[0], vl) + dot(wy[1], vh))
        for m in range(4):
            cut = slice(m * rows, (m + 1) * rows)
            out[f, m] = (
                2.0 * half[f, m]
                - prev[f, m]
                + coef[0, m] * (horiz[f, m] + yy[cut])
                + coef[1, m] * zz[cut]
                + coef[2, m] * zx[cut]
            )


def step(inner, half, other, halo, prev, coef, wz, wy):
    rows, depth = half.shape[2:]
    flat = pltpu.VMEM((8 * rows, depth), jnp.bfloat16)
    return pl.pallas_call(
        functools.partial(step_kernel, inner),
        out_shape=jax.ShapeDtypeStruct(half.shape, jnp.float32),
        in_specs=[VMEM] * 7,
        out_specs=VMEM,
        scratch_shapes=[flat] * 4 + [pltpu.VMEM(half.shape, jnp.float32)],
        compiler_params=pltpu.CompilerParams(vmem_limit_bytes=12 * MIB),
        name="inner_step" if inner else "outer_step",
    )(half, other, halo, prev, coef, wz, wy)


def find_slots(offsets, slots):
    for k in range(NOFF):
        slots[offsets[k]] = k


def add_terms(acc, slots, mute, snaps, inner, wanted):
    flip = is_flipped(inner)
    sign = 1 - 2 * flip
    slot = {h: slots[sign * h + HMAX] for h in range(-HMAX, HMAX + 1)}
    places = [natural(m, flip) for m in range(4)]
    locals_ = [m + flip * (3 - 2 * m) for m in range(4)]
    rows = acc.shape[2]

    def body(i, carry):
        span = pl.ds(pl.multiple_of(i * 8, 8), 8)
        for m in range(4):
            mask = mute[places[m], span]
            for h in range(-HMAX, HMAX + 1):
                if not wanted(h, m):
                    continue
                total = None
                for half, other, halo in snaps:
                    t = at(half, other, halo, 0, m - h)[span] * at(half, other, halo, 1, m + h)[span]
                    total = t if total is None else total + t
                acc[slot[h], locals_[m], span] += mask * total
        return carry

    lax.fori_loop(0, rows // 8, body, 0)


def half_planes(image, inner):
    return image.at[:, pl.ds(4 * is_flipped(inner), 4)]


def image_mid_kernel(image_in, offsets, mute, half, other, halo, acc, slots, sem):
    copy = pltpu.make_async_copy(half_planes(image_in, False), acc, sem)
    copy.start()
    find_slots(offsets, slots)
    copy.wait()
    add_terms(acc, slots, mute, [(half, other, halo)], False, lambda h, m: True)


def image_mid(image_in, offsets, mute, half, other, halo):
    shape = (NOFF, 4) + half.shape[2:]
    return pl.pallas_call(
        image_mid_kernel,
        out_shape=jax.ShapeDtypeStruct(shape, jnp.float32),
        in_specs=[ANY, SMEM] + [VMEM] * 4,
        out_specs=VMEM,
        scratch_shapes=[pltpu.SMEM((NOFF,), jnp.int32), pltpu.SemaphoreType.DMA],
        compiler_params=pltpu.CompilerParams(vmem_limit_bytes=8 * MIB),
        name="image_mid",
    )(image_in, offsets, mute, half, other, halo)


def image_inner_kernel(
    image_in, offsets, mute, in2, out2, hal2, in4, out4, hal4, image, src, rec, acc, slots, sem, sems
):
    fetch = pltpu.make_async_copy(half_planes(image_in, True), acc, sem)
    fetch.start()
    copies = []
    for inner, field4 in ((True, in4), (False, out4)):
        for f, last in ((0, src), (1, rec)):
            for m in range(4):
                copies.append(
                    pltpu.make_async_copy(
                        field4.at[f, m], last.at[natural(m, is_flipped(inner))], sems.at[len(copies)]
                    )
                )
    for c in copies:
        c.start()
    find_slots(offsets, slots)
    fetch.wait()
    add_terms(
        acc, slots, mute, [(in2, out2, hal2), (in4, out4, hal4)], True, lambda h, m: True
    )
    store = pltpu.make_async_copy(acc, half_planes(image, True), sem)
    store.start()
    for c in copies:
        c.wait()
    store.wait()


def image_inner(image_in, offsets, mute, snap2, snap4):
    shape = snap2[0].shape
    field = jax.ShapeDtypeStruct((8,) + shape[2:], jnp.float32)
    return pl.pallas_call(
        image_inner_kernel,
        out_shape=[jax.ShapeDtypeStruct(image_in.shape, jnp.float32), field, field],
        in_specs=[ANY, SMEM] + [VMEM] * 7,
        out_specs=[ANY] * 3,
        scratch_shapes=[
            pltpu.VMEM((NOFF, 4) + shape[2:], jnp.float32),
            pltpu.SMEM((NOFF,), jnp.int32),
            pltpu.SemaphoreType.DMA,
            pltpu.SemaphoreType.DMA((16,)),
        ],
        compiler_params=pltpu.CompilerParams(vmem_limit_bytes=8 * MIB),
        name="image_inner",
    )(image_in, offsets, mute, *snap2, *snap4)


def image_last_kernel(image_old, part, offsets, mute, half, other, halo, image, acc, slots, sem):
    del image_old
    find_slots(offsets, slots)
    acc[...] = part[...]
    add_terms(acc, slots, mute, [(half, other, halo)], False, lambda h, m: True)
    store = pltpu.make_async_copy(acc, half_planes(image, False), sem)
    store.start()
    store.wait()


def image_last(image, part, offsets, mute, snap4):
    return pl.pallas_call(
        image_last_kernel,
        out_shape=jax.ShapeDtypeStruct(image.shape, jnp.float32),
        in_specs=[ANY, VMEM, SMEM] + [VMEM] * 4,
        out_specs=ANY,
        scratch_shapes=[
            pltpu.VMEM(part.shape, jnp.float32),
            pltpu.SMEM((NOFF,), jnp.int32),
            pltpu.SemaphoreType.DMA,
        ],
        input_output_aliases={0: 0},
        compiler_params=pltpu.CompilerParams(vmem_limit_bytes=8 * MIB),
        name="image_last",
    )(image, part, offsets, mute, *snap4)


def across_chips(value):
    count = lax.axis_size("blk")
    pairs = [(i, i + 1) for i in range(1, count - 1, 2)]
    return lax.ppermute(value, "blk", pairs + [(b, a) for a, b in pairs])


def within_chip(value):
    return lax.ppermute(value, "blk", [(i, i ^ 1) for i in range(lax.axis_size("blk"))])


def per_device(
    source_prev,
    source_cur,
    receiver_prev,
    receiver_cur,
    coef_horiz,
    coef_vert,
    coef_mixed,
    live_depth,
    offsets,
    image_in,
):
    source_prev, source_cur = source_prev[0], source_cur[0]
    receiver_prev, receiver_cur = receiver_prev[0], receiver_cur[0]
    coefs = [coef_horiz[0], coef_vert[0], coef_mixed[0]]
    image_in = image_in[:, 0]
    rows, depth = source_cur.shape[1:]
    wz, wy = bands(depth, rows)
    depth_ids = lax.broadcasted_iota(jnp.int32, source_cur.shape, 2)
    mute = (depth_ids < live_depth[0][:, :, None]).astype(jnp.float32)

    (out,) = gather([source_cur, receiver_cur], [(0, False, (0, 1))])
    far = across_chips(out)
    inn, prev_out, prev_inn, coef_out, coef_inn = gather(
        [source_cur, receiver_cur, source_prev, receiver_prev] + coefs,
        [
            (0, True, (0, 1)),
            (1, False, (2, 3)),
            (2, True, (2, 3)),
            (3, False, (4, 5, 6)),
            (4, True, (4, 5, 6)),
        ],
    )
    near = within_chip(inn)
    acc = None
    for n in range(STEPS):
        new_inn = step(True, inn, out, near, prev_inn, coef_inn, wz, wy)
        new_out = step(False, out, inn, far, prev_out, coef_out, wz, wy)
        if n == STEPS // 2:
            snap2 = (inn, out, near)
            part = image_mid(image_in, offsets, mute, out, inn, far)
        prev_inn, prev_out, inn, out = inn, out, new_inn, new_out
        near = within_chip(inn)
        far = across_chips(out)
    image, source_last, receiver_last = image_inner(
        image_in, offsets, mute, snap2, (inn, out, near)
    )
    image = image_last(image, part, offsets, mute, (out, inn, far))
    return (image[:, None], source_last[None], receiver_last[None])


def solution(mesh):
    in_specs = (
        P(("shots", "blk"), None, None, None),
        P(("shots", "blk"), None, None, None),
        P(("shots", "blk"), None, None, None),
        P(("shots", "blk"), None, None, None),
        P("blk", None, None, None),
        P("blk", None, None, None),
        P("blk", None, None, None),
        P("blk", None, None),
        P(),
        P(None, ("shots", "blk"), None, None, None),
    )
    out_specs = (
        P(None, ("shots", "blk"), None, None, None),
        P(("shots", "blk"), None, None, None),
        P(("shots", "blk"), None, None, None),
    )
    return jax.shard_map(
        per_device, mesh=mesh, in_specs=in_specs, out_specs=out_specs, check_vma=False
    )
```

time: 129 us -> 87 us (0.67); the launches traced: 127 us -> 86.5 us
  other arithmetic: 41.7 us -> 0.13 us
  starting transfers between devices: 53.8 us -> 22.6 us
  waiting for transfers between devices: 3.47 us -> 30.2 us
  Pallas kernels: 0 us -> 25.2 us
  between operations: 24.2 us -> 0.96 us
  local copies, waits for them, and re-layouts: 3.98 us -> 7.39 us
    add x15 -> x0, other arithmetic: 32.5 us -> none  [the longest x8 18.2 us: stencil(): deriv_z + first_w[k - 1] * (padded[:, 4:4 + count_y, 4 + k:4 + k + depth]...]
    ppermute x18 -> x10, starting transfers between devices: 53.8 us -> 22.6 us  [the longest x5 22.2 us: across_chips(): return lax.ppermute(value, 'blk', pairs + [(b, a) for a, b in pairs])]
    ppermute x18 -> x10, waiting for transfers between devices: 3.47 us -> 30.2 us  [the longest x5 30.2 us: across_chips(): return lax.ppermute(value, 'blk', pairs + [(b, a) for a, b in pairs])]
    pallas_call x0 -> x13, Pallas kernels: none -> 25.2 us  [the longest x8 11.7 us: step(): pl.pallas_call(functools.partial(step_kernel, inner), out_shape=jax.Shape...]
    unnamed x26, local copies, waits for them, and re-layouts: 1.54 us -> 7.39 us
    another operation x5 -> x0, other arithmetic: 5.01 us -> none  [the longest x3 4.64 us: per_device(): snap_pad = snap_rims(jnp.stack([source_cur, receiver_cur]))]
    concatenate x9 -> x0, other arithmetic: 2.38 us -> none  [the longest x1 1.41 us: snap_rims(): return jnp.concatenate([from_below, snaps, from_above], 1)]
    slice x10 -> x0, local copies, waits for them, and re-layouts: 2.22 us -> none  [the longest x8 1.41 us: wave_rims(): lax.slice_in_dim(field, 0, RAD, axis=xdim)]
  transfers between devices with their start and end apart: 18 -> 10, of which waited for: 1 -> 5; matrix products, arithmetic and copies ran while one was open for 23% -> 0% of each run, Pallas kernels for 0% -> 20%
where the time goes in v1:
time: 87 us; the launch traced here: 86.5 us
  waiting for transfers between devices  30.2 us (35%)
  Pallas kernels  25.2 us (29%)
  starting transfers between devices  22.6 us (26%)
  local copies, waits for them, and re-layouts  7.39 us (8%)
  between operations  0.96 us (1%)
    ppermute x5, waiting for transfers between devices, across_chips(): return lax.ppermute(value, 'blk', pairs + [(b, a) for a, b in pairs])  30.2 us
    ppermute x5, starting transfers between devices, across_chips(): return lax.ppermute(value, 'blk', pairs + [(b, a) for a, b in pairs])  22.2 us
    pallas_call x8, Pallas kernels, step(): pl.pallas_call(functools.partial(step_kernel, inner), out_shape=jax.Shape...  11.7 us
    unnamed x26, local copies, waits for them, and re-layouts  7.39 us
    pallas_call x2, Pallas kernels, gather(): pl.pallas_call(functools.partial(gather_kernel, plan, len(arrays)), out_s...  5.52 us
    pallas_call x1, Pallas kernels, image_inner(): pl.pallas_call(image_inner_kernel, out_shape=[jax.ShapeDtypeStruct(image_...  3.39 us
    pallas_call x1, Pallas kernels, image_last(): pl.pallas_call(image_last_kernel, out_shape=jax.ShapeDtypeStruct(image.sh...  2.96 us
  transfers between devices with their start and end apart: 10, of which 5 were waited for; matrix products, arithmetic and copies ran while one was open for 0% of the time, Pallas kernels for 20%

profile of v1, /device:TPU:1, one launch (start us, length us, event | category | flops | bytes accessed | tf_op | source)
XLA Modules:
  0.0 86.5 jit_solution(16448830696585942840)
XLA Ops:
  0.6 0.0 copy-start.1
  0.6 0.0 copy-start
  0.7 0.0 copy-start.2
  0.7 1.1 %copy-done.2 = f32[1,8,64,256]{3,2,1,0:T(8,128)S(1)} copy-done((f32[1,8,64,256]{3,2,1,0:T(8,128)S(1)}, f32[1,8,64,256]{3,2,1,0:T(8,128)}, u32[]{:S(2)}) %copy-start.2) | copy-done | bytes 524312
  1.8 0.0 copy-start.3
  1.8 1.0 %copy-done.3 = f32[1,8,64,256]{3,2,1,0:T(8,128)S(1)} copy-done((f32[1,8,64,256]{3,2,1,0:T(8,128)S(1)}, f32[1,8,64,256]{3,2,1,0:T(8,128)}, u32[]{:S(2)}) %copy-start.3) | copy-done | bytes 524312
  2.8 0.0 copy-start.4
  2.8 1.0 %copy-done.4 = f32[1,8,64,256]{3,2,1,0:T(8,128)S(1)} copy-done((f32[1,8,64,256]{3,2,1,0:T(8,128)S(1)}, f32[1,8,64,256]{3,2,1,0:T(8,128)}, u32[]{:S(2)}) %copy-start.4) | copy-done | bytes 524312
  3.9 0.0 copy-start.5
  3.9 1.0 %copy-done.5 = f32[1,8,64,256]{3,2,1,0:T(8,128)S(1)} copy-done((f32[1,8,64,256]{3,2,1,0:T(8,128)S(1)}, f32[1,8,64,256]{3,2,1,0:T(8,128)}, u32[]{:S(2)}) %copy-start.5) | copy-done | bytes 524312
  4.9 0.0 copy-start.6
  4.9 1.0 %copy-done.6 = f32[1,8,64,256]{3,2,1,0:T(8,128)S(1)} copy-done((f32[1,8,64,256]{3,2,1,0:T(8,128)S(1)}, f32[1,8,64,256]{3,2,1,0:T(8,128)}, u32[]{:S(2)}) %copy-start.6) | copy-done | bytes 524312
  5.9 0.0 copy-start.7
  5.9 1.0 %copy-done.7 = f32[1,8,64,256]{3,2,1,0:T(8,128)S(1)} copy-done((f32[1,8,64,256]{3,2,1,0:T(8,128)S(1)}, f32[1,8,64,256]{3,2,1,0:T(8,128)}, u32[]{:S(2)}) %copy-start.7) | copy-done | bytes 524312
  7.0 0.0 copy-start.8
  7.0 1.0 %copy-done.8 = f32[1,8,64,256]{3,2,1,0:T(8,128)S(1)} copy-done((f32[1,8,64,256]{3,2,1,0:T(8,128)S(1)}, f32[1,8,64,256]{3,2,1,0:T(8,128)}, u32[]{:S(2)}) %copy-start.8) | copy-done | bytes 524312
  8.0 4.8 %gather.2 = (f32[2,4,64,256]{3,2,1,0:T(8,128)S(1)}, f32[2,4,64,256]{3,2,1,0:T(8,128)S(1)}, f32[2,4,64,256]{3,2,1,0:T(8,128)S(1)}, f32[3,4,64,256]{3,2,1,0:T(8,128)S(1)}, f32[3,4,64,256]{3,2,1,0:T(8,128)S(1)}) custom-call(f32[8,64,256]{2,1,0:T(8,128)S(1)} %bitcast.18, f32[8,64,256]{2,1,0:T(8,128)S(1)} %bitcast.20, f32[8,64,256]{2,1,0:T(8,128)S(1)} %bitcast.22, ...), custom_call_target="tpu_custom_call" | custom-call | tf_op jit(solution)/shard_map/gather/pallas_call | solution.py:89
  12.8 0.1 collective-permute-start
  12.9 0.7 gather.3.other.half.prev
  13.7 4.5 %collective-permute-start.1 = (f32[2,4,64,256]{3,2,1,0:T(8,128)S(1)}, f32[2,4,64,256]{3,2,1,0:T(8,128)S(1)}, u32[]{:S(2)}, u32[]{:S(2)}) collective-permute-start(f32[2,4,64,256]{3,2,1,0:T(8,128)S(1)} %gather.3.other.half.prev), channel_id=1, source_target_pairs={{1,2},{3,4},{5,6},{7,8},{9,10},{11,12},{13,14},{2,1},{4,3},{6,5},{... | collective-permute-start | bytes 1572872 | tf_op jit(solution)/shard_map/ppermute | solution.py:297
  18.2 0.0 collective-permute-done.halo
  18.2 0.0 copy-done.1
  18.3 0.0 copy-done
  18.3 1.5 %inner_step.4.half.other.prev = f32[2,4,64,256]{3,2,1,0:T(8,128)S(1)} custom-call(f32[2,4,64,256]{3,2,1,0:T(8,128)S(1)} %get-tuple-element.11.half.other.prev, f32[2,4,64,256]{3,2,1,0:T(8,128)S(1)} %gather.3.other.half.prev, f32[2,4,64,256]{3,2,1,0:T(8,128)S(1)} %collective-permute-done.halo, f32[2,4,64,256]{3,2,1,0:T(8,128)S(1)} %get-tuple-element.12.prev, ...), custom_call_target="tpu_custom_call" | custom-call | tf_op jit(solution)/shard_map/inner_step/pallas_call | solution.py:154
  19.7 0.1 collective-permute-start.2
  19.8 10.1 %collective-permute-done.1.halo = f32[2,4,64,256]{3,2,1,0:T(8,128)S(1)} collective-permute-done((f32[2,4,64,256]{3,2,1,0:T(8,128)S(1)}, f32[2,4,64,256]{3,2,1,0:T(8,128)S(1)}, u32[]{:S(2)}, u32[]{:S(2)}) %collective-permute-start.1) | collective-permute-done | bytes 524320 | tf_op jit(solution)/shard_map/ppermute | solution.py:297
  30.0 1.4 %outer_step.4.other.half.prev = f32[2,4,64,256]{3,2,1,0:T(8,128)S(1)} custom-call(f32[2,4,64,256]{3,2,1,0:T(8,128)S(1)} %gather.3.other.half.prev, f32[2,4,64,256]{3,2,1,0:T(8,128)S(1)} %get-tuple-element.11.half.other.prev, f32[2,4,64,256]{3,2,1,0:T(8,128)S(1)} %collective-permute-done.1.halo, f32[2,4,64,256]{3,2,1,0:T(8,128)S(1)} %get-tuple-element.14.prev, ...), custom_call_target="tpu_custom_call" | custom-call | tf_op jit(solution)/shard_map/outer_step/pallas_call | solution.py:154
  31.4 4.4 %collective-permute-start.3 = (f32[2,4,64,256]{3,2,1,0:T(8,128)S(1)}, f32[2,4,64,256]{3,2,1,0:T(8,128)S(1)}, u32[]{:S(2)}, u32[]{:S(2)}) collective-permute-start(f32[2,4,64,256]{3,2,1,0:T(8,128)S(1)} %outer_step.4.other.half.prev), channel_id=1, source_target_pairs={{1,2},{3,4},{5,6},{7,8},{9,10},{11,12},{13,14},{2,1},{4,3},{6,5},{... | collective-permute-start | bytes 1572872 | tf_op jit(solution)/shard_map/ppermute | solution.py:297
  35.8 0.0 collective-permute-done.2.halo
  35.8 1.5 %inner_step.5.half.other.prev.in2 = f32[2,4,64,256]{3,2,1,0:T(8,128)S(1)} custom-call(f32[2,4,64,256]{3,2,1,0:T(8,128)S(1)} %inner_step.4.half.other.prev, f32[2,4,64,256]{3,2,1,0:T(8,128)S(1)} %outer_step.4.other.half.prev, f32[2,4,64,256]{3,2,1,0:T(8,128)S(1)} %collective-permute-done.2.halo, f32[2,4,64,256]{3,2,1,0:T(8,128)S(1)} %get-tuple-element.11.half.other.prev, ...), custom_call_target="tpu_custom_call" | custom-call | tf_op jit(solution)/shard_map/inner_step/pallas_call | solution.py:154
  37.3 0.1 collective-permute-start.4
  37.4 7.1 %collective-permute-done.3.halo = f32[2,4,64,256]{3,2,1,0:T(8,128)S(1)} collective-permute-done((f32[2,4,64,256]{3,2,1,0:T(8,128)S(1)}, f32[2,4,64,256]{3,2,1,0:T(8,128)S(1)}, u32[]{:S(2)}, u32[]{:S(2)}) %collective-permute-start.3) | collective-permute-done | bytes 524320 | tf_op jit(solution)/shard_map/ppermute | solution.py:297
  44.4 1.4 %outer_step.5.other.half.prev.out2 = f32[2,4,64,256]{3,2,1,0:T(8,128)S(1)} custom-call(f32[2,4,64,256]{3,2,1,0:T(8,128)S(1)} %outer_step.4.other.half.prev, f32[2,4,64,256]{3,2,1,0:T(8,128)S(1)} %inner_step.4.half.other.prev, f32[2,4,64,256]{3,2,1,0:T(8,128)S(1)} %collective-permute-done.3.halo, f32[2,4,64,256]{3,2,1,0:T(8,128)S(1)} %gather.3.other.half.prev, ...), custom_call_target="tpu_custom_call" | custom-call | tf_op jit(solution)/shard_map/outer_step/pallas_call | solution.py:154
  45.9 4.4 %collective-permute-start.5 = (f32[2,4,64,256]{3,2,1,0:T(8,128)S(1)}, f32[2,4,64,256]{3,2,1,0:T(8,128)S(1)}, u32[]{:S(2)}, u32[]{:S(2)}) collective-permute-start(f32[2,4,64,256]{3,2,1,0:T(8,128)S(1)} %outer_step.5.other.half.prev.out2), channel_id=1, source_target_pairs={{1,2},{3,4},{5,6},{7,8},{9,10},{11,12},{13,14},{2,1},{4,3},{6,5},{... | collective-permute-start | bytes 1572872 | tf_op jit(solution)/shard_map/ppermute | solution.py:297
  50.3 0.0 collective-permute-done.4.halo.hal2
  50.3 1.5 %inner_step.6.half.other = f32[2,4,64,256]{3,2,1,0:T(8,128)S(1)} custom-call(f32[2,4,64,256]{3,2,1,0:T(8,128)S(1)} %inner_step.5.half.other.prev.in2, f32[2,4,64,256]{3,2,1,0:T(8,128)S(1)} %outer_step.5.other.half.prev.out2, f32[2,4,64,256]{3,2,1,0:T(8,128)S(1)} %collective-permute-done.4.halo.hal2, f32[2,4,64,256]{3,2,1,0:T(8,128)S(1)} %inner_step.4.half.other.prev, ...), custom_call_target="tpu_custom_call" | custom-call | tf_op jit(solution)/shard_map/inner_step/pallas_call | solution.py:154
  51.8 0.1 collective-permute-start.6
  51.9 5.5 %collective-permute-done.5.halo = f32[2,4,64,256]{3,2,1,0:T(8,128)S(1)} collective-permute-done((f32[2,4,64,256]{3,2,1,0:T(8,128)S(1)}, f32[2,4,64,256]{3,2,1,0:T(8,128)S(1)}, u32[]{:S(2)}, u32[]{:S(2)}) %collective-permute-start.5) | collective-permute-done | bytes 524320 | tf_op jit(solution)/shard_map/ppermute | solution.py:297
  57.4 0.0 slice-start
  57.4 1.5 %outer_step.6.other.half = f32[2,4,64,256]{3,2,1,0:T(8,128)S(1)} custom-call(f32[2,4,64,256]{3,2,1,0:T(8,128)S(1)} %outer_step.5.other.half.prev.out2, f32[2,4,64,256]{3,2,1,0:T(8,128)S(1)} %inner_step.5.half.other.prev.in2, f32[2,4,64,256]{3,2,1,0:T(8,128)S(1)} %collective-permute-done.5.halo, f32[2,4,64,256]{3,2,1,0:T(8,128)S(1)} %outer_step.4.other.half.prev, ...), custom_call_target="tpu_custom_call" | custom-call | tf_op jit(solution)/shard_map/outer_step/pallas_call | solution.py:154
  58.9 0.0 copy-start.10
  58.9 0.0 slice-start.1
  58.9 0.0 copy-start.9
  58.9 4.5 %collective-permute-start.7 = (f32[2,4,64,256]{3,2,1,0:T(8,128)S(1)}, f32[2,4,64,256]{3,2,1,0:T(8,128)S(1)}, u32[]{:S(2)}, u32[]{:S(2)}) collective-permute-start(f32[2,4,64,256]{3,2,1,0:T(8,128)S(1)} %outer_step.6.other.half), channel_id=1, source_target_pairs={{1,2},{3,4},{5,6},{7,8},{9,10},{11,12},{13,14},{2,1},{4,3},{6,5},{... | collective-permute-start | bytes 1572872 | tf_op jit(solution)/shard_map/ppermute | solution.py:297
  63.4 0.0 collective-permute-done.6.halo
  63.5 1.5 %inner_step.7.in4.other = f32[2,4,64,256]{3,2,1,0:T(8,128)S(1)} custom-call(f32[2,4,64,256]{3,2,1,0:T(8,128)S(1)} %inner_step.6.half.other, f32[2,4,64,256]{3,2,1,0:T(8,128)S(1)} %outer_step.6.other.half, f32[2,4,64,256]{3,2,1,0:T(8,128)S(1)} %collective-permute-done.6.halo, f32[2,4,64,256]{3,2,1,0:T(8,128)S(1)} %inner_step.5.half.other.prev.in2, ...), custom_call_target="tpu_custom_call" | custom-call | tf_op jit(solution)/shard_map/inner_step/pallas_call | solution.py:154
  64.9 0.1 collective-permute-start.8
  65.0 5.5 %collective-permute-done.7.halo = f32[2,4,64,256]{3,2,1,0:T(8,128)S(1)} collective-permute-done((f32[2,4,64,256]{3,2,1,0:T(8,128)S(1)}, f32[2,4,64,256]{3,2,1,0:T(8,128)S(1)}, u32[]{:S(2)}, u32[]{:S(2)}) %collective-permute-start.7) | collective-permute-done | bytes 524320 | tf_op jit(solution)/shard_map/ppermute | solution.py:297
  70.5 1.5 %outer_step.7.out4.half = f32[2,4,64,256]{3,2,1,0:T(8,128)S(1)} custom-call(f32[2,4,64,256]{3,2,1,0:T(8,128)S(1)} %outer_step.6.other.half, f32[2,4,64,256]{3,2,1,0:T(8,128)S(1)} %inner_step.6.half.other, f32[2,4,64,256]{3,2,1,0:T(8,128)S(1)} %collective-permute-done.7.halo, f32[2,4,64,256]{3,2,1,0:T(8,128)S(1)} %outer_step.5.other.half.prev.out2, ...), custom_call_target="tpu_custom_call" | custom-call | tf_op jit(solution)/shard_map/outer_step/pallas_call | solution.py:154
  72.0 4.4 %collective-permute-start.9 = (f32[2,4,64,256]{3,2,1,0:T(8,128)S(1)}, f32[2,4,64,256]{3,2,1,0:T(8,128)S(1)}, u32[]{:S(2)}, u32[]{:S(2)}) collective-permute-start(f32[2,4,64,256]{3,2,1,0:T(8,128)S(1)} %outer_step.7.out4.half), channel_id=1, source_target_pairs={{1,2},{3,4},{5,6},{7,8},{9,10},{11,12},{13,14},{2,1},{4,3},{6,5},{... | collective-permute-start | bytes 1572872 | tf_op jit(solution)/shard_map/ppermute | solution.py:297
  76.4 0.0 copy-done.10
  76.4 0.1 fusion.mute
  76.6 0.0 slice-done
  76.6 0.0 slice-done.1
  76.6 0.0 copy-done.9
  76.6 1.6 %image_mid.1.part = f32[9,4,64,256]{3,2,1,0:T(8,128)S(1)} custom-call(f32[9,8,64,256]{3,2,1,0:T(8,128)S(1)} %bitcast.16, s32[9]{0:T(128)S(1)} %copy-done.9, f32[8,64,256]{2,1,0:T(8,128)S(1)} %fusion.mute, f32[2,4,64,256]{3,2,1,0:T(8,128)S(1)} %outer_step.5.other.half.prev.out2, f32[2,4,64,256]{3,2,1,0:T(8,128)S(1)} %inner_step.5.half.other.prev.in2, ...), custom_call_target="tpu_custom_call" | custom-call | tf_op jit(solution)/shard_map/image_mid/pallas_call | solution.py:209
  78.2 0.0 collective-permute-done.8.hal4
  78.2 3.4 %image_inner.1 = (f32[9,8,64,256]{3,2,1,0:T(8,128)}, f32[8,64,256]{2,1,0:T(8,128)}, f32[8,64,256]{2,1,0:T(8,128)}) custom-call(f32[9,8,64,256]{3,2,1,0:T(8,128)S(1)} %bitcast.17, s32[9]{0:T(128)S(1)} %copy-done.9, f32[8,64,256]{2,1,0:T(8,128)S(1)} %fusion.mute, f32[2,4,64,256]{3,2,1,0:T(8,128)S(1)} %inner_step.5.half.other.prev.in2, ...), custom_call_target="tpu_custom_call" | custom-call | tf_op jit(solution)/shard_map/image_inner/pallas_call | solution.py:251
  81.6 1.9 %collective-permute-done.9.halo = f32[2,4,64,256]{3,2,1,0:T(8,128)S(1)} collective-permute-done((f32[2,4,64,256]{3,2,1,0:T(8,128)S(1)}, f32[2,4,64,256]{3,2,1,0:T(8,128)S(1)}, u32[]{:S(2)}, u32[]{:S(2)}) %collective-permute-start.9) | collective-permute-done | bytes 524320 | tf_op jit(solution)/shard_map/ppermute | solution.py:297
  83.5 3.0 %image_last.1 = f32[9,8,64,256]{3,2,1,0:T(8,128)} custom-call(f32[9,8,64,256]{3,2,1,0:T(8,128)} %get-tuple-element.16.image_old, f32[9,4,64,256]{3,2,1,0:T(8,128)S(1)} %image_mid.1.part, s32[9]{0:T(128)S(1)} %copy-done.9, f32[8,64,256]{2,1,0:T(8,128)S(1)} %fusion.mute, f32[2,4,64,256]{3,2,1,0:T(8,128)S(1)} %outer_step.7.out4.half, ...), custom_call_target="tpu_custom_call", output_to_operand_aliasing={{}: (0, {})} | custom-call | tf_op jit(solution)/shard_map/image_last/pallas_call | solution.py:278
  (1 shorter events, 0.0 us)
Async XLA Ops:
  0.6 17.6 %copy-start.1 = (bf16[2,256,256]{2,1,0:T(8,128)(2,1)S(1)}, bf16[2,256,256]{2,1,0:T(8,128)(2,1)}, u32[]{:S(2)}) copy-start(bf16[2,256,256]{2,1,0:T(8,128)(2,1)} %constant.5.clone.wy) | copy-start | bytes 786436
  0.6 17.6 %copy-start = (bf16[4,256,256]{2,1,0:T(8,128)(2,1)S(1)}, bf16[4,256,256]{2,1,0:T(8,128)(2,1)}, u32[]{:S(2)}) copy-start(bf16[4,256,256]{2,1,0:T(8,128)(2,1)} %constant.4.clone.wz) | copy-start | bytes 1572868
  0.7 1.1 %copy-start.2 = (f32[1,8,64,256]{3,2,1,0:T(8,128)S(1)}, f32[1,8,64,256]{3,2,1,0:T(8,128)}, u32[]{:S(2)}) copy-start(f32[1,8,64,256]{3,2,1,0:T(8,128)} %param.13) | copy-start | bytes 1572868
  1.8 1.0 %copy-start.3 = (f32[1,8,64,256]{3,2,1,0:T(8,128)S(1)}, f32[1,8,64,256]{3,2,1,0:T(8,128)}, u32[]{:S(2)}) copy-start(f32[1,8,64,256]{3,2,1,0:T(8,128)} %param.15) | copy-start | bytes 1572868
  2.8 1.0 %copy-start.4 = (f32[1,8,64,256]{3,2,1,0:T(8,128)S(1)}, f32[1,8,64,256]{3,2,1,0:T(8,128)}, u32[]{:S(2)}) copy-start(f32[1,8,64,256]{3,2,1,0:T(8,128)} %param.12) | copy-start | bytes 1572868
  3.9 1.0 %copy-start.5 = (f32[1,8,64,256]{3,2,1,0:T(8,128)S(1)}, f32[1,8,64,256]{3,2,1,0:T(8,128)}, u32[]{:S(2)}) copy-start(f32[1,8,64,256]{3,2,1,0:T(8,128)} %param.14) | copy-start | bytes 1572868
  4.9 1.0 %copy-start.6 = (f32[1,8,64,256]{3,2,1,0:T(8,128)S(1)}, f32[1,8,64,256]{3,2,1,0:T(8,128)}, u32[]{:S(2)}) copy-start(f32[1,8,64,256]{3,2,1,0:T(8,128)} %param.16) | copy-start | bytes 1572868
  5.9 1.0 %copy-start.7 = (f32[1,8,64,256]{3,2,1,0:T(8,128)S(1)}, f32[1,8,64,256]{3,2,1,0:T(8,128)}, u32[]{:S(2)}) copy-start(f32[1,8,64,256]{3,2,1,0:T(8,128)} %param.17) | copy-start | bytes 1572868
  7.0 1.0 %copy-start.8 = (f32[1,8,64,256]{3,2,1,0:T(8,128)S(1)}, f32[1,8,64,256]{3,2,1,0:T(8,128)}, u32[]{:S(2)}) copy-start(f32[1,8,64,256]{3,2,1,0:T(8,128)} %param.18) | copy-start | bytes 1572868
  12.8 5.4 %collective-permute-start = (f32[2,4,64,256]{3,2,1,0:T(8,128)S(1)}, f32[2,4,64,256]{3,2,1,0:T(8,128)S(1)}, u32[]{:S(2)}, u32[]{:S(2)}) collective-permute-start(f32[2,4,64,256]{3,2,1,0:T(8,128)S(1)} %get-tuple-element.11.half.other.prev), channel_id=1, source_target_pairs={{0,1},{1,0},{2,3},{3,2},{4,5},{5,4},{6,7},{7,6},{8,9},{9,8},{10,11... | collective-permute-start | bytes 1572872 | tf_op jit(solution)/shard_map/ppermute | solution.py:301
  13.7 16.3 %collective-permute-start.1 = (f32[2,4,64,256]{3,2,1,0:T(8,128)S(1)}, f32[2,4,64,256]{3,2,1,0:T(8,128)S(1)}, u32[]{:S(2)}, u32[]{:S(2)}) collective-permute-start(f32[2,4,64,256]{3,2,1,0:T(8,128)S(1)} %gather.3.other.half.prev), channel_id=1, source_target_pairs={{1,2},{3,4},{5,6},{7,8},{9,10},{11,12},{13,14},{2,1},{4,3},{6,5},{... | collective-permute-start | bytes 1572872 | tf_op jit(solution)/shard_map/ppermute | solution.py:297
  19.7 16.1 %collective-permute-start.2 = (f32[2,4,64,256]{3,2,1,0:T(8,128)S(1)}, f32[2,4,64,256]{3,2,1,0:T(8,128)S(1)}, u32[]{:S(2)}, u32[]{:S(2)}) collective-permute-start(f32[2,4,64,256]{3,2,1,0:T(8,128)S(1)} %inner_step.4.half.other.prev), channel_id=1, source_target_pairs={{0,1},{1,0},{2,3},{3,2},{4,5},{5,4},{6,7},{7,6},{8,9},{9,8},{10,11... | collective-permute-start | bytes 1572872 | tf_op jit(solution)/shard_map/ppermute | solution.py:301
  31.4 13.0 %collective-permute-start.3 = (f32[2,4,64,256]{3,2,1,0:T(8,128)S(1)}, f32[2,4,64,256]{3,2,1,0:T(8,128)S(1)}, u32[]{:S(2)}, u32[]{:S(2)}) collective-permute-start(f32[2,4,64,256]{3,2,1,0:T(8,128)S(1)} %outer_step.4.other.half.prev), channel_id=1, source_target_pairs={{1,2},{3,4},{5,6},{7,8},{9,10},{11,12},{13,14},{2,1},{4,3},{6,5},{... | collective-permute-start | bytes 1572872 | tf_op jit(solution)/shard_map/ppermute | solution.py:297
  37.3 13.0 %collective-permute-start.4 = (f32[2,4,64,256]{3,2,1,0:T(8,128)S(1)}, f32[2,4,64,256]{3,2,1,0:T(8,128)S(1)}, u32[]{:S(2)}, u32[]{:S(2)}) collective-permute-start(f32[2,4,64,256]{3,2,1,0:T(8,128)S(1)} %inner_step.5.half.other.prev.in2), channel_id=1, source_target_pairs={{0,1},{1,0},{2,3},{3,2},{4,5},{5,4},{6,7},{7,6},{8,9},{9,8},{10,11... | collective-permute-start | bytes 1572872 | tf_op jit(solution)/shard_map/ppermute | solution.py:301
  45.9 11.5 %collective-permute-start.5 = (f32[2,4,64,256]{3,2,1,0:T(8,128)S(1)}, f32[2,4,64,256]{3,2,1,0:T(8,128)S(1)}, u32[]{:S(2)}, u32[]{:S(2)}) collective-permute-start(f32[2,4,64,256]{3,2,1,0:T(8,128)S(1)} %outer_step.5.other.half.prev.out2), channel_id=1, source_target_pairs={{1,2},{3,4},{5,6},{7,8},{9,10},{11,12},{13,14},{2,1},{4,3},{6,5},{... | collective-permute-start | bytes 1572872 | tf_op jit(solution)/shard_map/ppermute | solution.py:297
  51.8 11.6 %collective-permute-start.6 = (f32[2,4,64,256]{3,2,1,0:T(8,128)S(1)}, f32[2,4,64,256]{3,2,1,0:T(8,128)S(1)}, u32[]{:S(2)}, u32[]{:S(2)}) collective-permute-start(f32[2,4,64,256]{3,2,1,0:T(8,128)S(1)} %inner_step.6.half.other), channel_id=1, source_target_pairs={{0,1},{1,0},{2,3},{3,2},{4,5},{5,4},{6,7},{7,6},{8,9},{9,8},{10,11... | collective-permute-start | bytes 1572872 | tf_op jit(solution)/shard_map/ppermute | solution.py:301
  57.4 19.2 %slice-start = ((s8[4718592]{0:T(1024)(128)(4,1)}), s8[4194304]{0:T(1024)(128)(4,1)S(1)}, s32[]{:S(2)}) async-start(s8[4718592]{0:T(1024)(128)(4,1)} %bitcast.14), calls=%async_computation | async-start | bytes 8388608
  58.9 17.6 %copy-start.10 = (s32[1,8,64]{2,1,0:T(8,128)S(1)}, s32[1,8,64]{2,1,0:T(8,128)}, u32[]{:S(2)}) copy-start(s32[1,8,64]{2,1,0:T(8,128)} %param.19) | copy-start | bytes 6148
  58.9 17.7 %slice-start.1 = ((s8[4718592]{0:T(1024)(128)(4,1)}), s8[524288]{0:T(1024)(128)(4,1)S(1)}, s32[]{:S(2)}) async-start(s8[4718592]{0:T(1024)(128)(4,1)} %bitcast.14), calls=%async_computation.1 | async-start | bytes 1048576
  58.9 17.7 %copy-start.9 = (s32[9]{0:T(128)S(1)}, s32[9]{0:T(128)}, u32[]{:S(2)}) copy-start(s32[9]{0:T(128)} %offsets.5) | copy-start | bytes 112
  58.9 11.6 %collective-permute-start.7 = (f32[2,4,64,256]{3,2,1,0:T(8,128)S(1)}, f32[2,4,64,256]{3,2,1,0:T(8,128)S(1)}, u32[]{:S(2)}, u32[]{:S(2)}) collective-permute-start(f32[2,4,64,256]{3,2,1,0:T(8,128)S(1)} %outer_step.6.other.half), channel_id=1, source_target_pairs={{1,2},{3,4},{5,6},{7,8},{9,10},{11,12},{13,14},{2,1},{4,3},{6,5},{... | collective-permute-start | bytes 1572872 | tf_op jit(solution)/shard_map/ppermute | solution.py:297
  64.9 13.3 %collective-permute-start.8 = (f32[2,4,64,256]{3,2,1,0:T(8,128)S(1)}, f32[2,4,64,256]{3,2,1,0:T(8,128)S(1)}, u32[]{:S(2)}, u32[]{:S(2)}) collective-permute-start(f32[2,4,64,256]{3,2,1,0:T(8,128)S(1)} %inner_step.7.in4.other), channel_id=1, source_target_pairs={{0,1},{1,0},{2,3},{3,2},{4,5},{5,4},{6,7},{7,6},{8,9},{9,8},{10,11... | collective-permute-start | bytes 1572872 | tf_op jit(solution)/shard_map/ppermute | solution.py:301
  72.0 11.5 %collective-permute-start.9 = (f32[2,4,64,256]{3,2,1,0:T(8,128)S(1)}, f32[2,4,64,256]{3,2,1,0:T(8,128)S(1)}, u32[]{:S(2)}, u32[]{:S(2)}) collective-permute-start(f32[2,4,64,256]{3,2,1,0:T(8,128)S(1)} %outer_step.7.out4.half), channel_id=1, source_target_pairs={{1,2},{3,4},{5,6},{7,8},{9,10},{11,12},{13,14},{2,1},{4,3},{6,5},{... | collective-permute-start | bytes 1572872 | tf_op jit(solution)/shard_map/ppermute | solution.py:297

commit v2 on v1

v2 whole, which is shorter than its diff:
```python
import functools

import jax
import jax.numpy as jnp
import numpy as np
from jax import lax
from jax.experimental import pallas as pl
from jax.experimental.pallas import tpu as pltpu
from jax.sharding import PartitionSpec as P

STEPS = 4
RAD = 4
HMAX = 4
NOFF = 9

second_w = (-205.0 / 72.0, 8.0 / 5.0, -1.0 / 5.0, 8.0 / 315.0, -1.0 / 560.0)
first_w = (4.0 / 5.0, -1.0 / 5.0, 4.0 / 105.0, -1.0 / 280.0)

VMEM = pl.BlockSpec(memory_space=pltpu.VMEM)
SMEM = pl.BlockSpec(memory_space=pltpu.SMEM)
ANY = pl.BlockSpec(memory_space=pl.ANY)
HBM = pl.BlockSpec(memory_space=pltpu.HBM)
MIB = 1 << 20
CHEAP = pl.CostEstimate(flops=1, transcendentals=0, bytes_accessed=1)


def parity():
    return lax.rem(lax.axis_index("blk"), 2)


def is_flipped(inner):
    odd = parity()
    return 1 - odd if inner else odd


def natural(plane, flipped):
    return plane + flipped * (7 - 2 * plane)


def at(half, other, halo, field, position):
    if position < 0:
        return halo.at[field, -1 - position]
    if position < 4:
        return half.at[field, position]
    return other.at[field, 7 - position]


SCALE = 5040
second_int = tuple(round(SCALE * w) for w in second_w)
first_int = tuple(round(840 * w) for w in first_w)
mixed_w = tuple(SCALE / 840 * w for w in first_w)


def bands(depth, rows):
    d = np.arange(depth)[None, :] - np.arange(depth)[:, None]
    r = np.arange(4 * rows)
    dr = np.where(r[None, :] // rows == r[:, None] // rows, r[None, :] - r[:, None], 99)
    dzz, dz = np.zeros(d.shape), np.zeros(d.shape)
    dyy = np.zeros(dr.shape)
    for k in range(1, 5):
        dzz[np.abs(d) == k] = second_int[k]
        dyy[np.abs(dr) == k] = second_int[k]
        dz[d == -k] = first_int[k - 1]
        dz[d == k] = -first_int[k - 1]
    return jnp.asarray(np.stack([dzz, dz]).astype(jnp.bfloat16)), jnp.asarray(dyy.astype(jnp.bfloat16))


def gather_kernel(plan, n_in, *refs):
    ins, outs, sem = refs[:n_in], refs[n_in:-1], refs[-1]
    copies = []
    for out_id, inner, sources in plan:
        flip = is_flipped(inner)
        for i, src in enumerate(sources):
            for m in range(4):
                copies.append(
                    pltpu.make_async_copy(
                        ins[src].at[natural(m, flip)], outs[out_id].at[i, m], sem.at[len(copies)]
                    )
                )
    for c in copies:
        c.start()
    for c in copies:
        c.wait()


def gather(arrays, plan):
    shape = arrays[0].shape[1:]
    arrays = [pltpu.with_memory_space_constraint(a, pltpu.HBM) for a in arrays]
    return pl.pallas_call(
        functools.partial(gather_kernel, plan, len(arrays)),
        out_shape=[jax.ShapeDtypeStruct((len(s), 4) + shape, jnp.float32) for _, _, s in plan],
        in_specs=[HBM] * len(arrays),
        out_specs=[VMEM] * len(plan),
        scratch_shapes=[pltpu.SemaphoreType.DMA((sum(4 * len(s) for _, _, s in plan),))],
        cost_estimate=CHEAP,
        compiler_params=pltpu.CompilerParams(vmem_limit_bytes=8 * MIB),
        name="gather",
    )(*arrays)


CHUNK = 16
dot = functools.partial(jnp.dot, preferred_element_type=jnp.float32)


def split(value):
    high = value.astype(jnp.bfloat16)
    return high, (value - high.astype(jnp.float32)).astype(jnp.bfloat16)


def advance(inner, half, other, halo, prev, coef, wz, wy, out, v_hi, v_lo, x_hi, x_lo, horiz):
    rows = half.shape[2]
    sign = (1 - 2 * is_flipped(inner)).astype(jnp.float32)
    wx = [sign * w for w in mixed_w]

    def first(i, carry):
        r = pl.multiple_of(i * CHUNK, CHUNK)
        span = pl.ds(r, CHUNK)
        for f in range(2):
            low = 0 if halo is None else -4
            line = {q: at(half, other, halo, f, q)[span] for q in range(low, 8)}
            for m in range(4):
                center = line[m]
                hx = (2.0 * SCALE * second_w[0]) * center
                dx = None
                for k in range(1, 5):
                    up = line[m + k]
                    if m - k in line:
                        both, t = up + line[m - k], up - line[m - k]
                    else:
                        both, t = up, up
                    hx = hx + float(second_int[k]) * both
                    t = wx[k - 1] * t
                    dx = t if dx is None else dx + t
                horiz[f, m, span] = hx
                at_row = pl.ds(pl.multiple_of((f * 4 + m) * rows + r, CHUNK), CHUNK)
                v_hi[at_row], v_lo[at_row] = split(center)
                x_hi[at_row], x_lo[at_row] = split(dx)
        return carry

    lax.fori_loop(0, rows // CHUNK, first, 0)
    for f in range(2):
        part = pl.ds(f * 4 * rows, 4 * rows)
        vh, vl, xh, xl = v_hi[part], v_lo[part], x_hi[part], x_lo[part]
        zz = dot(vh, wz[0]) + dot(vl, wz[0])
        zx = dot(xh, wz[1]) + dot(xl, wz[1])
        yy = dot(wy[...], vh) + dot(wy[...], vl)
        for m in range(4):
            cut = slice(m * rows, (m + 1) * rows)
            center = half[f, m]
            out[f, m] = (
                2.0 * center
                - prev[f, m]
                + (1.0 / SCALE)
                * (
                    coef[0, m] * (horiz[f, m] + yy[cut])
                    + coef[1, m] * (zz[cut] + (SCALE * second_w[0]) * center)
                    + coef[2, m] * zx[cut]
                )
            )


def under_kernel(
    inn, out, near, prev_inn, prev_out, coef_inn, coef_out, wz, wy, new_inn, base, *scratch
):
    advance(True, inn, out, near, prev_inn, coef_inn, wz, wy, new_inn, *scratch)
    advance(False, out, inn, None, prev_out, coef_out, wz, wy, base, *scratch)


def first_under_kernel(
    inn, out, near, wz, wy, source_prev, receiver_prev, coef_a, coef_b, coef_c,
    new_inn, base, coef_inn, coef_out, prev_inn, prev_out, sem, *scratch
):
    prevs = (source_prev, receiver_prev)
    coefs = (coef_a, coef_b, coef_c)
    copies = []
    for inner, prev, coef in ((True, prev_inn, coef_inn), (False, prev_out, coef_out)):
        for sources, target in ((coefs, coef), (prevs, prev)):
            for i, source in enumerate(sources):
                for m in range(4):
                    copies.append(
                        pltpu.make_async_copy(
                            source.at[natural(m, is_flipped(inner))], target.at[i, m], sem.at[len(copies)]
                        )
                    )
    for c in copies:
        c.start()
    for c in copies[:20]:
        c.wait()
    advance(True, inn, out, near, prev_inn, coef_inn, wz, wy, new_inn, *scratch)
    for c in copies[20:]:
        c.wait()
    advance(False, out, inn, None, prev_out, coef_out, wz, wy, base, *scratch)


def work_space(rows, depth):
    flat = pltpu.VMEM((8 * rows, depth), jnp.bfloat16)
    return [flat] * 4 + [pltpu.VMEM((2, 4, rows, depth), jnp.float32)]


def first_under(inn, out, near, wz, wy, arrays):
    rows, depth = inn.shape[2:]
    arrays = [pltpu.with_memory_space_constraint(a, pltpu.HBM) for a in arrays]
    pair = jax.ShapeDtypeStruct((2, 4, rows, depth), jnp.float32)
    three = jax.ShapeDtypeStruct((3, 4, rows, depth), jnp.float32)
    half = pltpu.VMEM((2, 4, rows, depth), jnp.float32)
    return pl.pallas_call(
        first_under_kernel,
        out_shape=[pair, pair, three, three],
        in_specs=[VMEM] * 5 + [HBM] * 5,
        out_specs=[VMEM] * 4,
        scratch_shapes=[half, half, pltpu.SemaphoreType.DMA((40,))] + work_space(rows, depth),
        cost_estimate=CHEAP,
        compiler_params=pltpu.CompilerParams(vmem_limit_bytes=12 * MIB),
        name="first_under",
    )(inn, out, near, wz, wy, *arrays)


def under(inn, out, near, prev_inn, prev_out, coef_inn, coef_out, wz, wy):
    shape = jax.ShapeDtypeStruct(inn.shape, jnp.float32)
    return pl.pallas_call(
        under_kernel,
        out_shape=[shape, shape],
        in_specs=[VMEM] * 9,
        out_specs=[VMEM] * 2,
        scratch_shapes=work_space(*inn.shape[2:]),
        cost_estimate=CHEAP,
        compiler_params=pltpu.CompilerParams(vmem_limit_bytes=12 * MIB),
        name="under",
    )(inn, out, near, prev_inn, prev_out, coef_inn, coef_out, wz, wy)


def finish_kernel(halo, base, coef, wz, out, hi, lo):
    rows = halo.shape[2]
    sign = (1 - 2 * is_flipped(False)).astype(jnp.float32)
    wx = [sign * w for w in mixed_w]
    for f in range(2):
        for j in range(4):
            at_row = pl.ds((f * 4 + j) * rows, rows)
            hi[at_row], lo[at_row] = split(halo[f, j])
    for f in range(2):
        part = pl.ds(f * 4 * rows, 4 * rows)
        dz = dot(hi[part], wz[1]) + dot(lo[part], wz[1])
        for m in range(4):
            hx = zx = None
            for k in range(m + 1, 5):
                j = k - m - 1
                t = float(second_int[k]) * halo[f, j]
                hx = t if hx is None else hx + t
                t = wx[k - 1] * dz[j * rows : (j + 1) * rows]
                zx = t if zx is None else zx + t
            out[f, m] = base[f, m] + (1.0 / SCALE) * (coef[0, m] * hx - coef[2, m] * zx)


def finish(halo, base, coef, wz):
    rows, depth = halo.shape[2:]
    return pl.pallas_call(
        finish_kernel,
        out_shape=jax.ShapeDtypeStruct(halo.shape, jnp.float32),
        in_specs=[VMEM] * 4,
        out_specs=VMEM,
        scratch_shapes=[pltpu.VMEM((8 * rows, depth), jnp.bfloat16)] * 2,
        cost_estimate=CHEAP,
        compiler_params=pltpu.CompilerParams(vmem_limit_bytes=8 * MIB),
        name="finish",
    )(halo, base, coef, wz)


def find_slots(offsets, slots):
    for k in range(NOFF):
        slots[offsets[k]] = k


def slot_of(slots, inner, h):
    return slots[(1 - 2 * is_flipped(inner)) * h + HMAX]


BY_REACH = (-4, 4, -3, 3, -2, 2, -1, 1, 0)


def add_terms(old, new, slot, h, planes, mute, snaps, inner):
    flip = is_flipped(inner)
    rows = old.shape[2]

    def body(i, carry):
        span = pl.ds(pl.multiple_of(i * CHUNK, CHUNK), CHUNK)
        for m in planes:
            total = None
            for half, other, halo in snaps:
                t = at(half, other, halo, 0, m - h)[span] * at(half, other, halo, 1, m + h)[span]
                total = t if total is None else total + t
            local = m + flip * (3 - 2 * m)
            new[slot, local, span] = old[slot, local, span] + mute[natural(m, flip), span] * total
        return carry

    lax.fori_loop(0, rows // CHUNK, body, 0)


def store_planes(buffer, image, slot, first, count, inner, sem):
    flip = is_flipped(inner)
    start = first + flip * (4 - 2 * first - count)
    return pltpu.make_async_copy(
        buffer.at[slot, pl.ds(start, count)], image.at[slot, pl.ds(4 * flip + start, count)], sem
    )


def image_mid_kernel(image_in, offsets, mute, half, other, halo, acc, slots, sem):
    find_slots(offsets, slots)
    near = pl.ds(4 * is_flipped(False), 4)
    slot = [slot_of(slots, False, h) for h in BY_REACH]
    copies = [
        pltpu.make_async_copy(image_in.at[k, near], acc.at[k], sem.at[i])
        for i, k in enumerate(slot)
    ]
    for c in copies:
        c.start()
    for i, h in enumerate(BY_REACH):
        copies[i].wait()
        add_terms(acc, acc, slot[i], h, range(4), mute, [(half, other, halo)], False)


def image_mid(image_in, offsets, mute, half, other, halo):
    shape = (NOFF, 4) + half.shape[2:]
    return pl.pallas_call(
        image_mid_kernel,
        out_shape=jax.ShapeDtypeStruct(shape, jnp.float32),
        in_specs=[HBM, SMEM] + [VMEM] * 4,
        out_specs=VMEM,
        scratch_shapes=[pltpu.SMEM((NOFF,), jnp.int32), pltpu.SemaphoreType.DMA((NOFF,))],
        cost_estimate=CHEAP,
        compiler_params=pltpu.CompilerParams(vmem_limit_bytes=8 * MIB),
        name="image_mid",
    )(image_in, offsets, mute, half, other, halo)


def image_main_kernel(
    image_in, part, offsets, mute, in2, out2, hal2, in4, out4, hal4,
    image, src, rec, acc, done, slots, sem, sems,
):
    find_slots(offsets, slots)
    inner_half = pl.ds(4 * is_flipped(True), 4)
    inner_slot = [slot_of(slots, True, h) for h in BY_REACH]
    outer_slot = [slot_of(slots, False, h) for h in BY_REACH]
    fetches = [
        pltpu.make_async_copy(image_in.at[k, inner_half], acc.at[k], sem.at[i])
        for i, k in enumerate(inner_slot)
    ]
    for c in fetches:
        c.start()
    copies = []
    for inner, field4 in ((True, in4), (False, out4)):
        for f, last in ((0, src), (1, rec)):
            for m in range(4):
                copies.append(
                    pltpu.make_async_copy(
                        field4.at[f, m], last.at[natural(m, is_flipped(inner))], sems.at[len(copies)]
                    )
                )
    for c in copies:
        c.start()
    stores = []
    for i, h in enumerate(BY_REACH):
        reach = abs(h)
        if reach == 4:
            continue
        k = outer_slot[i]
        add_terms(part, done, k, h, range(reach, 4), mute, [(out4, in4, None)], False)
        stores.append(store_planes(done, image, k, reach, 4 - reach, False, sem.at[NOFF + i]))
        stores[-1].start()
    for i, h in enumerate(BY_REACH):
        fetches[i].wait()
        k = inner_slot[i]
        add_terms(acc, acc, k, h, range(4), mute, [(in2, out2, hal2), (in4, out4, hal4)], True)
        stores.append(store_planes(acc, image, k, 0, 4, True, sem.at[i]))
        stores[-1].start()
    for c in copies + stores:
        c.wait()


def image_main(image_in, part, offsets, mute, snap2, snap4):
    shape = snap2[0].shape
    field = jax.ShapeDtypeStruct((8,) + shape[2:], jnp.float32)
    return pl.pallas_call(
        image_main_kernel,
        out_shape=[jax.ShapeDtypeStruct(image_in.shape, jnp.float32), field, field],
        in_specs=[HBM, VMEM, SMEM] + [VMEM] * 7,
        out_specs=[HBM] * 3,
        scratch_shapes=[
            pltpu.VMEM(part.shape, jnp.float32),
            pltpu.VMEM(part.shape, jnp.float32),
            pltpu.SMEM((NOFF,), jnp.int32),
            pltpu.SemaphoreType.DMA((2 * NOFF,)),
            pltpu.SemaphoreType.DMA((16,)),
        ],
        cost_estimate=CHEAP,
        compiler_params=pltpu.CompilerParams(vmem_limit_bytes=8 * MIB),
        name="image_main",
    )(image_in, part, offsets, mute, *snap2, *snap4)


def image_last_kernel(image_old, part, offsets, mute, half, other, halo, image, done, slots, sem):
    del image_old
    find_slots(offsets, slots)
    stores = []
    for i, h in enumerate(BY_REACH[:-1]):
        reach = abs(h)
        k = slot_of(slots, False, h)
        add_terms(part, done, k, h, range(reach), mute, [(half, other, halo)], False)
        stores.append(store_planes(done, image, k, 0, reach, False, sem.at[i]))
        stores[-1].start()
    for c in stores:
        c.wait()


def image_last(image, part, offsets, mute, snap4):
    return pl.pallas_call(
        image_last_kernel,
        out_shape=jax.ShapeDtypeStruct(image.shape, jnp.float32),
        in_specs=[HBM, VMEM, SMEM] + [VMEM] * 4,
        out_specs=HBM,
        scratch_shapes=[
            pltpu.VMEM(part.shape, jnp.float32),
            pltpu.SMEM((NOFF,), jnp.int32),
            pltpu.SemaphoreType.DMA((NOFF,)),
        ],
        input_output_aliases={0: 0},
        cost_estimate=CHEAP,
        compiler_params=pltpu.CompilerParams(vmem_limit_bytes=8 * MIB),
        name="image_last",
    )(image, part, offsets, mute, *snap4)


def across_chips(value, start=1, stride=2):
    count = lax.axis_size("blk")
    pairs = [(i, i + 1) for i in range(start, count - 1, stride)]
    return lax.ppermute(value, "blk", pairs + [(b, a) for a, b in pairs])


def within_chip(value):
    return lax.ppermute(value, "blk", [(i, i ^ 1) for i in range(lax.axis_size("blk"))])


def per_device(
    source_prev,
    source_cur,
    receiver_prev,
    receiver_cur,
    coef_horiz,
    coef_vert,
    coef_mixed,
    live_depth,
    offsets,
    image_in,
):
    source_prev, source_cur = source_prev[0], source_cur[0]
    receiver_prev, receiver_cur = receiver_prev[0], receiver_cur[0]
    coefs = [coef_horiz[0], coef_vert[0], coef_mixed[0]]
    image_in = image_in[:, 0]
    rows, depth = source_cur.shape[1:]
    wz, wy = bands(depth, rows)
    depth_ids = lax.broadcasted_iota(jnp.int32, source_cur.shape, 2)
    mute = (depth_ids < live_depth[0][:, :, None]).astype(jnp.float32)

    out, inn = gather([source_cur, receiver_cur], [(0, False, (0, 1)), (1, True, (0, 1))])
    far = across_chips(out)
    near = within_chip(inn)
    new_inn, base, coef_inn, coef_out = first_under(
        inn, out, near, wz, wy, [source_prev, receiver_prev] + coefs
    )
    for n in range(STEPS):
        if n == STEPS // 2 + 1:
            inn, part = lax.optimization_barrier((inn, part))
        if n > 0:
            new_inn, base = under(inn, out, near, prev_inn, prev_out, coef_inn, coef_out, wz, wy)
        new_out = finish(far, base, coef_out, wz)
        if n == STEPS // 2:
            snap2 = (inn, out, near)
            part = image_mid(image_in, offsets, mute, out, inn, far)
        prev_inn, prev_out, inn, out = inn, out, new_inn, new_out
        near = within_chip(inn)
        far = across_chips(out)
    image, source_last, receiver_last = image_main(
        image_in, part, offsets, mute, snap2, (inn, out, near)
    )
    image = image_last(image, part, offsets, mute, (out, inn, far))
    return (image[:, None], source_last[None], receiver_last[None])


def solution(mesh):
    in_specs = (
        P(("shots", "blk"), None, None, None),
        P(("shots", "blk"), None, None, None),
        P(("shots", "blk"), None, None, None),
        P(("shots", "blk"), None, None, None),
        P("blk", None, None, None),
        P("blk", None, None, None),
        P("blk", None, None, None),
        P("blk", None, None),
        P(),
        P(None, ("shots", "blk"), None, None, None),
    )
    out_specs = (
        P(None, ("shots", "blk"), None, None, None),
        P(("shots", "blk"), None, None, None),
        P(("shots", "blk"), None, None, None),
    )
    return jax.shard_map(
        per_device, mesh=mesh, in_specs=in_specs, out_specs=out_specs, check_vma=False
    )
```

time: 87 us -> 72 us (0.83)
  waiting for transfers between devices: 30.2 us -> 24.1 us
  local copies, waits for them, and re-layouts: 7.39 us -> 1.88 us
  Pallas kernels: 25.2 us -> 21.2 us
    ppermute x5, waiting for transfers between devices: 30.2 us -> 24.1 us  [across_chips(): return lax.ppermute(value, 'blk', pairs + [(b, a) for a, b in pairs])]
    unnamed x26 -> x16, local copies, waits for them, and re-layouts: 7.39 us -> 1.88 us
    pallas_call x2 -> x1, Pallas kernels: 5.52 us -> 1.42 us  [gather(): pl.pallas_call(functools.partial(gather_kernel, plan, len(arrays)), out_s...]
    pallas_call x9, Pallas kernels: 15.1 us -> 16.4 us  [the longest x3 7.23 us: under(): pl.pallas_call(under_kernel, out_shape=[shape, shape], in_specs=[VMEM] *...]
    pallas_call x1, Pallas kernels: 2.96 us -> 1.75 us  [image_last(): pl.pallas_call(image_last_kernel, out_shape=jax.ShapeDtypeStruct(image.sh...]
  transfers between devices with their start and end apart: 10 -> 10, of which waited for: 5 -> 5; matrix products, arithmetic and copies ran while one was open for 0% -> 0% of each run, Pallas kernels for 20% -> 25%
where the time goes in v2:
time: 72 us; the launch traced here: 71 us
  waiting for transfers between devices  24.1 us (33%)
  starting transfers between devices  22.7 us (32%)
  Pallas kernels  21.2 us (29%)
  local copies, waits for them, and re-layouts  1.88 us (3%)
  between operations  0.91 us (1%)
    ppermute x5, waiting for transfers between devices, across_chips(): return lax.ppermute(value, 'blk', pairs + [(b, a) for a, b in pairs])  24.1 us
    ppermute x5, starting transfers between devices, across_chips(): return lax.ppermute(value, 'blk', pairs + [(b, a) for a, b in pairs])  22.3 us
    pallas_call x3, Pallas kernels, under(): pl.pallas_call(under_kernel, out_shape=[shape, shape], in_specs=[VMEM] *...  7.23 us
    pallas_call x1, Pallas kernels, first_under(): pl.pallas_call(first_under_kernel, out_shape=[pair, pair, three, three],...  4.08 us
    pallas_call x1, Pallas kernels, image_main(): pl.pallas_call(image_main_kernel, out_shape=[jax.ShapeDtypeStruct(image_i...  3.23 us
    unnamed x16, local copies, waits for them, and re-layouts  1.88 us
    pallas_call x4, Pallas kernels, finish(): pl.pallas_call(finish_kernel, out_shape=jax.ShapeDtypeStruct(halo.shape,...  1.84 us
    pallas_call x1, Pallas kernels, image_last(): pl.pallas_call(image_last_kernel, out_shape=jax.ShapeDtypeStruct(image.sh...  1.75 us
  transfers between devices with their start and end apart: 10, of which 5 were waited for; matrix products, arithmetic and copies ran while one was open for 0% of the time, Pallas kernels for 25%

profile of v2, /device:TPU:1, one launch (start us, length us, event | category | flops | bytes accessed | tf_op | source)
XLA Modules:
  0.0 71.0 jit_solution(3472216711062566186)
XLA Ops:
  0.6 0.0 copy-start.1
  0.6 1.4 %gather.1 = (f32[2,4,64,256]{3,2,1,0:T(8,128)S(1)}, f32[2,4,64,256]{3,2,1,0:T(8,128)S(1)}) custom-call(f32[8,64,256]{2,1,0:T(8,128)} %bitcast.24, f32[8,64,256]{2,1,0:T(8,128)} %bitcast.25), custom_call_target="tpu_custom_call" | custom-call | flops 1 | bytes 1 | tf_op jit(solution)/shard_map/gather/pallas_call | solution.py:89
  2.1 0.1 collective-permute-start
  2.2 4.5 %collective-permute-start.1 = (f32[2,4,64,256]{3,2,1,0:T(8,128)S(1)}, f32[2,4,64,256]{3,2,1,0:T(8,128)S(1)}, u32[]{:S(2)}, u32[]{:S(2)}) collective-permute-start(f32[2,4,64,256]{3,2,1,0:T(8,128)S(1)} %get-tuple-element.21.out.prev_out), channel_id=1, source_target_pairs={{1,2},{3,4},{5,6},{7,8},{9,10},{11,12},{13,14},{2,1},{4,3},{6,5},{... | collective-permute-start | bytes 1572872 | tf_op jit(solution)/shard_map/ppermute | solution.py:435
  6.7 0.0 collective-permute-done.near
  6.7 0.0 copy-start
  6.7 0.9 %copy-done = bf16[2,256,256]{2,1,0:T(8,128)(2,1)S(1)} copy-done((bf16[2,256,256]{2,1,0:T(8,128)(2,1)S(1)}, bf16[2,256,256]{2,1,0:T(8,128)(2,1)}, u32[]{:S(2)}) %copy-start) | copy-done | bytes 262168
  7.7 0.0 copy-start.2
  7.7 0.9 %copy-done.2 = bf16[256,256]{1,0:T(8,128)(2,1)S(1)} copy-done((bf16[256,256]{1,0:T(8,128)(2,1)S(1)}, bf16[256,256]{1,0:T(8,128)(2,1)}, u32[]{:S(2)}) %copy-start.2) | copy-done | bytes 131096
  8.6 4.1 %first_under.1 = (f32[2,4,64,256]{3,2,1,0:T(8,128)S(1)}, f32[2,4,64,256]{3,2,1,0:T(8,128)S(1)}, f32[3,4,64,256]{3,2,1,0:T(8,128)S(1)}, f32[3,4,64,256]{3,2,1,0:T(8,128)S(1)}) custom-call(f32[2,4,64,256]{3,2,1,0:T(8,128)S(1)} %get-tuple-element.20.inn.prev_inn, f32[2,4,64,256]{3,2,1,0:T(8,128)S(1)} %get-tuple-element.21.out.prev_out, ...), custom_call_target="tpu_custom_call" | custom-call | flops 1 | bytes 1 | tf_op jit(solution)/shard_map/first_under/pallas_call | solution.py:206
  12.7 0.1 collective-permute-start.2
  12.7 5.7 %collective-permute-done.1.halo = f32[2,4,64,256]{3,2,1,0:T(8,128)S(1)} collective-permute-done((f32[2,4,64,256]{3,2,1,0:T(8,128)S(1)}, f32[2,4,64,256]{3,2,1,0:T(8,128)S(1)}, u32[]{:S(2)}, u32[]{:S(2)}) %collective-permute-start.1) | collective-permute-done | bytes 524320 | tf_op jit(solution)/shard_map/ppermute | solution.py:435
  18.4 0.0 copy-start.3
  18.4 0.5 finish.4.out.prev_out
  18.9 4.4 %collective-permute-start.3 = (f32[2,4,64,256]{3,2,1,0:T(8,128)S(1)}, f32[2,4,64,256]{3,2,1,0:T(8,128)S(1)}, u32[]{:S(2)}, u32[]{:S(2)}) collective-permute-start(f32[2,4,64,256]{3,2,1,0:T(8,128)S(1)} %finish.4.out.prev_out), channel_id=1, source_target_pairs={{1,2},{3,4},{5,6},{7,8},{9,10},{11,12},{13,14},{2,1},{4,3},{6,5},{... | collective-permute-start | bytes 1572872 | tf_op jit(solution)/shard_map/ppermute | solution.py:435
  23.3 0.0 collective-permute-done.2.near
  23.3 0.0 copy-done.1
  23.3 2.4 %under.3 = (f32[2,4,64,256]{3,2,1,0:T(8,128)S(1)}, f32[2,4,64,256]{3,2,1,0:T(8,128)S(1)}) custom-call(f32[2,4,64,256]{3,2,1,0:T(8,128)S(1)} %get-tuple-element.22.inn.prev_inn, f32[2,4,64,256]{3,2,1,0:T(8,128)S(1)} %finish.4.out.prev_out, f32[2,4,64,256]{3,2,1,0:T(8,128)S(1)} %collective-permute-done.2.near, ...), custom_call_target="tpu_custom_call" | custom-call | flops 1 | bytes 1 | tf_op jit(solution)/shard_map/under/pallas_call | solution.py:220
  25.7 0.1 collective-permute-start.4
  25.8 6.2 %collective-permute-done.3.halo = f32[2,4,64,256]{3,2,1,0:T(8,128)S(1)} collective-permute-done((f32[2,4,64,256]{3,2,1,0:T(8,128)S(1)}, f32[2,4,64,256]{3,2,1,0:T(8,128)S(1)}, u32[]{:S(2)}, u32[]{:S(2)}) %collective-permute-start.3) | collective-permute-done | bytes 524320 | tf_op jit(solution)/shard_map/ppermute | solution.py:435
  32.0 0.0 copy-start.5
  32.0 0.0 slice-start
  32.0 0.0 copy-start.4
  32.0 0.5 finish.5.out.half.prev_out.out2
  32.4 0.0 slice-start.1
  32.5 4.7 %collective-permute-start.5 = (f32[2,4,64,256]{3,2,1,0:T(8,128)S(1)}, f32[2,4,64,256]{3,2,1,0:T(8,128)S(1)}, u32[]{:S(2)}, u32[]{:S(2)}) collective-permute-start(f32[2,4,64,256]{3,2,1,0:T(8,128)S(1)} %finish.5.out.half.prev_out.out2), channel_id=1, source_target_pairs={{1,2},{3,4},{5,6},{7,8},{9,10},{11,12},{13,14},{2,1},{4,3},{6,5},{... | collective-permute-start | bytes 1572872 | tf_op jit(solution)/shard_map/ppermute | solution.py:435
  37.1 0.0 collective-permute-done.4.near.hal2
  37.1 0.0 copy-done.3
  37.1 2.4 %under.4 = (f32[2,4,64,256]{3,2,1,0:T(8,128)S(1)}, f32[2,4,64,256]{3,2,1,0:T(8,128)S(1)}) custom-call(f32[2,4,64,256]{3,2,1,0:T(8,128)S(1)} %get-tuple-element.26.inn.other.prev_inn.in2, f32[2,4,64,256]{3,2,1,0:T(8,128)S(1)} %finish.5.out.half.prev_out.out2, f32[2,4,64,256]{3,2,1,0:T(8,128)S(1)} %collective-permute-done.4.near.hal2, ...), custom_call_target="tpu_custom_call" | custom-call | flops 1 | bytes 1 | tf_op jit(solution)/shard_map/under/pallas_call | solution.py:220
  39.6 0.1 collective-permute-start.6
  39.7 4.6 %collective-permute-done.5.halo = f32[2,4,64,256]{3,2,1,0:T(8,128)S(1)} collective-permute-done((f32[2,4,64,256]{3,2,1,0:T(8,128)S(1)}, f32[2,4,64,256]{3,2,1,0:T(8,128)S(1)}, u32[]{:S(2)}, u32[]{:S(2)}) %collective-permute-start.5) | collective-permute-done | bytes 524320 | tf_op jit(solution)/shard_map/ppermute | solution.py:435
  44.2 0.4 finish.6.out
  44.7 4.4 %collective-permute-start.7 = (f32[2,4,64,256]{3,2,1,0:T(8,128)S(1)}, f32[2,4,64,256]{3,2,1,0:T(8,128)S(1)}, u32[]{:S(2)}, u32[]{:S(2)}) collective-permute-start(f32[2,4,64,256]{3,2,1,0:T(8,128)S(1)} %finish.6.out), channel_id=1, source_target_pairs={{1,2},{3,4},{5,6},{7,8},{9,10},{11,12},{13,14},{2,1},{4,3},{6,5},{... | collective-permute-start | bytes 1572872 | tf_op jit(solution)/shard_map/ppermute | solution.py:435
  49.1 0.0 copy-done.5
  49.1 0.1 fusion.mute
  49.2 0.0 slice-done
  49.2 0.0 copy-done.4
  49.3 0.0 slice-done.1
  49.3 1.7 %image_mid.1.part = f32[9,4,64,256]{3,2,1,0:T(8,128)S(1)} custom-call(f32[9,8,64,256]{3,2,1,0:T(8,128)S(1)} %bitcast.16, s32[9]{0:T(128)S(1)} %copy-done.4, f32[8,64,256]{2,1,0:T(8,128)S(1)} %fusion.mute, f32[2,4,64,256]{3,2,1,0:T(8,128)S(1)} %finish.5.out.half.prev_out.out2, f32[2,4,64,256]{3,2,1,0:T(8,128)S(1)} %get-tuple-element.26.inn.other.prev_inn.in2, ...), custom_call_target="tpu_custom_call" | custom-call | flops 1 | bytes 1 | tf_op jit(solution)/shard_map/image_mid/pallas_call | solution.py:323
  50.9 0.0 collective-permute-done.6.near
  50.9 2.4 %under.5 = (f32[2,4,64,256]{3,2,1,0:T(8,128)S(1)}, f32[2,4,64,256]{3,2,1,0:T(8,128)S(1)}) custom-call(f32[2,4,64,256]{3,2,1,0:T(8,128)S(1)} %get-tuple-element.30.inn, f32[2,4,64,256]{3,2,1,0:T(8,128)S(1)} %finish.6.out, f32[2,4,64,256]{3,2,1,0:T(8,128)S(1)} %collective-permute-done.6.near, f32[2,4,64,256]{3,2,1,0:T(8,128)S(1)} %get-tuple-element.26.inn.other.prev_inn.in2, ...), custom_call_target="tpu_custom_call" | custom-call | flops 1 | bytes 1 | tf_op jit(solution)/shard_map/under/pallas_call | solution.py:220
  53.4 0.1 collective-permute-start.8
  53.4 2.8 %collective-permute-done.7.halo = f32[2,4,64,256]{3,2,1,0:T(8,128)S(1)} collective-permute-done((f32[2,4,64,256]{3,2,1,0:T(8,128)S(1)}, f32[2,4,64,256]{3,2,1,0:T(8,128)S(1)}, u32[]{:S(2)}, u32[]{:S(2)}) %collective-permute-start.7) | collective-permute-done | bytes 524320 | tf_op jit(solution)/shard_map/ppermute | solution.py:435
  56.2 0.4 finish.7.out4.half
  56.6 4.4 %collective-permute-start.9 = (f32[2,4,64,256]{3,2,1,0:T(8,128)S(1)}, f32[2,4,64,256]{3,2,1,0:T(8,128)S(1)}, u32[]{:S(2)}, u32[]{:S(2)}) collective-permute-start(f32[2,4,64,256]{3,2,1,0:T(8,128)S(1)} %finish.7.out4.half), channel_id=1, source_target_pairs={{1,2},{3,4},{5,6},{7,8},{9,10},{11,12},{13,14},{2,1},{4,3},{6,5},{... | collective-permute-start | bytes 1572872 | tf_op jit(solution)/shard_map/ppermute | solution.py:435
  61.0 0.0 collective-permute-done.8.hal4
  61.0 3.2 %image_main.1 = (f32[9,8,64,256]{3,2,1,0:T(8,128)}, f32[8,64,256]{2,1,0:T(8,128)}, f32[8,64,256]{2,1,0:T(8,128)}) custom-call(f32[9,8,64,256]{3,2,1,0:T(8,128)S(1)} %bitcast.17, f32[9,4,64,256]{3,2,1,0:T(8,128)S(1)} %image_mid.1.part, s32[9]{0:T(128)S(1)} %copy-done.4, f32[8,64,256]{2,1,0:T(8,128)S(1)} %fusion.mute, ...), custom_call_target="tpu_custom_call" | custom-call | flops 1 | bytes 1 | tf_op jit(solution)/shard_map/image_main/pallas_call | solution.py:382
  64.3 4.9 %collective-permute-done.9.halo = f32[2,4,64,256]{3,2,1,0:T(8,128)S(1)} collective-permute-done((f32[2,4,64,256]{3,2,1,0:T(8,128)S(1)}, f32[2,4,64,256]{3,2,1,0:T(8,128)S(1)}, u32[]{:S(2)}, u32[]{:S(2)}) %collective-permute-start.9) | collective-permute-done | bytes 524320 | tf_op jit(solution)/shard_map/ppermute | solution.py:435
  69.2 1.7 %image_last.1 = f32[9,8,64,256]{3,2,1,0:T(8,128)} custom-call(f32[9,8,64,256]{3,2,1,0:T(8,128)} %get-tuple-element.34.image_old, f32[9,4,64,256]{3,2,1,0:T(8,128)S(1)} %image_mid.1.part, s32[9]{0:T(128)S(1)} %copy-done.4, f32[8,64,256]{2,1,0:T(8,128)S(1)} %fusion.mute, f32[2,4,64,256]{3,2,1,0:T(8,128)S(1)} %finish.7.out4.half, ...), custom_call_target="tpu_custom_call", output_to_operand_aliasing={{}: (0, {})} | custom-call | flops 1 | bytes 1 | tf_op jit(solution)/shard_map/image_last/pallas_call | solution.py:415
  (1 shorter events, 0.0 us)
Async XLA Ops:
  0.6 22.7 %copy-start.1 = (bf16[2,256,256]{2,1,0:T(8,128)(2,1)S(1)}, bf16[2,256,256]{2,1,0:T(8,128)(2,1)}, u32[]{:S(2)}) copy-start(bf16[2,256,256]{2,1,0:T(8,128)(2,1)} %constant.4.clone.wz) | copy-start | bytes 786436
  2.1 4.6 %collective-permute-start = (f32[2,4,64,256]{3,2,1,0:T(8,128)S(1)}, f32[2,4,64,256]{3,2,1,0:T(8,128)S(1)}, u32[]{:S(2)}, u32[]{:S(2)}) collective-permute-start(f32[2,4,64,256]{3,2,1,0:T(8,128)S(1)} %get-tuple-element.20.inn.prev_inn), channel_id=1, source_target_pairs={{0,1},{1,0},{2,3},{3,2},{4,5},{5,4},{6,7},{7,6},{8,9},{9,8},{10,11... | collective-permute-start | bytes 1572872 | tf_op jit(solution)/shard_map/ppermute | solution.py:439
  2.2 16.2 %collective-permute-start.1 = (f32[2,4,64,256]{3,2,1,0:T(8,128)S(1)}, f32[2,4,64,256]{3,2,1,0:T(8,128)S(1)}, u32[]{:S(2)}, u32[]{:S(2)}) collective-permute-start(f32[2,4,64,256]{3,2,1,0:T(8,128)S(1)} %get-tuple-element.21.out.prev_out), channel_id=1, source_target_pairs={{1,2},{3,4},{5,6},{7,8},{9,10},{11,12},{13,14},{2,1},{4,3},{6,5},{... | collective-permute-start | bytes 1572872 | tf_op jit(solution)/shard_map/ppermute | solution.py:435
  6.7 1.0 %copy-start = (bf16[2,256,256]{2,1,0:T(8,128)(2,1)S(1)}, bf16[2,256,256]{2,1,0:T(8,128)(2,1)}, u32[]{:S(2)}) copy-start(bf16[2,256,256]{2,1,0:T(8,128)(2,1)} %constant.4.clone.wz) | copy-start | bytes 786436
  7.7 0.9 %copy-start.2 = (bf16[256,256]{1,0:T(8,128)(2,1)S(1)}, bf16[256,256]{1,0:T(8,128)(2,1)}, u32[]{:S(2)}) copy-start(bf16[256,256]{1,0:T(8,128)(2,1)} %constant.5.clone.wy) | copy-start | bytes 393220
  12.7 10.7 %collective-permute-start.2 = (f32[2,4,64,256]{3,2,1,0:T(8,128)S(1)}, f32[2,4,64,256]{3,2,1,0:T(8,128)S(1)}, u32[]{:S(2)}, u32[]{:S(2)}) collective-permute-start(f32[2,4,64,256]{3,2,1,0:T(8,128)S(1)} %get-tuple-element.22.inn.prev_inn), channel_id=1, source_target_pairs={{0,1},{1,0},{2,3},{3,2},{4,5},{5,4},{6,7},{7,6},{8,9},{9,8},{10,11... | collective-permute-start | bytes 1572872 | tf_op jit(solution)/shard_map/ppermute | solution.py:439
  18.4 18.7 %copy-start.3 = (bf16[256,256]{1,0:T(8,128)(2,1)S(1)}, bf16[256,256]{1,0:T(8,128)(2,1)}, u32[]{:S(2)}) copy-start(bf16[256,256]{1,0:T(8,128)(2,1)} %constant.5.clone.wy) | copy-start | bytes 393220
  18.9 13.1 %collective-permute-start.3 = (f32[2,4,64,256]{3,2,1,0:T(8,128)S(1)}, f32[2,4,64,256]{3,2,1,0:T(8,128)S(1)}, u32[]{:S(2)}, u32[]{:S(2)}) collective-permute-start(f32[2,4,64,256]{3,2,1,0:T(8,128)S(1)} %finish.4.out.prev_out), channel_id=1, source_target_pairs={{1,2},{3,4},{5,6},{7,8},{9,10},{11,12},{13,14},{2,1},{4,3},{6,5},{... | collective-permute-start | bytes 1572872 | tf_op jit(solution)/shard_map/ppermute | solution.py:435
  25.7 11.4 %collective-permute-start.4 = (f32[2,4,64,256]{3,2,1,0:T(8,128)S(1)}, f32[2,4,64,256]{3,2,1,0:T(8,128)S(1)}, u32[]{:S(2)}, u32[]{:S(2)}) collective-permute-start(f32[2,4,64,256]{3,2,1,0:T(8,128)S(1)} %get-tuple-element.26.inn.other.prev_inn.in2), channel_id=1, source_target_pairs={{0,1},{1,0},{2,3},{3,2},{4,5},{5,4},{6,7},{7,6},{8,9},{9,8},{10,11... | collective-permute-start | bytes 1572872 | tf_op jit(solution)/shard_map/ppermute | solution.py:439
  32.0 17.1 %copy-start.5 = (s32[1,8,64]{2,1,0:T(8,128)S(1)}, s32[1,8,64]{2,1,0:T(8,128)}, u32[]{:S(2)}) copy-start(s32[1,8,64]{2,1,0:T(8,128)} %param.19) | copy-start | bytes 6148
  32.0 17.3 %slice-start = ((s8[4718592]{0:T(1024)(128)(4,1)}), s8[4194304]{0:T(1024)(128)(4,1)S(1)}, s32[]{:S(2)}) async-start(s8[4718592]{0:T(1024)(128)(4,1)} %bitcast.14), calls=%async_computation | async-start | bytes 8388608
  32.0 17.3 %copy-start.4 = (s32[9]{0:T(128)S(1)}, s32[9]{0:T(128)}, u32[]{:S(2)}) copy-start(s32[9]{0:T(128)} %offsets.5) | copy-start | bytes 112
  32.4 16.8 %slice-start.1 = ((s8[4718592]{0:T(1024)(128)(4,1)}), s8[524288]{0:T(1024)(128)(4,1)S(1)}, s32[]{:S(2)}) async-start(s8[4718592]{0:T(1024)(128)(4,1)} %bitcast.14), calls=%async_computation.1 | async-start | bytes 1048576
  32.5 11.8 %collective-permute-start.5 = (f32[2,4,64,256]{3,2,1,0:T(8,128)S(1)}, f32[2,4,64,256]{3,2,1,0:T(8,128)S(1)}, u32[]{:S(2)}, u32[]{:S(2)}) collective-permute-start(f32[2,4,64,256]{3,2,1,0:T(8,128)S(1)} %finish.5.out.half.prev_out.out2), channel_id=1, source_target_pairs={{1,2},{3,4},{5,6},{7,8},{9,10},{11,12},{13,14},{2,1},{4,3},{6,5},{... | collective-permute-start | bytes 1572872 | tf_op jit(solution)/shard_map/ppermute | solution.py:435
  39.6 11.4 %collective-permute-start.6 = (f32[2,4,64,256]{3,2,1,0:T(8,128)S(1)}, f32[2,4,64,256]{3,2,1,0:T(8,128)S(1)}, u32[]{:S(2)}, u32[]{:S(2)}) collective-permute-start(f32[2,4,64,256]{3,2,1,0:T(8,128)S(1)} %get-tuple-element.30.inn), channel_id=1, source_target_pairs={{0,1},{1,0},{2,3},{3,2},{4,5},{5,4},{6,7},{7,6},{8,9},{9,8},{10,11... | collective-permute-start | bytes 1572872 | tf_op jit(solution)/shard_map/ppermute | solution.py:439
  44.7 11.5 %collective-permute-start.7 = (f32[2,4,64,256]{3,2,1,0:T(8,128)S(1)}, f32[2,4,64,256]{3,2,1,0:T(8,128)S(1)}, u32[]{:S(2)}, u32[]{:S(2)}) collective-permute-start(f32[2,4,64,256]{3,2,1,0:T(8,128)S(1)} %finish.6.out), channel_id=1, source_target_pairs={{1,2},{3,4},{5,6},{7,8},{9,10},{11,12},{13,14},{2,1},{4,3},{6,5},{... | collective-permute-start | bytes 1572872 | tf_op jit(solution)/shard_map/ppermute | solution.py:435
  53.4 7.7 %collective-permute-start.8 = (f32[2,4,64,256]{3,2,1,0:T(8,128)S(1)}, f32[2,4,64,256]{3,2,1,0:T(8,128)S(1)}, u32[]{:S(2)}, u32[]{:S(2)}) collective-permute-start(f32[2,4,64,256]{3,2,1,0:T(8,128)S(1)} %get-tuple-element.32.in4.other), channel_id=1, source_target_pairs={{0,1},{1,0},{2,3},{3,2},{4,5},{5,4},{6,7},{7,6},{8,9},{9,8},{10,11... | collective-permute-start | bytes 1572872 | tf_op jit(solution)/shard_map/ppermute | solution.py:439
  56.6 12.6 %collective-permute-start.9 = (f32[2,4,64,256]{3,2,1,0:T(8,128)S(1)}, f32[2,4,64,256]{3,2,1,0:T(8,128)S(1)}, u32[]{:S(2)}, u32[]{:S(2)}) collective-permute-start(f32[2,4,64,256]{3,2,1,0:T(8,128)S(1)} %finish.7.out4.half), channel_id=1, source_target_pairs={{1,2},{3,4},{5,6},{7,8},{9,10},{11,12},{13,14},{2,1},{4,3},{6,5},{... | collective-permute-start | bytes 1572872 | tf_op jit(solution)/shard_map/ppermute | solution.py:435

commit v3 on v2

--- a/solution.py
+++ b/solution.py
@@ -112,10 +112,9 @@
     sign = (1 - 2 * is_flipped(inner)).astype(jnp.float32)
     wx = [sign * w for w in mixed_w]
 
-    def first(i, carry):
-        r = pl.multiple_of(i * CHUNK, CHUNK)
-        span = pl.ds(r, CHUNK)
-        for f in range(2):
+    for f in range(2):
+        for r in range(0, rows, CHUNK):
+            span = pl.ds(r, CHUNK)
             low = 0 if halo is None else -4
             line = {q: at(half, other, halo, f, q)[span] for q in range(low, 8)}
             for m in range(4):
@@ -132,13 +131,9 @@
                     t = wx[k - 1] * t
                     dx = t if dx is None else dx + t
                 horiz[f, m, span] = hx
-                at_row = pl.ds(pl.multiple_of((f * 4 + m) * rows + r, CHUNK), CHUNK)
+                at_row = pl.ds((f * 4 + m) * rows + r, CHUNK)
                 v_hi[at_row], v_lo[at_row] = split(center)
                 x_hi[at_row], x_lo[at_row] = split(dx)
-        return carry
-
-    lax.fori_loop(0, rows // CHUNK, first, 0)
-    for f in range(2):
         part = pl.ds(f * 4 * rows, 4 * rows)
         vh, vl, xh, xl = v_hi[part], v_lo[part], x_hi[part], x_lo[part]
         zz = dot(vh, wz[0]) + dot(vl, wz[0])
@@ -159,14 +154,15 @@
             )
 
 
-def under_kernel(
-    inn, out, near, prev_inn, prev_out, coef_inn, coef_out, wz, wy, new_inn, base, *scratch
-):
+def inner_kernel(inn, out, near, prev_inn, coef_inn, wz, wy, new_inn, *scratch):
     advance(True, inn, out, near, prev_inn, coef_inn, wz, wy, new_inn, *scratch)
+
+
+def base_kernel(out, inn, prev_out, coef_out, wz, wy, base, *scratch):
     advance(False, out, inn, None, prev_out, coef_out, wz, wy, base, *scratch)
 
 
-def first_under_kernel(
+def first_kernel(
     inn, out, near, wz, wy, source_prev, receiver_prev, coef_a, coef_b, coef_c,
     new_inn, base, coef_inn, coef_out, prev_inn, prev_out, sem, *scratch
 ):
@@ -197,36 +193,36 @@
     return [flat] * 4 + [pltpu.VMEM((2, 4, rows, depth), jnp.float32)]
 
 
-def first_under(inn, out, near, wz, wy, arrays):
+def first(inn, out, near, wz, wy, arrays):
     rows, depth = inn.shape[2:]
     arrays = [pltpu.with_memory_space_constraint(a, pltpu.HBM) for a in arrays]
     pair = jax.ShapeDtypeStruct((2, 4, rows, depth), jnp.float32)
     three = jax.ShapeDtypeStruct((3, 4, rows, depth), jnp.float32)
     half = pltpu.VMEM((2, 4, rows, depth), jnp.float32)
     return pl.pallas_call(
-        first_under_kernel,
+        first_kernel,
         out_shape=[pair, pair, three, three],
         in_specs=[VMEM] * 5 + [HBM] * 5,
         out_specs=[VMEM] * 4,
         scratch_shapes=[half, half, pltpu.SemaphoreType.DMA((40,))] + work_space(rows, depth),
         cost_estimate=CHEAP,
         compiler_params=pltpu.CompilerParams(vmem_limit_bytes=12 * MIB),
-        name="first_under",
+        name="first",
     )(inn, out, near, wz, wy, *arrays)
 
 
-def under(inn, out, near, prev_inn, prev_out, coef_inn, coef_out, wz, wy):
-    shape = jax.ShapeDtypeStruct(inn.shape, jnp.float32)
-    return pl.pallas_call(
-        under_kernel,
-        out_shape=[shape, shape],
-        in_specs=[VMEM] * 9,
-        out_specs=[VMEM] * 2,
-        scratch_shapes=work_space(*inn.shape[2:]),
+def half_step(kernel, name, *operands):
+    shape = operands[0].shape
+    return pl.pallas_call(
+        kernel,
+        out_shape=jax.ShapeDtypeStruct(shape, jnp.float32),
+        in_specs=[VMEM] * len(operands),
+        out_specs=VMEM,
+        scratch_shapes=work_space(*shape[2:]),
         cost_estimate=CHEAP,
         compiler_params=pltpu.CompilerParams(vmem_limit_bytes=12 * MIB),
-        name="under",
-    )(inn, out, near, prev_inn, prev_out, coef_inn, coef_out, wz, wy)
+        name=name,
+    )(*operands)
 
 
 def finish_kernel(halo, base, coef, wz, out, hi, lo):
@@ -463,14 +459,13 @@
     out, inn = gather([source_cur, receiver_cur], [(0, False, (0, 1)), (1, True, (0, 1))])
     far = across_chips(out)
     near = within_chip(inn)
-    new_inn, base, coef_inn, coef_out = first_under(
+    new_inn, base, coef_inn, coef_out = first(
         inn, out, near, wz, wy, [source_prev, receiver_prev] + coefs
     )
     for n in range(STEPS):
-        if n == STEPS // 2 + 1:
-            inn, part = lax.optimization_barrier((inn, part))
         if n > 0:
-            new_inn, base = under(inn, out, near, prev_inn, prev_out, coef_inn, coef_out, wz, wy)
+            base = half_step(base_kernel, "base", out, inn, prev_out, coef_out, wz, wy)
+            new_inn = half_step(inner_kernel, "inner", inn, out, near, prev_inn, coef_inn, wz, wy)
         new_out = finish(far, base, coef_out, wz)
         if n == STEPS // 2:
             snap2 = (inn, out, near)

time: 72 us -> 70.3 us (0.976)
  Pallas kernels: 21.2 us -> 19.3 us
  waiting for transfers between devices: 24.1 us -> 24.9 us
    pallas_call x4 -> x7, Pallas kernels: 11.3 us -> 9.41 us  [the longest x6 5.84 us: half_step(): pl.pallas_call(kernel, out_shape=jax.ShapeDtypeStruct(shape, jnp.float32)...]
    ppermute x5, waiting for transfers between devices: 24.1 us -> 24.9 us  [across_chips(): return lax.ppermute(value, 'blk', pairs + [(b, a) for a, b in pairs])]
  transfers between devices with their start and end apart: 10 -> 10, of which waited for: 5 -> 5; matrix products, arithmetic and copies ran while one was open for 0% -> 0% of each run, Pallas kernels for 25% -> 23%
where the time goes in v3:
time: 70.3 us; the launch traced here: 69.9 us
  waiting for transfers between devices  24.9 us (35%)
  starting transfers between devices  22.7 us (32%)
  Pallas kernels  19.3 us (27%)
  local copies, waits for them, and re-layouts  1.89 us (3%)
  between operations  0.94 us (1%)
    ppermute x5, waiting for transfers between devices, across_chips(): return lax.ppermute(value, 'blk', pairs + [(b, a) for a, b in pairs])  24.9 us
    ppermute x5, starting transfers between devices, across_chips(): return lax.ppermute(value, 'blk', pairs + [(b, a) for a, b in pairs])  22.3 us
    pallas_call x6, Pallas kernels, half_step(): pl.pallas_call(kernel, out_shape=jax.ShapeDtypeStruct(shape, jnp.float32)...  5.84 us
    pallas_call x1, Pallas kernels, first(): pl.pallas_call(first_kernel, out_shape=[pair, pair, three, three], in_spe...  3.57 us
    pallas_call x1, Pallas kernels, image_main(): pl.pallas_call(image_main_kernel, out_shape=[jax.ShapeDtypeStruct(image_i...  3.23 us
    unnamed x16, local copies, waits for them, and re-layouts  1.89 us
    pallas_call x4, Pallas kernels, finish(): pl.pallas_call(finish_kernel, out_shape=jax.ShapeDtypeStruct(halo.shape,...  1.86 us
    pallas_call x1, Pallas kernels, image_last(): pl.pallas_call(image_last_kernel, out_shape=jax.ShapeDtypeStruct(image.sh...  1.75 us
  transfers between devices with their start and end apart: 10, of which 5 were waited for; matrix products, arithmetic and copies ran while one was open for 0% of the time, Pallas kernels for 23%

profile of v3, /device:TPU:1, one launch (start us, length us, event | category | flops | bytes accessed | tf_op | source)
XLA Modules:
  0.0 69.9 jit_solution(13192859187923576018)
XLA Ops:
  0.6 1.4 %gather.1 = (f32[2,4,64,256]{3,2,1,0:T(8,128)S(1)}, f32[2,4,64,256]{3,2,1,0:T(8,128)S(1)}) custom-call(f32[8,64,256]{2,1,0:T(8,128)} %bitcast.24, f32[8,64,256]{2,1,0:T(8,128)} %bitcast.25), custom_call_target="tpu_custom_call" | custom-call | flops 1 | bytes 1 | tf_op jit(solution)/shard_map/gather/pallas_call | solution.py:89
  2.0 0.1 collective-permute-start.1
  2.1 4.5 %collective-permute-start = (f32[2,4,64,256]{3,2,1,0:T(8,128)S(1)}, f32[2,4,64,256]{3,2,1,0:T(8,128)S(1)}, u32[]{:S(2)}, u32[]{:S(2)}) collective-permute-start(f32[2,4,64,256]{3,2,1,0:T(8,128)S(1)} %get-tuple-element.12.out.prev_out), channel_id=1, source_target_pairs={{1,2},{3,4},{5,6},{7,8},{9,10},{11,12},{13,14},{2,1},{4,3},{6,5},{... | collective-permute-start | bytes 1572872 | tf_op jit(solution)/shard_map/ppermute | solution.py:431
  6.6 0.0 collective-permute-done.1.near
  6.7 0.0 copy-start
  6.7 0.9 %copy-done = bf16[2,256,256]{2,1,0:T(8,128)(2,1)S(1)} copy-done((bf16[2,256,256]{2,1,0:T(8,128)(2,1)S(1)}, bf16[2,256,256]{2,1,0:T(8,128)(2,1)}, u32[]{:S(2)}) %copy-start) | copy-done | bytes 262168
  7.6 0.0 copy-start.2
  7.6 0.9 %copy-done.2 = bf16[256,256]{1,0:T(8,128)(2,1)S(1)} copy-done((bf16[256,256]{1,0:T(8,128)(2,1)S(1)}, bf16[256,256]{1,0:T(8,128)(2,1)}, u32[]{:S(2)}) %copy-start.2) | copy-done | bytes 131096
  8.5 0.0 copy-start.1
  8.5 3.6 %first.1 = (f32[2,4,64,256]{3,2,1,0:T(8,128)S(1)}, f32[2,4,64,256]{3,2,1,0:T(8,128)S(1)}, f32[3,4,64,256]{3,2,1,0:T(8,128)S(1)}, f32[3,4,64,256]{3,2,1,0:T(8,128)S(1)}) custom-call(f32[2,4,64,256]{3,2,1,0:T(8,128)S(1)} %get-tuple-element.13.inn.prev_inn, f32[2,4,64,256]{3,2,1,0:T(8,128)S(1)} %get-tuple-element.12.out.prev_out, ...), custom_call_target="tpu_custom_call" | custom-call | flops 1 | bytes 1 | tf_op jit(solution)/shard_map/first/pallas_call | solution.py:202
  12.1 0.1 collective-permute-start.3
  12.2 6.2 %collective-permute-done.halo = f32[2,4,64,256]{3,2,1,0:T(8,128)S(1)} collective-permute-done((f32[2,4,64,256]{3,2,1,0:T(8,128)S(1)}, f32[2,4,64,256]{3,2,1,0:T(8,128)S(1)}, u32[]{:S(2)}, u32[]{:S(2)}) %collective-permute-start) | collective-permute-done | bytes 524320 | tf_op jit(solution)/shard_map/ppermute | solution.py:431
  18.4 0.4 finish.4.out.prev_out
  18.8 4.4 %collective-permute-start.2 = (f32[2,4,64,256]{3,2,1,0:T(8,128)S(1)}, f32[2,4,64,256]{3,2,1,0:T(8,128)S(1)}, u32[]{:S(2)}, u32[]{:S(2)}) collective-permute-start(f32[2,4,64,256]{3,2,1,0:T(8,128)S(1)} %finish.4.out.prev_out), channel_id=1, source_target_pairs={{1,2},{3,4},{5,6},{7,8},{9,10},{11,12},{13,14},{2,1},{4,3},{6,5},{... | collective-permute-start | bytes 1572872 | tf_op jit(solution)/shard_map/ppermute | solution.py:431
  23.2 0.8 %base.3 = f32[2,4,64,256]{3,2,1,0:T(8,128)S(1)} custom-call(f32[2,4,64,256]{3,2,1,0:T(8,128)S(1)} %finish.4.out.prev_out, f32[2,4,64,256]{3,2,1,0:T(8,128)S(1)} %get-tuple-element.16.inn.prev_inn, f32[2,4,64,256]{3,2,1,0:T(8,128)S(1)} %get-tuple-element.12.out.prev_out, f32[3,4,64,256]{3,2,1,0:T(8,128)S(1)} %get-tuple-element.15.coef.coef_out, ...), custom_call_target="tpu_custom_call" | custom-call | flops 1 | bytes 1 | tf_op jit(solution)/shard_map/base/pallas_call | solution.py:216
  24.1 0.0 collective-permute-done.3.near
  24.1 0.0 copy-done.1
  24.1 1.0 %inner.3.other.inn.prev_inn.in2 = f32[2,4,64,256]{3,2,1,0:T(8,128)S(1)} custom-call(f32[2,4,64,256]{3,2,1,0:T(8,128)S(1)} %get-tuple-element.16.inn.prev_inn, f32[2,4,64,256]{3,2,1,0:T(8,128)S(1)} %finish.4.out.prev_out, f32[2,4,64,256]{3,2,1,0:T(8,128)S(1)} %collective-permute-done.3.near, f32[2,4,64,256]{3,2,1,0:T(8,128)S(1)} %get-tuple-element.13.inn.prev_inn, ...), custom_call_target="tpu_custom_call" | custom-call | flops 1 | bytes 1 | tf_op jit(solution)/shard_map/inner/pallas_call | solution.py:216
  25.1 0.1 collective-permute-start.5
  25.2 6.7 %collective-permute-done.2.halo = f32[2,4,64,256]{3,2,1,0:T(8,128)S(1)} collective-permute-done((f32[2,4,64,256]{3,2,1,0:T(8,128)S(1)}, f32[2,4,64,256]{3,2,1,0:T(8,128)S(1)}, u32[]{:S(2)}, u32[]{:S(2)}) %collective-permute-start.2) | collective-permute-done | bytes 524320 | tf_op jit(solution)/shard_map/ppermute | solution.py:431
  31.9 0.4 finish.5.half.out.prev_out.out2
  32.3 0.0 copy-start.3
  32.4 4.5 %collective-permute-start.4 = (f32[2,4,64,256]{3,2,1,0:T(8,128)S(1)}, f32[2,4,64,256]{3,2,1,0:T(8,128)S(1)}, u32[]{:S(2)}, u32[]{:S(2)}) collective-permute-start(f32[2,4,64,256]{3,2,1,0:T(8,128)S(1)} %finish.5.half.out.prev_out.out2), channel_id=1, source_target_pairs={{1,2},{3,4},{5,6},{7,8},{9,10},{11,12},{13,14},{2,1},{4,3},{6,5},{... | collective-permute-start | bytes 1572872 | tf_op jit(solution)/shard_map/ppermute | solution.py:431
  36.9 1.0 %base.4 = f32[2,4,64,256]{3,2,1,0:T(8,128)S(1)} custom-call(f32[2,4,64,256]{3,2,1,0:T(8,128)S(1)} %finish.5.half.out.prev_out.out2, f32[2,4,64,256]{3,2,1,0:T(8,128)S(1)} %inner.3.other.inn.prev_inn.in2, f32[2,4,64,256]{3,2,1,0:T(8,128)S(1)} %finish.4.out.prev_out, f32[3,4,64,256]{3,2,1,0:T(8,128)S(1)} %get-tuple-element.15.coef.coef_out, ...), custom_call_target="tpu_custom_call" | custom-call | flops 1 | bytes 1 | tf_op jit(solution)/shard_map/base/pallas_call | solution.py:216
  37.9 0.0 collective-permute-done.5.near.hal2
  37.9 0.0 slice-start
  37.9 1.1 %inner.4.inn = f32[2,4,64,256]{3,2,1,0:T(8,128)S(1)} custom-call(f32[2,4,64,256]{3,2,1,0:T(8,128)S(1)} %inner.3.other.inn.prev_inn.in2, f32[2,4,64,256]{3,2,1,0:T(8,128)S(1)} %finish.5.half.out.prev_out.out2, f32[2,4,64,256]{3,2,1,0:T(8,128)S(1)} %collective-permute-done.5.near.hal2, f32[2,4,64,256]{3,2,1,0:T(8,128)S(1)} %get-tuple-element.16.inn.prev_inn, ...), custom_call_target="tpu_custom_call" | custom-call | flops 1 | bytes 1 | tf_op jit(solution)/shard_map/inner/pallas_call | solution.py:216
  39.0 0.1 collective-permute-start.6
  39.1 4.9 %collective-permute-done.4.halo = f32[2,4,64,256]{3,2,1,0:T(8,128)S(1)} collective-permute-done((f32[2,4,64,256]{3,2,1,0:T(8,128)S(1)}, f32[2,4,64,256]{3,2,1,0:T(8,128)S(1)}, u32[]{:S(2)}, u32[]{:S(2)}) %collective-permute-start.4) | collective-permute-done | bytes 524320 | tf_op jit(solution)/shard_map/ppermute | solution.py:431
  44.0 0.5 finish.6.out
  44.5 0.0 copy-start.5
  44.5 0.0 slice-start.1
  44.5 0.0 copy-start.4
  44.5 4.5 %collective-permute-start.7 = (f32[2,4,64,256]{3,2,1,0:T(8,128)S(1)}, f32[2,4,64,256]{3,2,1,0:T(8,128)S(1)}, u32[]{:S(2)}, u32[]{:S(2)}) collective-permute-start(f32[2,4,64,256]{3,2,1,0:T(8,128)S(1)} %finish.6.out), channel_id=1, source_target_pairs={{1,2},{3,4},{5,6},{7,8},{9,10},{11,12},{13,14},{2,1},{4,3},{6,5},{... | collective-permute-start | bytes 1572872 | tf_op jit(solution)/shard_map/ppermute | solution.py:431
  49.0 0.0 copy-done.3
  49.1 0.9 %base.5 = f32[2,4,64,256]{3,2,1,0:T(8,128)S(1)} custom-call(f32[2,4,64,256]{3,2,1,0:T(8,128)S(1)} %finish.6.out, f32[2,4,64,256]{3,2,1,0:T(8,128)S(1)} %inner.4.inn, f32[2,4,64,256]{3,2,1,0:T(8,128)S(1)} %finish.5.half.out.prev_out.out2, f32[3,4,64,256]{3,2,1,0:T(8,128)S(1)} %get-tuple-element.15.coef.coef_out, bf16[2,256,256]{2,1,0:T(8,128)(2,1)S(1)} %copy-done.1, ...), custom_call_target="tpu_custom_call" | custom-call | flops 1 | bytes 1 | tf_op jit(solution)/shard_map/base/pallas_call | solution.py:216
  49.9 0.0 collective-permute-done.6.near
  49.9 1.0 %inner.5.in4.other = f32[2,4,64,256]{3,2,1,0:T(8,128)S(1)} custom-call(f32[2,4,64,256]{3,2,1,0:T(8,128)S(1)} %inner.4.inn, f32[2,4,64,256]{3,2,1,0:T(8,128)S(1)} %finish.6.out, f32[2,4,64,256]{3,2,1,0:T(8,128)S(1)} %collective-permute-done.6.near, f32[2,4,64,256]{3,2,1,0:T(8,128)S(1)} %inner.3.other.inn.prev_inn.in2, ...), custom_call_target="tpu_custom_call" | custom-call | flops 1 | bytes 1 | tf_op jit(solution)/shard_map/inner/pallas_call | solution.py:216
  51.0 0.1 collective-permute-start.8
  51.0 5.1 %collective-permute-done.7.halo = f32[2,4,64,256]{3,2,1,0:T(8,128)S(1)} collective-permute-done((f32[2,4,64,256]{3,2,1,0:T(8,128)S(1)}, f32[2,4,64,256]{3,2,1,0:T(8,128)S(1)}, u32[]{:S(2)}, u32[]{:S(2)}) %collective-permute-start.7) | collective-permute-done | bytes 524320 | tf_op jit(solution)/shard_map/ppermute | solution.py:431
  56.2 0.5 finish.7.out4.half
  56.6 4.4 %collective-permute-start.9 = (f32[2,4,64,256]{3,2,1,0:T(8,128)S(1)}, f32[2,4,64,256]{3,2,1,0:T(8,128)S(1)}, u32[]{:S(2)}, u32[]{:S(2)}) collective-permute-start(f32[2,4,64,256]{3,2,1,0:T(8,128)S(1)} %finish.7.out4.half), channel_id=1, source_target_pairs={{1,2},{3,4},{5,6},{7,8},{9,10},{11,12},{13,14},{2,1},{4,3},{6,5},{... | collective-permute-start | bytes 1572872 | tf_op jit(solution)/shard_map/ppermute | solution.py:431
  61.0 0.0 copy-done.5
  61.1 0.1 fusion.mute
  61.2 0.0 slice-done
  61.2 0.0 slice-done.1
  61.2 0.0 copy-done.4
  61.2 1.7 %image_mid.1.part = f32[9,4,64,256]{3,2,1,0:T(8,128)S(1)} custom-call(f32[9,8,64,256]{3,2,1,0:T(8,128)S(1)} %bitcast.16, s32[9]{0:T(128)S(1)} %copy-done.4, f32[8,64,256]{2,1,0:T(8,128)S(1)} %fusion.mute, f32[2,4,64,256]{3,2,1,0:T(8,128)S(1)} %finish.5.half.out.prev_out.out2, f32[2,4,64,256]{3,2,1,0:T(8,128)S(1)} %inner.3.other.inn.prev_inn.in2, ...), custom_call_target="tpu_custom_call" | custom-call | flops 1 | bytes 1 | tf_op jit(solution)/shard_map/image_mid/pallas_call | solution.py:319
  62.9 0.0 collective-permute-done.8.hal4
  62.9 3.2 %image_main.1 = (f32[9,8,64,256]{3,2,1,0:T(8,128)}, f32[8,64,256]{2,1,0:T(8,128)}, f32[8,64,256]{2,1,0:T(8,128)}) custom-call(f32[9,8,64,256]{3,2,1,0:T(8,128)S(1)} %bitcast.17, f32[9,4,64,256]{3,2,1,0:T(8,128)S(1)} %image_mid.1.part, s32[9]{0:T(128)S(1)} %copy-done.4, f32[8,64,256]{2,1,0:T(8,128)S(1)} %fusion.mute, ...), custom_call_target="tpu_custom_call" | custom-call | flops 1 | bytes 1 | tf_op jit(solution)/shard_map/image_main/pallas_call | solution.py:378
  66.1 2.0 %collective-permute-done.9.halo = f32[2,4,64,256]{3,2,1,0:T(8,128)S(1)} collective-permute-done((f32[2,4,64,256]{3,2,1,0:T(8,128)S(1)}, f32[2,4,64,256]{3,2,1,0:T(8,128)S(1)}, u32[]{:S(2)}, u32[]{:S(2)}) %collective-permute-start.9) | collective-permute-done | bytes 524320 | tf_op jit(solution)/shard_map/ppermute | solution.py:431
  68.1 1.7 %image_last.1 = f32[9,8,64,256]{3,2,1,0:T(8,128)} custom-call(f32[9,8,64,256]{3,2,1,0:T(8,128)} %get-tuple-element.18.image_old, f32[9,4,64,256]{3,2,1,0:T(8,128)S(1)} %image_mid.1.part, s32[9]{0:T(128)S(1)} %copy-done.4, f32[8,64,256]{2,1,0:T(8,128)S(1)} %fusion.mute, f32[2,4,64,256]{3,2,1,0:T(8,128)S(1)} %finish.7.out4.half, ...), custom_call_target="tpu_custom_call", output_to_operand_aliasing={{}: (0, {})} | custom-call | flops 1 | bytes 1 | tf_op jit(solution)/shard_map/image_last/pallas_call | solution.py:411
  (1 shorter events, 0.0 us)
Async XLA Ops:
  2.0 4.6 %collective-permute-start.1 = (f32[2,4,64,256]{3,2,1,0:T(8,128)S(1)}, f32[2,4,64,256]{3,2,1,0:T(8,128)S(1)}, u32[]{:S(2)}, u32[]{:S(2)}) collective-permute-start(f32[2,4,64,256]{3,2,1,0:T(8,128)S(1)} %get-tuple-element.13.inn.prev_inn), channel_id=1, source_target_pairs={{0,1},{1,0},{2,3},{3,2},{4,5},{5,4},{6,7},{7,6},{8,9},{9,8},{10,11... | collective-permute-start | bytes 1572872 | tf_op jit(solution)/shard_map/ppermute | solution.py:435
  2.1 16.2 %collective-permute-start = (f32[2,4,64,256]{3,2,1,0:T(8,128)S(1)}, f32[2,4,64,256]{3,2,1,0:T(8,128)S(1)}, u32[]{:S(2)}, u32[]{:S(2)}) collective-permute-start(f32[2,4,64,256]{3,2,1,0:T(8,128)S(1)} %get-tuple-element.12.out.prev_out), channel_id=1, source_target_pairs={{1,2},{3,4},{5,6},{7,8},{9,10},{11,12},{13,14},{2,1},{4,3},{6,5},{... | collective-permute-start | bytes 1572872 | tf_op jit(solution)/shard_map/ppermute | solution.py:431
  6.7 1.0 %copy-start = (bf16[2,256,256]{2,1,0:T(8,128)(2,1)S(1)}, bf16[2,256,256]{2,1,0:T(8,128)(2,1)}, u32[]{:S(2)}) copy-start(bf16[2,256,256]{2,1,0:T(8,128)(2,1)} %constant.4.clone.wz) | copy-start | bytes 786436
  7.6 0.9 %copy-start.2 = (bf16[256,256]{1,0:T(8,128)(2,1)S(1)}, bf16[256,256]{1,0:T(8,128)(2,1)}, u32[]{:S(2)}) copy-start(bf16[256,256]{1,0:T(8,128)(2,1)} %constant.5.clone.wy) | copy-start | bytes 393220
  8.5 15.6 %copy-start.1 = (bf16[2,256,256]{2,1,0:T(8,128)(2,1)S(1)}, bf16[2,256,256]{2,1,0:T(8,128)(2,1)}, u32[]{:S(2)}) copy-start(bf16[2,256,256]{2,1,0:T(8,128)(2,1)} %constant.4.clone.wz) | copy-start | bytes 786436
  12.1 12.0 %collective-permute-start.3 = (f32[2,4,64,256]{3,2,1,0:T(8,128)S(1)}, f32[2,4,64,256]{3,2,1,0:T(8,128)S(1)}, u32[]{:S(2)}, u32[]{:S(2)}) collective-permute-start(f32[2,4,64,256]{3,2,1,0:T(8,128)S(1)} %get-tuple-element.16.inn.prev_inn), channel_id=1, source_target_pairs={{0,1},{1,0},{2,3},{3,2},{4,5},{5,4},{6,7},{7,6},{8,9},{9,8},{10,11... | collective-permute-start | bytes 1572872 | tf_op jit(solution)/shard_map/ppermute | solution.py:435
  18.8 13.1 %collective-permute-start.2 = (f32[2,4,64,256]{3,2,1,0:T(8,128)S(1)}, f32[2,4,64,256]{3,2,1,0:T(8,128)S(1)}, u32[]{:S(2)}, u32[]{:S(2)}) collective-permute-start(f32[2,4,64,256]{3,2,1,0:T(8,128)S(1)} %finish.4.out.prev_out), channel_id=1, source_target_pairs={{1,2},{3,4},{5,6},{7,8},{9,10},{11,12},{13,14},{2,1},{4,3},{6,5},{... | collective-permute-start | bytes 1572872 | tf_op jit(solution)/shard_map/ppermute | solution.py:431
  25.1 12.8 %collective-permute-start.5 = (f32[2,4,64,256]{3,2,1,0:T(8,128)S(1)}, f32[2,4,64,256]{3,2,1,0:T(8,128)S(1)}, u32[]{:S(2)}, u32[]{:S(2)}) collective-permute-start(f32[2,4,64,256]{3,2,1,0:T(8,128)S(1)} %inner.3.other.inn.prev_inn.in2), channel_id=1, source_target_pairs={{0,1},{1,0},{2,3},{3,2},{4,5},{5,4},{6,7},{7,6},{8,9},{9,8},{10,11... | collective-permute-start | bytes 1572872 | tf_op jit(solution)/shard_map/ppermute | solution.py:435
  32.3 16.7 %copy-start.3 = (bf16[256,256]{1,0:T(8,128)(2,1)S(1)}, bf16[256,256]{1,0:T(8,128)(2,1)}, u32[]{:S(2)}) copy-start(bf16[256,256]{1,0:T(8,128)(2,1)} %constant.5.clone.wy) | copy-start | bytes 393220
  32.4 11.6 %collective-permute-start.4 = (f32[2,4,64,256]{3,2,1,0:T(8,128)S(1)}, f32[2,4,64,256]{3,2,1,0:T(8,128)S(1)}, u32[]{:S(2)}, u32[]{:S(2)}) collective-permute-start(f32[2,4,64,256]{3,2,1,0:T(8,128)S(1)} %finish.5.half.out.prev_out.out2), channel_id=1, source_target_pairs={{1,2},{3,4},{5,6},{7,8},{9,10},{11,12},{13,14},{2,1},{4,3},{6,5},{... | collective-permute-start | bytes 1572872 | tf_op jit(solution)/shard_map/ppermute | solution.py:431
  37.9 23.3 %slice-start = ((s8[4718592]{0:T(1024)(128)(4,1)}), s8[4194304]{0:T(1024)(128)(4,1)S(1)}, s32[]{:S(2)}) async-start(s8[4718592]{0:T(1024)(128)(4,1)} %bitcast.14), calls=%async_computation | async-start | bytes 8388608
  39.0 10.9 %collective-permute-start.6 = (f32[2,4,64,256]{3,2,1,0:T(8,128)S(1)}, f32[2,4,64,256]{3,2,1,0:T(8,128)S(1)}, u32[]{:S(2)}, u32[]{:S(2)}) collective-permute-start(f32[2,4,64,256]{3,2,1,0:T(8,128)S(1)} %inner.4.inn), channel_id=1, source_target_pairs={{0,1},{1,0},{2,3},{3,2},{4,5},{5,4},{6,7},{7,6},{8,9},{9,8},{10,11... | collective-permute-start | bytes 1572872 | tf_op jit(solution)/shard_map/ppermute | solution.py:435
  44.5 16.6 %copy-start.5 = (s32[1,8,64]{2,1,0:T(8,128)S(1)}, s32[1,8,64]{2,1,0:T(8,128)}, u32[]{:S(2)}) copy-start(s32[1,8,64]{2,1,0:T(8,128)} %param.19) | copy-start | bytes 6148
  44.5 16.7 %slice-start.1 = ((s8[4718592]{0:T(1024)(128)(4,1)}), s8[524288]{0:T(1024)(128)(4,1)S(1)}, s32[]{:S(2)}) async-start(s8[4718592]{0:T(1024)(128)(4,1)} %bitcast.14), calls=%async_computation.1 | async-start | bytes 1048576
  44.5 16.7 %copy-start.4 = (s32[9]{0:T(128)S(1)}, s32[9]{0:T(128)}, u32[]{:S(2)}) copy-start(s32[9]{0:T(128)} %offsets.5) | copy-start | bytes 112
  44.5 11.6 %collective-permute-start.7 = (f32[2,4,64,256]{3,2,1,0:T(8,128)S(1)}, f32[2,4,64,256]{3,2,1,0:T(8,128)S(1)}, u32[]{:S(2)}, u32[]{:S(2)}) collective-permute-start(f32[2,4,64,256]{3,2,1,0:T(8,128)S(1)} %finish.6.out), channel_id=1, source_target_pairs={{1,2},{3,4},{5,6},{7,8},{9,10},{11,12},{13,14},{2,1},{4,3},{6,5},{... | collective-permute-start | bytes 1572872 | tf_op jit(solution)/shard_map/ppermute | solution.py:431
  51.0 11.9 %collective-permute-start.8 = (f32[2,4,64,256]{3,2,1,0:T(8,128)S(1)}, f32[2,4,64,256]{3,2,1,0:T(8,128)S(1)}, u32[]{:S(2)}, u32[]{:S(2)}) collective-permute-start(f32[2,4,64,256]{3,2,1,0:T(8,128)S(1)} %inner.5.in4.other), channel_id=1, source_target_pairs={{0,1},{1,0},{2,3},{3,2},{4,5},{5,4},{6,7},{7,6},{8,9},{9,8},{10,11... | collective-permute-start | bytes 1572872 | tf_op jit(solution)/shard_map/ppermute | solution.py:435
  56.6 11.5 %collective-permute-start.9 = (f32[2,4,64,256]{3,2,1,0:T(8,128)S(1)}, f32[2,4,64,256]{3,2,1,0:T(8,128)S(1)}, u32[]{:S(2)}, u32[]{:S(2)}) collective-permute-start(f32[2,4,64,256]{3,2,1,0:T(8,128)S(1)} %finish.7.out4.half), channel_id=1, source_target_pairs={{1,2},{3,4},{5,6},{7,8},{9,10},{11,12},{13,14},{2,1},{4,3},{6,5},{... | collective-permute-start | bytes 1572872 | tf_op jit(solution)/shard_map/ppermute | solution.py:431

commit v4 on v3

--- a/solution.py
+++ b/solution.py
@@ -21,6 +21,7 @@
 ANY = pl.BlockSpec(memory_space=pl.ANY)
 HBM = pl.BlockSpec(memory_space=pltpu.HBM)
 MIB = 1 << 20
+BIG = pl.CostEstimate(flops=10000000000, transcendentals=0, bytes_accessed=20000000)
 CHEAP = pl.CostEstimate(flops=1, transcendentals=0, bytes_accessed=1)
 
 
@@ -39,10 +40,14 @@
 
 def at(half, other, halo, field, position):
     if position < 0:
-        return halo.at[field, -1 - position]
+        return pick(halo, field, -1 - position)
     if position < 4:
-        return half.at[field, position]
-    return other.at[field, 7 - position]
+        return pick(half, field, position)
+    return pick(other, field, 7 - position)
+
+
+def pick(fields, field, plane):
+    return fields[field].at[plane] if isinstance(fields, tuple) else fields.at[field, plane]
 
 
 SCALE = 5040
@@ -92,7 +97,7 @@
         in_specs=[HBM] * len(arrays),
         out_specs=[VMEM] * len(plan),
         scratch_shapes=[pltpu.SemaphoreType.DMA((sum(4 * len(s) for _, _, s in plan),))],
-        cost_estimate=CHEAP,
+        cost_estimate=BIG,
         compiler_params=pltpu.CompilerParams(vmem_limit_bytes=8 * MIB),
         name="gather",
     )(*arrays)
@@ -163,29 +168,32 @@
 
 
 def first_kernel(
-    inn, out, near, wz, wy, source_prev, receiver_prev, coef_a, coef_b, coef_c,
-    new_inn, base, coef_inn, coef_out, prev_inn, prev_out, sem, *scratch
+    out, inn, wz, wy, source_prev, receiver_prev, coef_a, coef_b, coef_c,
+    base, coef_inn, coef_out, prev_inn, prev_out, sem, *scratch
 ):
+    coefs = (coef_a, coef_b, coef_c)
     prevs = (source_prev, receiver_prev)
-    coefs = (coef_a, coef_b, coef_c)
     copies = []
-    for inner, prev, coef in ((True, prev_inn, coef_inn), (False, prev_out, coef_out)):
-        for sources, target in ((coefs, coef), (prevs, prev)):
-            for i, source in enumerate(sources):
-                for m in range(4):
-                    copies.append(
-                        pltpu.make_async_copy(
-                            source.at[natural(m, is_flipped(inner))], target.at[i, m], sem.at[len(copies)]
-                        )
+    for inner, pairs in (
+        (False, [(c, coef_out.at[i]) for i, c in enumerate(coefs)]),
+        (False, [(c, prev_out.at[i]) for i, c in enumerate(prevs)]),
+        (True, [(c, coef_inn.at[i]) for i, c in enumerate(coefs)]),
+        (True, [(c, prev_inn.at[i]) for i, c in enumerate(prevs)]),
+    ):
+        for source, target in pairs:
+            for m in range(4):
+                copies.append(
+                    pltpu.make_async_copy(
+                        source.at[natural(m, is_flipped(inner))], target.at[m], sem.at[len(copies)]
                     )
+                )
     for c in copies:
         c.start()
     for c in copies[:20]:
         c.wait()
-    advance(True, inn, out, near, prev_inn, coef_inn, wz, wy, new_inn, *scratch)
+    advance(False, out, inn, None, prev_out, coef_out, wz, wy, base, *scratch)
     for c in copies[20:]:
         c.wait()
-    advance(False, out, inn, None, prev_out, coef_out, wz, wy, base, *scratch)
 
 
 def work_space(rows, depth):
@@ -193,22 +201,22 @@
     return [flat] * 4 + [pltpu.VMEM((2, 4, rows, depth), jnp.float32)]
 
 
-def first(inn, out, near, wz, wy, arrays):
-    rows, depth = inn.shape[2:]
+def first(out, inn, wz, wy, arrays):
+    rows, depth = out.shape[2:]
     arrays = [pltpu.with_memory_space_constraint(a, pltpu.HBM) for a in arrays]
     pair = jax.ShapeDtypeStruct((2, 4, rows, depth), jnp.float32)
     three = jax.ShapeDtypeStruct((3, 4, rows, depth), jnp.float32)
     half = pltpu.VMEM((2, 4, rows, depth), jnp.float32)
     return pl.pallas_call(
         first_kernel,
-        out_shape=[pair, pair, three, three],
-        in_specs=[VMEM] * 5 + [HBM] * 5,
+        out_shape=[pair, three, three, pair],
+        in_specs=[VMEM] * 4 + [HBM] * 5,
         out_specs=[VMEM] * 4,
-        scratch_shapes=[half, half, pltpu.SemaphoreType.DMA((40,))] + work_space(rows, depth),
-        cost_estimate=CHEAP,
+        scratch_shapes=[half, pltpu.SemaphoreType.DMA((40,))] + work_space(rows, depth),
+        cost_estimate=BIG,
         compiler_params=pltpu.CompilerParams(vmem_limit_bytes=12 * MIB),
         name="first",
-    )(inn, out, near, wz, wy, *arrays)
+    )(out, inn, wz, wy, *arrays)
 
 
 def half_step(kernel, name, *operands):
@@ -456,16 +464,17 @@
     depth_ids = lax.broadcasted_iota(jnp.int32, source_cur.shape, 2)
     mute = (depth_ids < live_depth[0][:, :, None]).astype(jnp.float32)
 
-    out, inn = gather([source_cur, receiver_cur], [(0, False, (0, 1)), (1, True, (0, 1))])
+    (out,) = gather([source_cur, receiver_cur], [(0, False, (0, 1))])
     far = across_chips(out)
+    (inn,) = gather([source_cur, receiver_cur], [(0, True, (0, 1))])
     near = within_chip(inn)
-    new_inn, base, coef_inn, coef_out = first(
-        inn, out, near, wz, wy, [source_prev, receiver_prev] + coefs
+    base, coef_inn, coef_out, prev_inn = first(
+        out, inn, wz, wy, [source_prev, receiver_prev] + coefs
     )
     for n in range(STEPS):
         if n > 0:
             base = half_step(base_kernel, "base", out, inn, prev_out, coef_out, wz, wy)
-            new_inn = half_step(inner_kernel, "inner", inn, out, near, prev_inn, coef_inn, wz, wy)
+        new_inn = half_step(inner_kernel, "inner", inn, out, near, prev_inn, coef_inn, wz, wy)
         new_out = finish(far, base, coef_out, wz)
         if n == STEPS // 2:
             snap2 = (inn, out, near)

time: 70.3 us -> 69.3 us (0.986)
  local copies, waits for them, and re-layouts: 1.89 us -> 0.04 us
  Pallas kernels: 19.3 us -> 20.1 us
    unnamed x16 -> x12, local copies, waits for them, and re-layouts: 1.89 us -> 0.04 us
    pallas_call x1, Pallas kernels: 3.57 us -> 2.57 us  [first(): pl.pallas_call(first_kernel, out_shape=[pair, three, three, pair], in_spe...]
    pallas_call x6 -> x7, Pallas kernels: 5.84 us -> 6.83 us  [half_step(): pl.pallas_call(kernel, out_shape=jax.ShapeDtypeStruct(shape, jnp.float32)...]
    pallas_call x1 -> x2, Pallas kernels: 1.39 us -> 2.28 us  [gather(): pl.pallas_call(functools.partial(gather_kernel, plan, len(arrays)), out_s...]
  transfers between devices with their start and end apart: 10 -> 10, of which waited for: 5 -> 5; matrix products, arithmetic and copies ran while one was open for 0% -> 0% of each run, Pallas kernels for 23% -> 25%
where the time goes in v4:
time: 69.3 us; the launch traced here: 68.9 us
  waiting for transfers between devices  24.5 us (35%)
  starting transfers between devices  23.2 us (33%)
  Pallas kernels  20.1 us (29%)
  between operations  0.95 us (1%)
    ppermute x5, waiting for transfers between devices, across_chips(): return lax.ppermute(value, 'blk', pairs + [(b, a) for a, b in pairs])  24.5 us
    ppermute x5, starting transfers between devices, across_chips(): return lax.ppermute(value, 'blk', pairs + [(b, a) for a, b in pairs])  22.4 us
    pallas_call x7, Pallas kernels, half_step(): pl.pallas_call(kernel, out_shape=jax.ShapeDtypeStruct(shape, jnp.float32)...  6.83 us
    pallas_call x1, Pallas kernels, image_main(): pl.pallas_call(image_main_kernel, out_shape=[jax.ShapeDtypeStruct(image_i...  3.23 us
    pallas_call x1, Pallas kernels, first(): pl.pallas_call(first_kernel, out_shape=[pair, three, three, pair], in_spe...  2.57 us
    pallas_call x2, Pallas kernels, gather(): pl.pallas_call(functools.partial(gather_kernel, plan, len(arrays)), out_s...  2.28 us
    pallas_call x4, Pallas kernels, finish(): pl.pallas_call(finish_kernel, out_shape=jax.ShapeDtypeStruct(halo.shape,...  1.82 us
    pallas_call x1, Pallas kernels, image_last(): pl.pallas_call(image_last_kernel, out_shape=jax.ShapeDtypeStruct(image.sh...  1.75 us
  transfers between devices with their start and end apart: 10, of which 5 were waited for; matrix products, arithmetic and copies ran while one was open for 0% of the time, Pallas kernels for 25%

profile of v4, /device:TPU:1, one launch (start us, length us, event | category | flops | bytes accessed | tf_op | source)
XLA Modules:
  0.0 68.9 jit_solution(927037549469522388)
XLA Ops:
  0.6 1.1 %gather.2.out.prev_out = f32[2,4,64,256]{3,2,1,0:T(8,128)S(1)} custom-call(f32[8,64,256]{2,1,0:T(8,128)} %bitcast.20, f32[8,64,256]{2,1,0:T(8,128)} %bitcast.22), custom_call_target="tpu_custom_call" | custom-call | flops 10000000000 | bytes 20000000 | tf_op jit(solution)/shard_map/gather/pallas_call | solution.py:94
  1.8 0.0 copy-start
  1.8 0.0 copy-start.1
  1.8 4.7 %collective-permute-start = (f32[2,4,64,256]{3,2,1,0:T(8,128)S(1)}, f32[2,4,64,256]{3,2,1,0:T(8,128)S(1)}, u32[]{:S(2)}, u32[]{:S(2)}) collective-permute-start(f32[2,4,64,256]{3,2,1,0:T(8,128)S(1)} %gather.2.out.prev_out), channel_id=1, source_target_pairs={{1,2},{3,4},{5,6},{7,8},{9,10},{11,12},{13,14},{2,1},{4,3},{6,5},{... | collective-permute-start | bytes 1572872 | tf_op jit(solution)/shard_map/ppermute | solution.py:439
  6.5 1.1 %gather.3.inn.prev_inn = f32[2,4,64,256]{3,2,1,0:T(8,128)S(1)} custom-call(f32[8,64,256]{2,1,0:T(8,128)} %bitcast.21, f32[8,64,256]{2,1,0:T(8,128)} %bitcast.23), custom_call_target="tpu_custom_call" | custom-call | flops 10000000000 | bytes 20000000 | tf_op jit(solution)/shard_map/gather/pallas_call | solution.py:94
  7.6 0.1 collective-permute-start.2
  7.7 0.0 copy-done
  7.7 0.0 copy-done.1
  7.7 2.6 %first.1 = (f32[2,4,64,256]{3,2,1,0:T(8,128)S(1)}, f32[3,4,64,256]{3,2,1,0:T(8,128)S(1)}, f32[3,4,64,256]{3,2,1,0:T(8,128)S(1)}, f32[2,4,64,256]{3,2,1,0:T(8,128)S(1)}) custom-call(f32[2,4,64,256]{3,2,1,0:T(8,128)S(1)} %gather.2.out.prev_out, f32[2,4,64,256]{3,2,1,0:T(8,128)S(1)} %gather.3.inn.prev_inn, bf16[2,256,256]{2,1,0:T(8,128)(2,1)S(1)} %copy-done, ...), custom_call_target="tpu_custom_call" | custom-call | flops 10000000000 | bytes 20000000 | tf_op jit(solution)/shard_map/first/pallas_call | solution.py:210
  10.3 0.0 collective-permute-done.2.near
  10.3 1.0 %inner.4.inn.prev_inn = f32[2,4,64,256]{3,2,1,0:T(8,128)S(1)} custom-call(f32[2,4,64,256]{3,2,1,0:T(8,128)S(1)} %gather.3.inn.prev_inn, f32[2,4,64,256]{3,2,1,0:T(8,128)S(1)} %gather.2.out.prev_out, f32[2,4,64,256]{3,2,1,0:T(8,128)S(1)} %collective-permute-done.2.near, f32[2,4,64,256]{3,2,1,0:T(8,128)S(1)} %get-tuple-element.12.prev_inn, ...), custom_call_target="tpu_custom_call" | custom-call | flops 1 | bytes 1 | tf_op jit(solution)/shard_map/inner/pallas_call | solution.py:224
  11.3 0.5 collective-permute-start.3
  11.8 6.4 %collective-permute-done.halo = f32[2,4,64,256]{3,2,1,0:T(8,128)S(1)} collective-permute-done((f32[2,4,64,256]{3,2,1,0:T(8,128)S(1)}, f32[2,4,64,256]{3,2,1,0:T(8,128)S(1)}, u32[]{:S(2)}, u32[]{:S(2)}) %collective-permute-start) | collective-permute-done | bytes 524320 | tf_op jit(solution)/shard_map/ppermute | solution.py:439
  18.2 0.4 finish.4.out.prev_out
  18.7 4.4 %collective-permute-start.1 = (f32[2,4,64,256]{3,2,1,0:T(8,128)S(1)}, f32[2,4,64,256]{3,2,1,0:T(8,128)S(1)}, u32[]{:S(2)}, u32[]{:S(2)}) collective-permute-start(f32[2,4,64,256]{3,2,1,0:T(8,128)S(1)} %finish.4.out.prev_out), channel_id=1, source_target_pairs={{1,2},{3,4},{5,6},{7,8},{9,10},{11,12},{13,14},{2,1},{4,3},{6,5},{... | collective-permute-start | bytes 1572872 | tf_op jit(solution)/shard_map/ppermute | solution.py:439
  23.1 0.8 %base.3 = f32[2,4,64,256]{3,2,1,0:T(8,128)S(1)} custom-call(f32[2,4,64,256]{3,2,1,0:T(8,128)S(1)} %finish.4.out.prev_out, f32[2,4,64,256]{3,2,1,0:T(8,128)S(1)} %inner.4.inn.prev_inn, f32[2,4,64,256]{3,2,1,0:T(8,128)S(1)} %gather.2.out.prev_out, f32[3,4,64,256]{3,2,1,0:T(8,128)S(1)} %get-tuple-element.11.coef.coef_out, bf16[2,256,256]{2,1,0:T(8,128)(2,1)S(1)} %copy-done, ...), custom_call_target="tpu_custom_call" | custom-call | flops 1 | bytes 1 | tf_op jit(solution)/shard_map/base/pallas_call | solution.py:224
  23.9 0.0 collective-permute-done.3.near
  23.9 1.0 %inner.5.other.inn.prev_inn.in2 = f32[2,4,64,256]{3,2,1,0:T(8,128)S(1)} custom-call(f32[2,4,64,256]{3,2,1,0:T(8,128)S(1)} %inner.4.inn.prev_inn, f32[2,4,64,256]{3,2,1,0:T(8,128)S(1)} %finish.4.out.prev_out, f32[2,4,64,256]{3,2,1,0:T(8,128)S(1)} %collective-permute-done.3.near, f32[2,4,64,256]{3,2,1,0:T(8,128)S(1)} %gather.3.inn.prev_inn, ...), custom_call_target="tpu_custom_call" | custom-call | flops 1 | bytes 1 | tf_op jit(solution)/shard_map/inner/pallas_call | solution.py:224
  24.9 0.1 collective-permute-start.5
  25.0 6.1 %collective-permute-done.1.halo = f32[2,4,64,256]{3,2,1,0:T(8,128)S(1)} collective-permute-done((f32[2,4,64,256]{3,2,1,0:T(8,128)S(1)}, f32[2,4,64,256]{3,2,1,0:T(8,128)S(1)}, u32[]{:S(2)}, u32[]{:S(2)}) %collective-permute-start.1) | collective-permute-done | bytes 524320 | tf_op jit(solution)/shard_map/ppermute | solution.py:439
  31.1 0.4 finish.5.half.out.prev_out.out2
  31.5 4.4 %collective-permute-start.4 = (f32[2,4,64,256]{3,2,1,0:T(8,128)S(1)}, f32[2,4,64,256]{3,2,1,0:T(8,128)S(1)}, u32[]{:S(2)}, u32[]{:S(2)}) collective-permute-start(f32[2,4,64,256]{3,2,1,0:T(8,128)S(1)} %finish.5.half.out.prev_out.out2), channel_id=1, source_target_pairs={{1,2},{3,4},{5,6},{7,8},{9,10},{11,12},{13,14},{2,1},{4,3},{6,5},{... | collective-permute-start | bytes 1572872 | tf_op jit(solution)/shard_map/ppermute | solution.py:439
  35.9 1.0 %base.4 = f32[2,4,64,256]{3,2,1,0:T(8,128)S(1)} custom-call(f32[2,4,64,256]{3,2,1,0:T(8,128)S(1)} %finish.5.half.out.prev_out.out2, f32[2,4,64,256]{3,2,1,0:T(8,128)S(1)} %inner.5.other.inn.prev_inn.in2, f32[2,4,64,256]{3,2,1,0:T(8,128)S(1)} %finish.4.out.prev_out, f32[3,4,64,256]{3,2,1,0:T(8,128)S(1)} %get-tuple-element.11.coef.coef_out, ...), custom_call_target="tpu_custom_call" | custom-call | flops 1 | bytes 1 | tf_op jit(solution)/shard_map/base/pallas_call | solution.py:224
  36.9 0.0 collective-permute-done.5.near.hal2
  36.9 0.0 slice-start
  36.9 1.1 %inner.6.inn = f32[2,4,64,256]{3,2,1,0:T(8,128)S(1)} custom-call(f32[2,4,64,256]{3,2,1,0:T(8,128)S(1)} %inner.5.other.inn.prev_inn.in2, f32[2,4,64,256]{3,2,1,0:T(8,128)S(1)} %finish.5.half.out.prev_out.out2, f32[2,4,64,256]{3,2,1,0:T(8,128)S(1)} %collective-permute-done.5.near.hal2, f32[2,4,64,256]{3,2,1,0:T(8,128)S(1)} %inner.4.inn.prev_inn, ...), custom_call_target="tpu_custom_call" | custom-call | flops 1 | bytes 1 | tf_op jit(solution)/shard_map/inner/pallas_call | solution.py:224
  38.1 0.1 collective-permute-start.6
  38.2 4.9 %collective-permute-done.4.halo = f32[2,4,64,256]{3,2,1,0:T(8,128)S(1)} collective-permute-done((f32[2,4,64,256]{3,2,1,0:T(8,128)S(1)}, f32[2,4,64,256]{3,2,1,0:T(8,128)S(1)}, u32[]{:S(2)}, u32[]{:S(2)}) %collective-permute-start.4) | collective-permute-done | bytes 524320 | tf_op jit(solution)/shard_map/ppermute | solution.py:439
  43.0 0.5 finish.6.out
  43.5 0.0 copy-start.3
  43.5 0.0 slice-start.1
  43.5 0.0 copy-start.2
  43.6 4.5 %collective-permute-start.7 = (f32[2,4,64,256]{3,2,1,0:T(8,128)S(1)}, f32[2,4,64,256]{3,2,1,0:T(8,128)S(1)}, u32[]{:S(2)}, u32[]{:S(2)}) collective-permute-start(f32[2,4,64,256]{3,2,1,0:T(8,128)S(1)} %finish.6.out), channel_id=1, source_target_pairs={{1,2},{3,4},{5,6},{7,8},{9,10},{11,12},{13,14},{2,1},{4,3},{6,5},{... | collective-permute-start | bytes 1572872 | tf_op jit(solution)/shard_map/ppermute | solution.py:439
  48.1 0.9 %base.5 = f32[2,4,64,256]{3,2,1,0:T(8,128)S(1)} custom-call(f32[2,4,64,256]{3,2,1,0:T(8,128)S(1)} %finish.6.out, f32[2,4,64,256]{3,2,1,0:T(8,128)S(1)} %inner.6.inn, f32[2,4,64,256]{3,2,1,0:T(8,128)S(1)} %finish.5.half.out.prev_out.out2, f32[3,4,64,256]{3,2,1,0:T(8,128)S(1)} %get-tuple-element.11.coef.coef_out, bf16[2,256,256]{2,1,0:T(8,128)(2,1)S(1)} %copy-done, ...), custom_call_target="tpu_custom_call" | custom-call | flops 1 | bytes 1 | tf_op jit(solution)/shard_map/base/pallas_call | solution.py:224
  49.0 0.0 collective-permute-done.6.near
  49.0 1.0 %inner.7.in4.other = f32[2,4,64,256]{3,2,1,0:T(8,128)S(1)} custom-call(f32[2,4,64,256]{3,2,1,0:T(8,128)S(1)} %inner.6.inn, f32[2,4,64,256]{3,2,1,0:T(8,128)S(1)} %finish.6.out, f32[2,4,64,256]{3,2,1,0:T(8,128)S(1)} %collective-permute-done.6.near, f32[2,4,64,256]{3,2,1,0:T(8,128)S(1)} %inner.5.other.inn.prev_inn.in2, ...), custom_call_target="tpu_custom_call" | custom-call | flops 1 | bytes 1 | tf_op jit(solution)/shard_map/inner/pallas_call | solution.py:224
  50.0 0.1 collective-permute-start.8
  50.1 5.1 %collective-permute-done.7.halo = f32[2,4,64,256]{3,2,1,0:T(8,128)S(1)} collective-permute-done((f32[2,4,64,256]{3,2,1,0:T(8,128)S(1)}, f32[2,4,64,256]{3,2,1,0:T(8,128)S(1)}, u32[]{:S(2)}, u32[]{:S(2)}) %collective-permute-start.7) | collective-permute-done | bytes 524320 | tf_op jit(solution)/shard_map/ppermute | solution.py:439
  55.2 0.4 finish.7.out4.half
  55.6 4.4 %collective-permute-start.9 = (f32[2,4,64,256]{3,2,1,0:T(8,128)S(1)}, f32[2,4,64,256]{3,2,1,0:T(8,128)S(1)}, u32[]{:S(2)}, u32[]{:S(2)}) collective-permute-start(f32[2,4,64,256]{3,2,1,0:T(8,128)S(1)} %finish.7.out4.half), channel_id=1, source_target_pairs={{1,2},{3,4},{5,6},{7,8},{9,10},{11,12},{13,14},{2,1},{4,3},{6,5},{... | collective-permute-start | bytes 1572872 | tf_op jit(solution)/shard_map/ppermute | solution.py:439
  60.0 0.0 copy-done.3
  60.0 0.1 fusion.mute
  60.2 0.0 slice-done
  60.2 0.0 slice-done.1
  60.2 0.0 copy-done.2
  60.2 1.7 %image_mid.1.part = f32[9,4,64,256]{3,2,1,0:T(8,128)S(1)} custom-call(f32[9,8,64,256]{3,2,1,0:T(8,128)S(1)} %bitcast.16, s32[9]{0:T(128)S(1)} %copy-done.2, f32[8,64,256]{2,1,0:T(8,128)S(1)} %fusion.mute, f32[2,4,64,256]{3,2,1,0:T(8,128)S(1)} %finish.5.half.out.prev_out.out2, f32[2,4,64,256]{3,2,1,0:T(8,128)S(1)} %inner.5.other.inn.prev_inn.in2, ...), custom_call_target="tpu_custom_call" | custom-call | flops 1 | bytes 1 | tf_op jit(solution)/shard_map/image_mid/pallas_call | solution.py:327
  61.9 0.0 collective-permute-done.8.hal4
  61.9 3.2 %image_main.1 = (f32[9,8,64,256]{3,2,1,0:T(8,128)}, f32[8,64,256]{2,1,0:T(8,128)}, f32[8,64,256]{2,1,0:T(8,128)}) custom-call(f32[9,8,64,256]{3,2,1,0:T(8,128)S(1)} %bitcast.17, f32[9,4,64,256]{3,2,1,0:T(8,128)S(1)} %image_mid.1.part, s32[9]{0:T(128)S(1)} %copy-done.2, f32[8,64,256]{2,1,0:T(8,128)S(1)} %fusion.mute, ...), custom_call_target="tpu_custom_call" | custom-call | flops 1 | bytes 1 | tf_op jit(solution)/shard_map/image_main/pallas_call | solution.py:386
  65.1 2.0 %collective-permute-done.9.halo = f32[2,4,64,256]{3,2,1,0:T(8,128)S(1)} collective-permute-done((f32[2,4,64,256]{3,2,1,0:T(8,128)S(1)}, f32[2,4,64,256]{3,2,1,0:T(8,128)S(1)}, u32[]{:S(2)}, u32[]{:S(2)}) %collective-permute-start.9) | collective-permute-done | bytes 524320 | tf_op jit(solution)/shard_map/ppermute | solution.py:439
  67.1 1.7 %image_last.1 = f32[9,8,64,256]{3,2,1,0:T(8,128)} custom-call(f32[9,8,64,256]{3,2,1,0:T(8,128)} %get-tuple-element.14.image_old, f32[9,4,64,256]{3,2,1,0:T(8,128)S(1)} %image_mid.1.part, s32[9]{0:T(128)S(1)} %copy-done.2, f32[8,64,256]{2,1,0:T(8,128)S(1)} %fusion.mute, f32[2,4,64,256]{3,2,1,0:T(8,128)S(1)} %finish.7.out4.half, ...), custom_call_target="tpu_custom_call", output_to_operand_aliasing={{}: (0, {})} | custom-call | flops 1 | bytes 1 | tf_op jit(solution)/shard_map/image_last/pallas_call | solution.py:419
  (1 shorter events, 0.0 us)
Async XLA Ops:
  1.8 5.9 %copy-start = (bf16[2,256,256]{2,1,0:T(8,128)(2,1)S(1)}, bf16[2,256,256]{2,1,0:T(8,128)(2,1)}, u32[]{:S(2)}) copy-start(bf16[2,256,256]{2,1,0:T(8,128)(2,1)} %constant.4.clone.wz) | copy-start | bytes 786436
  1.8 5.9 %copy-start.1 = (bf16[256,256]{1,0:T(8,128)(2,1)S(1)}, bf16[256,256]{1,0:T(8,128)(2,1)}, u32[]{:S(2)}) copy-start(bf16[256,256]{1,0:T(8,128)(2,1)} %constant.5.clone.wy) | copy-start | bytes 393220
  1.8 16.4 %collective-permute-start = (f32[2,4,64,256]{3,2,1,0:T(8,128)S(1)}, f32[2,4,64,256]{3,2,1,0:T(8,128)S(1)}, u32[]{:S(2)}, u32[]{:S(2)}) collective-permute-start(f32[2,4,64,256]{3,2,1,0:T(8,128)S(1)} %gather.2.out.prev_out), channel_id=1, source_target_pairs={{1,2},{3,4},{5,6},{7,8},{9,10},{11,12},{13,14},{2,1},{4,3},{6,5},{... | collective-permute-start | bytes 1572872 | tf_op jit(solution)/shard_map/ppermute | solution.py:439
  7.6 2.7 %collective-permute-start.2 = (f32[2,4,64,256]{3,2,1,0:T(8,128)S(1)}, f32[2,4,64,256]{3,2,1,0:T(8,128)S(1)}, u32[]{:S(2)}, u32[]{:S(2)}) collective-permute-start(f32[2,4,64,256]{3,2,1,0:T(8,128)S(1)} %gather.3.inn.prev_inn), channel_id=1, source_target_pairs={{0,1},{1,0},{2,3},{3,2},{4,5},{5,4},{6,7},{7,6},{8,9},{9,8},{10,11... | collective-permute-start | bytes 1572872 | tf_op jit(solution)/shard_map/ppermute | solution.py:443
  11.3 12.6 %collective-permute-start.3 = (f32[2,4,64,256]{3,2,1,0:T(8,128)S(1)}, f32[2,4,64,256]{3,2,1,0:T(8,128)S(1)}, u32[]{:S(2)}, u32[]{:S(2)}) collective-permute-start(f32[2,4,64,256]{3,2,1,0:T(8,128)S(1)} %inner.4.inn.prev_inn), channel_id=1, source_target_pairs={{0,1},{1,0},{2,3},{3,2},{4,5},{5,4},{6,7},{7,6},{8,9},{9,8},{10,11... | collective-permute-start | bytes 1572872 | tf_op jit(solution)/shard_map/ppermute | solution.py:443
  18.7 12.4 %collective-permute-start.1 = (f32[2,4,64,256]{3,2,1,0:T(8,128)S(1)}, f32[2,4,64,256]{3,2,1,0:T(8,128)S(1)}, u32[]{:S(2)}, u32[]{:S(2)}) collective-permute-start(f32[2,4,64,256]{3,2,1,0:T(8,128)S(1)} %finish.4.out.prev_out), channel_id=1, source_target_pairs={{1,2},{3,4},{5,6},{7,8},{9,10},{11,12},{13,14},{2,1},{4,3},{6,5},{... | collective-permute-start | bytes 1572872 | tf_op jit(solution)/shard_map/ppermute | solution.py:439
  24.9 12.0 %collective-permute-start.5 = (f32[2,4,64,256]{3,2,1,0:T(8,128)S(1)}, f32[2,4,64,256]{3,2,1,0:T(8,128)S(1)}, u32[]{:S(2)}, u32[]{:S(2)}) collective-permute-start(f32[2,4,64,256]{3,2,1,0:T(8,128)S(1)} %inner.5.other.inn.prev_inn.in2), channel_id=1, source_target_pairs={{0,1},{1,0},{2,3},{3,2},{4,5},{5,4},{6,7},{7,6},{8,9},{9,8},{10,11... | collective-permute-start | bytes 1572872 | tf_op jit(solution)/shard_map/ppermute | solution.py:443
  31.5 11.5 %collective-permute-start.4 = (f32[2,4,64,256]{3,2,1,0:T(8,128)S(1)}, f32[2,4,64,256]{3,2,1,0:T(8,128)S(1)}, u32[]{:S(2)}, u32[]{:S(2)}) collective-permute-start(f32[2,4,64,256]{3,2,1,0:T(8,128)S(1)} %finish.5.half.out.prev_out.out2), channel_id=1, source_target_pairs={{1,2},{3,4},{5,6},{7,8},{9,10},{11,12},{13,14},{2,1},{4,3},{6,5},{... | collective-permute-start | bytes 1572872 | tf_op jit(solution)/shard_map/ppermute | solution.py:439
  36.9 23.3 %slice-start = ((s8[4718592]{0:T(1024)(128)(4,1)}), s8[4194304]{0:T(1024)(128)(4,1)S(1)}, s32[]{:S(2)}) async-start(s8[4718592]{0:T(1024)(128)(4,1)} %bitcast.14), calls=%async_computation | async-start | bytes 8388608
  38.1 10.9 %collective-permute-start.6 = (f32[2,4,64,256]{3,2,1,0:T(8,128)S(1)}, f32[2,4,64,256]{3,2,1,0:T(8,128)S(1)}, u32[]{:S(2)}, u32[]{:S(2)}) collective-permute-start(f32[2,4,64,256]{3,2,1,0:T(8,128)S(1)} %inner.6.inn), channel_id=1, source_target_pairs={{0,1},{1,0},{2,3},{3,2},{4,5},{5,4},{6,7},{7,6},{8,9},{9,8},{10,11... | collective-permute-start | bytes 1572872 | tf_op jit(solution)/shard_map/ppermute | solution.py:443
  43.5 16.5 %copy-start.3 = (s32[1,8,64]{2,1,0:T(8,128)S(1)}, s32[1,8,64]{2,1,0:T(8,128)}, u32[]{:S(2)}) copy-start(s32[1,8,64]{2,1,0:T(8,128)} %param.19) | copy-start | bytes 6148
  43.5 16.7 %slice-start.1 = ((s8[4718592]{0:T(1024)(128)(4,1)}), s8[524288]{0:T(1024)(128)(4,1)S(1)}, s32[]{:S(2)}) async-start(s8[4718592]{0:T(1024)(128)(4,1)} %bitcast.14), calls=%async_computation.1 | async-start | bytes 1048576
  43.5 16.7 %copy-start.2 = (s32[9]{0:T(128)S(1)}, s32[9]{0:T(128)}, u32[]{:S(2)}) copy-start(s32[9]{0:T(128)} %offsets.5) | copy-start | bytes 112
  43.6 11.6 %collective-permute-start.7 = (f32[2,4,64,256]{3,2,1,0:T(8,128)S(1)}, f32[2,4,64,256]{3,2,1,0:T(8,128)S(1)}, u32[]{:S(2)}, u32[]{:S(2)}) collective-permute-start(f32[2,4,64,256]{3,2,1,0:T(8,128)S(1)} %finish.6.out), channel_id=1, source_target_pairs={{1,2},{3,4},{5,6},{7,8},{9,10},{11,12},{13,14},{2,1},{4,3},{6,5},{... | collective-permute-start | bytes 1572872 | tf_op jit(solution)/shard_map/ppermute | solution.py:439
  50.0 11.9 %collective-permute-start.8 = (f32[2,4,64,256]{3,2,1,0:T(8,128)S(1)}, f32[2,4,64,256]{3,2,1,0:T(8,128)S(1)}, u32[]{:S(2)}, u32[]{:S(2)}) collective-permute-start(f32[2,4,64,256]{3,2,1,0:T(8,128)S(1)} %inner.7.in4.other), channel_id=1, source_target_pairs={{0,1},{1,0},{2,3},{3,2},{4,5},{5,4},{6,7},{7,6},{8,9},{9,8},{10,11... | collective-permute-start | bytes 1572872 | tf_op jit(solution)/shard_map/ppermute | solution.py:443
  55.6 11.5 %collective-permute-start.9 = (f32[2,4,64,256]{3,2,1,0:T(8,128)S(1)}, f32[2,4,64,256]{3,2,1,0:T(8,128)S(1)}, u32[]{:S(2)}, u32[]{:S(2)}) collective-permute-start(f32[2,4,64,256]{3,2,1,0:T(8,128)S(1)} %finish.7.out4.half), channel_id=1, source_target_pairs={{1,2},{3,4},{5,6},{7,8},{9,10},{11,12},{13,14},{2,1},{4,3},{6,5},{... | collective-permute-start | bytes 1572872 | tf_op jit(solution)/shard_map/ppermute | solution.py:439

commit v5 on v4

--- a/solution.py
+++ b/solution.py
@@ -281,22 +281,27 @@
 BY_REACH = (-4, 4, -3, 3, -2, 2, -1, 1, 0)
 
 
-def add_terms(old, new, slot, h, planes, mute, snaps, inner):
+def add_terms(old, new, slots, planes, mute, snaps, inner):
     flip = is_flipped(inner)
     rows = old.shape[2]
+    chunk = CHUNK
+    while chunk < rows and 2 * chunk * len(planes) * len(slots) <= 128:
+        chunk *= 2
 
     def body(i, carry):
-        span = pl.ds(pl.multiple_of(i * CHUNK, CHUNK), CHUNK)
+        span = pl.ds(pl.multiple_of(i * chunk, chunk), chunk)
         for m in planes:
-            total = None
-            for half, other, halo in snaps:
-                t = at(half, other, halo, 0, m - h)[span] * at(half, other, halo, 1, m + h)[span]
-                total = t if total is None else total + t
             local = m + flip * (3 - 2 * m)
-            new[slot, local, span] = old[slot, local, span] + mute[natural(m, flip), span] * total
+            mask = mute[natural(m, flip), span]
+            for h, slot in slots.items():
+                total = None
+                for half, other, halo in snaps:
+                    t = at(half, other, halo, 0, m - h)[span] * at(half, other, halo, 1, m + h)[span]
+                    total = t if total is None else total + t
+                new[slot, local, span] = old[slot, local, span] + mask * total
         return carry
 
-    lax.fori_loop(0, rows // CHUNK, body, 0)
+    lax.fori_loop(0, rows // chunk, body, 0)
 
 
 def store_planes(buffer, image, slot, first, count, inner, sem):
@@ -319,7 +324,7 @@
         c.start()
     for i, h in enumerate(BY_REACH):
         copies[i].wait()
-        add_terms(acc, acc, slot[i], h, range(4), mute, [(half, other, halo)], False)
+        add_terms(acc, acc, {h: slot[i]}, range(4), mute, [(half, other, halo)], False)
 
 
 def image_mid(image_in, offsets, mute, half, other, halo):
@@ -338,12 +343,14 @@
 
 def image_main_kernel(
     image_in, part, offsets, mute, in2, out2, hal2, in4, out4, hal4,
-    image, src, rec, acc, done, slots, sem, sems,
+    image, src, rec, table, acc, done, slots, sem, sems,
 ):
     find_slots(offsets, slots)
     inner_half = pl.ds(4 * is_flipped(True), 4)
     inner_slot = [slot_of(slots, True, h) for h in BY_REACH]
     outer_slot = [slot_of(slots, False, h) for h in BY_REACH]
+    for h, k in zip(BY_REACH, outer_slot):
+        table[pl.ds(h + HMAX, 1)] = jnp.full((1, table.shape[1]), k, jnp.int32)
     fetches = [
         pltpu.make_async_copy(image_in.at[k, inner_half], acc.at[k], sem.at[i])
         for i, k in enumerate(inner_slot)
@@ -367,13 +374,13 @@
         if reach == 4:
             continue
         k = outer_slot[i]
-        add_terms(part, done, k, h, range(reach, 4), mute, [(out4, in4, None)], False)
+        add_terms(part, done, {h: k}, range(reach, 4), mute, [(out4, in4, None)], False)
         stores.append(store_planes(done, image, k, reach, 4 - reach, False, sem.at[NOFF + i]))
         stores[-1].start()
     for i, h in enumerate(BY_REACH):
         fetches[i].wait()
         k = inner_slot[i]
-        add_terms(acc, acc, k, h, range(4), mute, [(in2, out2, hal2), (in4, out4, hal4)], True)
+        add_terms(acc, acc, {h: k}, range(4), mute, [(in2, out2, hal2), (in4, out4, hal4)], True)
         stores.append(store_planes(acc, image, k, 0, 4, True, sem.at[i]))
         stores[-1].start()
     for c in copies + stores:
@@ -385,9 +392,12 @@
     field = jax.ShapeDtypeStruct((8,) + shape[2:], jnp.float32)
     return pl.pallas_call(
         image_main_kernel,
-        out_shape=[jax.ShapeDtypeStruct(image_in.shape, jnp.float32), field, field],
+        out_shape=[
+            jax.ShapeDtypeStruct(image_in.shape, jnp.float32), field, field,
+            jax.ShapeDtypeStruct((NOFF, 128), jnp.int32),
+        ],
         in_specs=[HBM, VMEM, SMEM] + [VMEM] * 7,
-        out_specs=[HBM] * 3,
+        out_specs=[HBM] * 3 + [VMEM],
         scratch_shapes=[
             pltpu.VMEM(part.shape, jnp.float32),
             pltpu.VMEM(part.shape, jnp.float32),
@@ -401,36 +411,34 @@
     )(image_in, part, offsets, mute, *snap2, *snap4)
 
 
-def image_last_kernel(image_old, part, offsets, mute, half, other, halo, image, done, slots, sem):
+def image_last_kernel(image_old, part, table, mute, half, other, halo, image, done, sem):
     del image_old
-    find_slots(offsets, slots)
     stores = []
-    for i, h in enumerate(BY_REACH[:-1]):
-        reach = abs(h)
-        k = slot_of(slots, False, h)
-        add_terms(part, done, k, h, range(reach), mute, [(half, other, halo)], False)
-        stores.append(store_planes(done, image, k, 0, reach, False, sem.at[i]))
-        stores[-1].start()
+    for reach in range(HMAX, 0, -1):
+        pair = {h: table[h + HMAX, 0] for h in (-reach, reach)}
+        add_terms(part, done, pair, range(reach), mute, [(half, other, halo)], False)
+        for k in pair.values():
+            stores.append(store_planes(done, image, k, 0, reach, False, sem.at[len(stores)]))
+            stores[-1].start()
     for c in stores:
         c.wait()
 
 
-def image_last(image, part, offsets, mute, snap4):
+def image_last(image, part, table, mute, snap4):
     return pl.pallas_call(
         image_last_kernel,
         out_shape=jax.ShapeDtypeStruct(image.shape, jnp.float32),
-        in_specs=[HBM, VMEM, SMEM] + [VMEM] * 4,
+        in_specs=[HBM] + [VMEM] * 6,
         out_specs=HBM,
         scratch_shapes=[
             pltpu.VMEM(part.shape, jnp.float32),
-            pltpu.SMEM((NOFF,), jnp.int32),
             pltpu.SemaphoreType.DMA((NOFF,)),
         ],
         input_output_aliases={0: 0},
         cost_estimate=CHEAP,
         compiler_params=pltpu.CompilerParams(vmem_limit_bytes=8 * MIB),
         name="image_last",
-    )(image, part, offsets, mute, *snap4)
+    )(image, part, table, mute, *snap4)
 
 
 def across_chips(value, start=1, stride=2):
@@ -482,10 +490,10 @@
         prev_inn, prev_out, inn, out = inn, out, new_inn, new_out
         near = within_chip(inn)
         far = across_chips(out)
-    image, source_last, receiver_last = image_main(
+    image, source_last, receiver_last, table = image_main(
         image_in, part, offsets, mute, snap2, (inn, out, near)
     )
-    image = image_last(image, part, offsets, mute, (out, inn, far))
+    image = image_last(image, part, table, mute, (out, inn, far))
     return (image[:, None], source_last[None], receiver_last[None])
 
 

time: 69.3 us -> 68.8 us (level)
  Pallas kernels: 20.1 us -> 19.4 us
where the time goes in v5:
time: 68.8 us; the launch traced here: 68.4 us
  waiting for transfers between devices  24.7 us (36%)
  starting transfers between devices  23.2 us (34%)
  Pallas kernels  19.4 us (28%)
  between operations  0.95 us (1%)
    ppermute x5, waiting for transfers between devices, across_chips(): return lax.ppermute(value, 'blk', pairs + [(b, a) for a, b in pairs])  24.7 us
    ppermute x5, starting transfers between devices, across_chips(): return lax.ppermute(value, 'blk', pairs + [(b, a) for a, b in pairs])  22.4 us
    pallas_call x7, Pallas kernels, half_step(): pl.pallas_call(kernel, out_shape=jax.ShapeDtypeStruct(shape, jnp.float32)...  6.92 us
    pallas_call x1, Pallas kernels, image_main(): pl.pallas_call(image_main_kernel, out_shape=[jax.ShapeDtypeStruct(image_i...  3.14 us
    pallas_call x1, Pallas kernels, first(): pl.pallas_call(first_kernel, out_shape=[pair, three, three, pair], in_spe...  2.57 us
    pallas_call x2, Pallas kernels, gather(): pl.pallas_call(functools.partial(gather_kernel, plan, len(arrays)), out_s...  2.28 us
    pallas_call x4, Pallas kernels, finish(): pl.pallas_call(finish_kernel, out_shape=jax.ShapeDtypeStruct(halo.shape,...  1.79 us
    pallas_call x1, Pallas kernels, image_mid(): pl.pallas_call(image_mid_kernel, out_shape=jax.ShapeDtypeStruct(shape, jn...  1.42 us
  transfers between devices with their start and end apart: 10, of which 5 were waited for; matrix products, arithmetic and copies ran while one was open for 0% of the time, Pallas kernels for 25%

profile of v5, /device:TPU:1, one launch (start us, length us, event | category | flops | bytes accessed | tf_op | source)
XLA Modules:
  0.0 68.4 jit_solution(18082110960188149651)
XLA Ops:
  0.6 1.1 %gather.2.out.prev_out = f32[2,4,64,256]{3,2,1,0:T(8,128)S(1)} custom-call(f32[8,64,256]{2,1,0:T(8,128)} %bitcast.20, f32[8,64,256]{2,1,0:T(8,128)} %bitcast.22), custom_call_target="tpu_custom_call" | custom-call | flops 10000000000 | bytes 20000000 | tf_op jit(solution)/shard_map/gather/pallas_call | solution.py:94
  1.8 0.0 copy-start
  1.8 0.0 copy-start.1
  1.8 4.7 %collective-permute-start = (f32[2,4,64,256]{3,2,1,0:T(8,128)S(1)}, f32[2,4,64,256]{3,2,1,0:T(8,128)S(1)}, u32[]{:S(2)}, u32[]{:S(2)}) collective-permute-start(f32[2,4,64,256]{3,2,1,0:T(8,128)S(1)} %gather.2.out.prev_out), channel_id=1, source_target_pairs={{1,2},{3,4},{5,6},{7,8},{9,10},{11,12},{13,14},{2,1},{4,3},{6,5},{... | collective-permute-start | bytes 1572872 | tf_op jit(solution)/shard_map/ppermute | solution.py:447
  6.5 1.1 %gather.3.inn.prev_inn = f32[2,4,64,256]{3,2,1,0:T(8,128)S(1)} custom-call(f32[8,64,256]{2,1,0:T(8,128)} %bitcast.21, f32[8,64,256]{2,1,0:T(8,128)} %bitcast.23), custom_call_target="tpu_custom_call" | custom-call | flops 10000000000 | bytes 20000000 | tf_op jit(solution)/shard_map/gather/pallas_call | solution.py:94
  7.6 0.1 collective-permute-start.2
  7.7 0.0 copy-done
  7.7 0.0 copy-done.1
  7.7 2.6 %first.1 = (f32[2,4,64,256]{3,2,1,0:T(8,128)S(1)}, f32[3,4,64,256]{3,2,1,0:T(8,128)S(1)}, f32[3,4,64,256]{3,2,1,0:T(8,128)S(1)}, f32[2,4,64,256]{3,2,1,0:T(8,128)S(1)}) custom-call(f32[2,4,64,256]{3,2,1,0:T(8,128)S(1)} %gather.2.out.prev_out, f32[2,4,64,256]{3,2,1,0:T(8,128)S(1)} %gather.3.inn.prev_inn, bf16[2,256,256]{2,1,0:T(8,128)(2,1)S(1)} %copy-done, ...), custom_call_target="tpu_custom_call" | custom-call | flops 10000000000 | bytes 20000000 | tf_op jit(solution)/shard_map/first/pallas_call | solution.py:210
  10.3 0.0 collective-permute-done.2.near
  10.3 1.0 %inner.4.inn.prev_inn = f32[2,4,64,256]{3,2,1,0:T(8,128)S(1)} custom-call(f32[2,4,64,256]{3,2,1,0:T(8,128)S(1)} %gather.3.inn.prev_inn, f32[2,4,64,256]{3,2,1,0:T(8,128)S(1)} %gather.2.out.prev_out, f32[2,4,64,256]{3,2,1,0:T(8,128)S(1)} %collective-permute-done.2.near, f32[2,4,64,256]{3,2,1,0:T(8,128)S(1)} %get-tuple-element.13.prev_inn, ...), custom_call_target="tpu_custom_call" | custom-call | flops 1 | bytes 1 | tf_op jit(solution)/shard_map/inner/pallas_call | solution.py:224
  11.3 0.5 collective-permute-start.3
  11.8 6.4 %collective-permute-done.halo = f32[2,4,64,256]{3,2,1,0:T(8,128)S(1)} collective-permute-done((f32[2,4,64,256]{3,2,1,0:T(8,128)S(1)}, f32[2,4,64,256]{3,2,1,0:T(8,128)S(1)}, u32[]{:S(2)}, u32[]{:S(2)}) %collective-permute-start) | collective-permute-done | bytes 524320 | tf_op jit(solution)/shard_map/ppermute | solution.py:447
  18.2 0.4 finish.4.out.prev_out
  18.7 4.4 %collective-permute-start.1 = (f32[2,4,64,256]{3,2,1,0:T(8,128)S(1)}, f32[2,4,64,256]{3,2,1,0:T(8,128)S(1)}, u32[]{:S(2)}, u32[]{:S(2)}) collective-permute-start(f32[2,4,64,256]{3,2,1,0:T(8,128)S(1)} %finish.4.out.prev_out), channel_id=1, source_target_pairs={{1,2},{3,4},{5,6},{7,8},{9,10},{11,12},{13,14},{2,1},{4,3},{6,5},{... | collective-permute-start | bytes 1572872 | tf_op jit(solution)/shard_map/ppermute | solution.py:447
  23.1 0.8 %base.3 = f32[2,4,64,256]{3,2,1,0:T(8,128)S(1)} custom-call(f32[2,4,64,256]{3,2,1,0:T(8,128)S(1)} %finish.4.out.prev_out, f32[2,4,64,256]{3,2,1,0:T(8,128)S(1)} %inner.4.inn.prev_inn, f32[2,4,64,256]{3,2,1,0:T(8,128)S(1)} %gather.2.out.prev_out, f32[3,4,64,256]{3,2,1,0:T(8,128)S(1)} %get-tuple-element.12.coef.coef_out, bf16[2,256,256]{2,1,0:T(8,128)(2,1)S(1)} %copy-done, ...), custom_call_target="tpu_custom_call" | custom-call | flops 1 | bytes 1 | tf_op jit(solution)/shard_map/base/pallas_call | solution.py:224
  23.9 0.0 collective-permute-done.3.near
  23.9 1.0 %inner.5.other.inn.prev_inn.in2 = f32[2,4,64,256]{3,2,1,0:T(8,128)S(1)} custom-call(f32[2,4,64,256]{3,2,1,0:T(8,128)S(1)} %inner.4.inn.prev_inn, f32[2,4,64,256]{3,2,1,0:T(8,128)S(1)} %finish.4.out.prev_out, f32[2,4,64,256]{3,2,1,0:T(8,128)S(1)} %collective-permute-done.3.near, f32[2,4,64,256]{3,2,1,0:T(8,128)S(1)} %gather.3.inn.prev_inn, ...), custom_call_target="tpu_custom_call" | custom-call | flops 1 | bytes 1 | tf_op jit(solution)/shard_map/inner/pallas_call | solution.py:224
  24.9 0.1 collective-permute-start.5
  25.0 6.1 %collective-permute-done.1.halo = f32[2,4,64,256]{3,2,1,0:T(8,128)S(1)} collective-permute-done((f32[2,4,64,256]{3,2,1,0:T(8,128)S(1)}, f32[2,4,64,256]{3,2,1,0:T(8,128)S(1)}, u32[]{:S(2)}, u32[]{:S(2)}) %collective-permute-start.1) | collective-permute-done | bytes 524320 | tf_op jit(solution)/shard_map/ppermute | solution.py:447
  31.1 0.4 finish.5.half.out.prev_out.out2
  31.5 4.4 %collective-permute-start.4 = (f32[2,4,64,256]{3,2,1,0:T(8,128)S(1)}, f32[2,4,64,256]{3,2,1,0:T(8,128)S(1)}, u32[]{:S(2)}, u32[]{:S(2)}) collective-permute-start(f32[2,4,64,256]{3,2,1,0:T(8,128)S(1)} %finish.5.half.out.prev_out.out2), channel_id=1, source_target_pairs={{1,2},{3,4},{5,6},{7,8},{9,10},{11,12},{13,14},{2,1},{4,3},{6,5},{... | collective-permute-start | bytes 1572872 | tf_op jit(solution)/shard_map/ppermute | solution.py:447
  35.9 1.0 %base.4 = f32[2,4,64,256]{3,2,1,0:T(8,128)S(1)} custom-call(f32[2,4,64,256]{3,2,1,0:T(8,128)S(1)} %finish.5.half.out.prev_out.out2, f32[2,4,64,256]{3,2,1,0:T(8,128)S(1)} %inner.5.other.inn.prev_inn.in2, f32[2,4,64,256]{3,2,1,0:T(8,128)S(1)} %finish.4.out.prev_out, f32[3,4,64,256]{3,2,1,0:T(8,128)S(1)} %get-tuple-element.12.coef.coef_out, ...), custom_call_target="tpu_custom_call" | custom-call | flops 1 | bytes 1 | tf_op jit(solution)/shard_map/base/pallas_call | solution.py:224
  37.0 0.0 collective-permute-done.5.near.hal2
  37.0 0.0 slice-start
  37.0 1.2 %inner.6.inn = f32[2,4,64,256]{3,2,1,0:T(8,128)S(1)} custom-call(f32[2,4,64,256]{3,2,1,0:T(8,128)S(1)} %inner.5.other.inn.prev_inn.in2, f32[2,4,64,256]{3,2,1,0:T(8,128)S(1)} %finish.5.half.out.prev_out.out2, f32[2,4,64,256]{3,2,1,0:T(8,128)S(1)} %collective-permute-done.5.near.hal2, f32[2,4,64,256]{3,2,1,0:T(8,128)S(1)} %inner.4.inn.prev_inn, ...), custom_call_target="tpu_custom_call" | custom-call | flops 1 | bytes 1 | tf_op jit(solution)/shard_map/inner/pallas_call | solution.py:224
  38.2 0.1 collective-permute-start.6
  38.2 4.8 %collective-permute-done.4.halo = f32[2,4,64,256]{3,2,1,0:T(8,128)S(1)} collective-permute-done((f32[2,4,64,256]{3,2,1,0:T(8,128)S(1)}, f32[2,4,64,256]{3,2,1,0:T(8,128)S(1)}, u32[]{:S(2)}, u32[]{:S(2)}) %collective-permute-start.4) | collective-permute-done | bytes 524320 | tf_op jit(solution)/shard_map/ppermute | solution.py:447
  43.0 0.5 finish.6.out
  43.5 0.0 copy-start.3
  43.5 0.0 slice-start.1
  43.5 0.0 copy-start.2
  43.5 4.5 %collective-permute-start.7 = (f32[2,4,64,256]{3,2,1,0:T(8,128)S(1)}, f32[2,4,64,256]{3,2,1,0:T(8,128)S(1)}, u32[]{:S(2)}, u32[]{:S(2)}) collective-permute-start(f32[2,4,64,256]{3,2,1,0:T(8,128)S(1)} %finish.6.out), channel_id=1, source_target_pairs={{1,2},{3,4},{5,6},{7,8},{9,10},{11,12},{13,14},{2,1},{4,3},{6,5},{... | collective-permute-start | bytes 1572872 | tf_op jit(solution)/shard_map/ppermute | solution.py:447
  48.1 0.9 %base.5 = f32[2,4,64,256]{3,2,1,0:T(8,128)S(1)} custom-call(f32[2,4,64,256]{3,2,1,0:T(8,128)S(1)} %finish.6.out, f32[2,4,64,256]{3,2,1,0:T(8,128)S(1)} %inner.6.inn, f32[2,4,64,256]{3,2,1,0:T(8,128)S(1)} %finish.5.half.out.prev_out.out2, f32[3,4,64,256]{3,2,1,0:T(8,128)S(1)} %get-tuple-element.12.coef.coef_out, bf16[2,256,256]{2,1,0:T(8,128)(2,1)S(1)} %copy-done, ...), custom_call_target="tpu_custom_call" | custom-call | flops 1 | bytes 1 | tf_op jit(solution)/shard_map/base/pallas_call | solution.py:224
  48.9 0.0 collective-permute-done.6.near
  48.9 1.0 %inner.7.in4.other = f32[2,4,64,256]{3,2,1,0:T(8,128)S(1)} custom-call(f32[2,4,64,256]{3,2,1,0:T(8,128)S(1)} %inner.6.inn, f32[2,4,64,256]{3,2,1,0:T(8,128)S(1)} %finish.6.out, f32[2,4,64,256]{3,2,1,0:T(8,128)S(1)} %collective-permute-done.6.near, f32[2,4,64,256]{3,2,1,0:T(8,128)S(1)} %inner.5.other.inn.prev_inn.in2, ...), custom_call_target="tpu_custom_call" | custom-call | flops 1 | bytes 1 | tf_op jit(solution)/shard_map/inner/pallas_call | solution.py:224
  50.0 0.1 collective-permute-start.8
  50.0 5.1 %collective-permute-done.7.halo = f32[2,4,64,256]{3,2,1,0:T(8,128)S(1)} collective-permute-done((f32[2,4,64,256]{3,2,1,0:T(8,128)S(1)}, f32[2,4,64,256]{3,2,1,0:T(8,128)S(1)}, u32[]{:S(2)}, u32[]{:S(2)}) %collective-permute-start.7) | collective-permute-done | bytes 524320 | tf_op jit(solution)/shard_map/ppermute | solution.py:447
  55.2 0.4 finish.7.out4.half
  55.6 4.4 %collective-permute-start.9 = (f32[2,4,64,256]{3,2,1,0:T(8,128)S(1)}, f32[2,4,64,256]{3,2,1,0:T(8,128)S(1)}, u32[]{:S(2)}, u32[]{:S(2)}) collective-permute-start(f32[2,4,64,256]{3,2,1,0:T(8,128)S(1)} %finish.7.out4.half), channel_id=1, source_target_pairs={{1,2},{3,4},{5,6},{7,8},{9,10},{11,12},{13,14},{2,1},{4,3},{6,5},{... | collective-permute-start | bytes 1572872 | tf_op jit(solution)/shard_map/ppermute | solution.py:447
  60.0 0.0 copy-done.3
  60.0 0.1 fusion.mute
  60.2 0.0 slice-done
  60.2 0.0 slice-done.1
  60.2 0.0 copy-done.2
  60.2 1.4 %image_mid.1.part = f32[9,4,64,256]{3,2,1,0:T(8,128)S(1)} custom-call(f32[9,8,64,256]{3,2,1,0:T(8,128)S(1)} %bitcast.16, s32[9]{0:T(128)S(1)} %copy-done.2, f32[8,64,256]{2,1,0:T(8,128)S(1)} %fusion.mute, f32[2,4,64,256]{3,2,1,0:T(8,128)S(1)} %finish.5.half.out.prev_out.out2, f32[2,4,64,256]{3,2,1,0:T(8,128)S(1)} %inner.5.other.inn.prev_inn.in2, ...), custom_call_target="tpu_custom_call" | custom-call | flops 1 | bytes 1 | tf_op jit(solution)/shard_map/image_mid/pallas_call | solution.py:332
  61.6 0.0 collective-permute-done.8.hal4
  61.6 3.1 %image_main.1 = (f32[9,8,64,256]{3,2,1,0:T(8,128)}, f32[8,64,256]{2,1,0:T(8,128)}, f32[8,64,256]{2,1,0:T(8,128)}, s32[9,128]{1,0:T(8,128)S(1)}) custom-call(f32[9,8,64,256]{3,2,1,0:T(8,128)S(1)} %bitcast.17, f32[9,4,64,256]{3,2,1,0:T(8,128)S(1)} %image_mid.1.part, s32[9]{0:T(128)S(1)} %copy-done.2, f32[8,64,256]{2,1,0:T(8,128)S(1)} %fusion.mute, ...), custom_call_target="tpu_custom_call" | custom-call | flops 1 | bytes 1 | tf_op jit(solution)/shard_map/image_main/pallas_call | solution.py:393
  64.8 2.3 %collective-permute-done.9.halo = f32[2,4,64,256]{3,2,1,0:T(8,128)S(1)} collective-permute-done((f32[2,4,64,256]{3,2,1,0:T(8,128)S(1)}, f32[2,4,64,256]{3,2,1,0:T(8,128)S(1)}, u32[]{:S(2)}, u32[]{:S(2)}) %collective-permute-start.9) | collective-permute-done | bytes 524320 | tf_op jit(solution)/shard_map/ppermute | solution.py:447
  67.1 1.3 %image_last.1 = f32[9,8,64,256]{3,2,1,0:T(8,128)} custom-call(f32[9,8,64,256]{3,2,1,0:T(8,128)} %get-tuple-element.15.image_old, f32[9,4,64,256]{3,2,1,0:T(8,128)S(1)} %image_mid.1.part, s32[9,128]{1,0:T(8,128)S(1)} %get-tuple-element.16.table, f32[8,64,256]{2,1,0:T(8,128)S(1)} %fusion.mute, ...), custom_call_target="tpu_custom_call", output_to_operand_aliasing={{}: (0, {})} | custom-call | flops 1 | bytes 1 | tf_op jit(solution)/shard_map/image_last/pallas_call | solution.py:428
  (1 shorter events, 0.0 us)
Async XLA Ops:
  1.8 5.9 %copy-start = (bf16[2,256,256]{2,1,0:T(8,128)(2,1)S(1)}, bf16[2,256,256]{2,1,0:T(8,128)(2,1)}, u32[]{:S(2)}) copy-start(bf16[2,256,256]{2,1,0:T(8,128)(2,1)} %constant.4.clone.wz) | copy-start | bytes 786436
  1.8 5.9 %copy-start.1 = (bf16[256,256]{1,0:T(8,128)(2,1)S(1)}, bf16[256,256]{1,0:T(8,128)(2,1)}, u32[]{:S(2)}) copy-start(bf16[256,256]{1,0:T(8,128)(2,1)} %constant.5.clone.wy) | copy-start | bytes 393220
  1.8 16.4 %collective-permute-start = (f32[2,4,64,256]{3,2,1,0:T(8,128)S(1)}, f32[2,4,64,256]{3,2,1,0:T(8,128)S(1)}, u32[]{:S(2)}, u32[]{:S(2)}) collective-permute-start(f32[2,4,64,256]{3,2,1,0:T(8,128)S(1)} %gather.2.out.prev_out), channel_id=1, source_target_pairs={{1,2},{3,4},{5,6},{7,8},{9,10},{11,12},{13,14},{2,1},{4,3},{6,5},{... | collective-permute-start | bytes 1572872 | tf_op jit(solution)/shard_map/ppermute | solution.py:447
  7.6 2.7 %collective-permute-start.2 = (f32[2,4,64,256]{3,2,1,0:T(8,128)S(1)}, f32[2,4,64,256]{3,2,1,0:T(8,128)S(1)}, u32[]{:S(2)}, u32[]{:S(2)}) collective-permute-start(f32[2,4,64,256]{3,2,1,0:T(8,128)S(1)} %gather.3.inn.prev_inn), channel_id=1, source_target_pairs={{0,1},{1,0},{2,3},{3,2},{4,5},{5,4},{6,7},{7,6},{8,9},{9,8},{10,11... | collective-permute-start | bytes 1572872 | tf_op jit(solution)/shard_map/ppermute | solution.py:451
  11.3 12.6 %collective-permute-start.3 = (f32[2,4,64,256]{3,2,1,0:T(8,128)S(1)}, f32[2,4,64,256]{3,2,1,0:T(8,128)S(1)}, u32[]{:S(2)}, u32[]{:S(2)}) collective-permute-start(f32[2,4,64,256]{3,2,1,0:T(8,128)S(1)} %inner.4.inn.prev_inn), channel_id=1, source_target_pairs={{0,1},{1,0},{2,3},{3,2},{4,5},{5,4},{6,7},{7,6},{8,9},{9,8},{10,11... | collective-permute-start | bytes 1572872 | tf_op jit(solution)/shard_map/ppermute | solution.py:451
  18.7 12.4 %collective-permute-start.1 = (f32[2,4,64,256]{3,2,1,0:T(8,128)S(1)}, f32[2,4,64,256]{3,2,1,0:T(8,128)S(1)}, u32[]{:S(2)}, u32[]{:S(2)}) collective-permute-start(f32[2,4,64,256]{3,2,1,0:T(8,128)S(1)} %finish.4.out.prev_out), channel_id=1, source_target_pairs={{1,2},{3,4},{5,6},{7,8},{9,10},{11,12},{13,14},{2,1},{4,3},{6,5},{... | collective-permute-start | bytes 1572872 | tf_op jit(solution)/shard_map/ppermute | solution.py:447
  24.9 12.1 %collective-permute-start.5 = (f32[2,4,64,256]{3,2,1,0:T(8,128)S(1)}, f32[2,4,64,256]{3,2,1,0:T(8,128)S(1)}, u32[]{:S(2)}, u32[]{:S(2)}) collective-permute-start(f32[2,4,64,256]{3,2,1,0:T(8,128)S(1)} %inner.5.other.inn.prev_inn.in2), channel_id=1, source_target_pairs={{0,1},{1,0},{2,3},{3,2},{4,5},{5,4},{6,7},{7,6},{8,9},{9,8},{10,11... | collective-permute-start | bytes 1572872 | tf_op jit(solution)/shard_map/ppermute | solution.py:451
  31.5 11.5 %collective-permute-start.4 = (f32[2,4,64,256]{3,2,1,0:T(8,128)S(1)}, f32[2,4,64,256]{3,2,1,0:T(8,128)S(1)}, u32[]{:S(2)}, u32[]{:S(2)}) collective-permute-start(f32[2,4,64,256]{3,2,1,0:T(8,128)S(1)} %finish.5.half.out.prev_out.out2), channel_id=1, source_target_pairs={{1,2},{3,4},{5,6},{7,8},{9,10},{11,12},{13,14},{2,1},{4,3},{6,5},{... | collective-permute-start | bytes 1572872 | tf_op jit(solution)/shard_map/ppermute | solution.py:447
  37.0 23.2 %slice-start = ((s8[4718592]{0:T(1024)(128)(4,1)}), s8[4194304]{0:T(1024)(128)(4,1)S(1)}, s32[]{:S(2)}) async-start(s8[4718592]{0:T(1024)(128)(4,1)} %bitcast.14), calls=%async_computation | async-start | bytes 8388608
  38.2 10.8 %collective-permute-start.6 = (f32[2,4,64,256]{3,2,1,0:T(8,128)S(1)}, f32[2,4,64,256]{3,2,1,0:T(8,128)S(1)}, u32[]{:S(2)}, u32[]{:S(2)}) collective-permute-start(f32[2,4,64,256]{3,2,1,0:T(8,128)S(1)} %inner.6.inn), channel_id=1, source_target_pairs={{0,1},{1,0},{2,3},{3,2},{4,5},{5,4},{6,7},{7,6},{8,9},{9,8},{10,11... | collective-permute-start | bytes 1572872 | tf_op jit(solution)/shard_map/ppermute | solution.py:451
  43.5 16.5 %copy-start.3 = (s32[1,8,64]{2,1,0:T(8,128)S(1)}, s32[1,8,64]{2,1,0:T(8,128)}, u32[]{:S(2)}) copy-start(s32[1,8,64]{2,1,0:T(8,128)} %param.19) | copy-start | bytes 6148
  43.5 16.7 %slice-start.1 = ((s8[4718592]{0:T(1024)(128)(4,1)}), s8[524288]{0:T(1024)(128)(4,1)S(1)}, s32[]{:S(2)}) async-start(s8[4718592]{0:T(1024)(128)(4,1)} %bitcast.14), calls=%async_computation.1 | async-start | bytes 1048576
  43.5 16.7 %copy-start.2 = (s32[9]{0:T(128)S(1)}, s32[9]{0:T(128)}, u32[]{:S(2)}) copy-start(s32[9]{0:T(128)} %offsets.3) | copy-start | bytes 112
  43.5 11.6 %collective-permute-start.7 = (f32[2,4,64,256]{3,2,1,0:T(8,128)S(1)}, f32[2,4,64,256]{3,2,1,0:T(8,128)S(1)}, u32[]{:S(2)}, u32[]{:S(2)}) collective-permute-start(f32[2,4,64,256]{3,2,1,0:T(8,128)S(1)} %finish.6.out), channel_id=1, source_target_pairs={{1,2},{3,4},{5,6},{7,8},{9,10},{11,12},{13,14},{2,1},{4,3},{6,5},{... | collective-permute-start | bytes 1572872 | tf_op jit(solution)/shard_map/ppermute | solution.py:447
  50.0 11.7 %collective-permute-start.8 = (f32[2,4,64,256]{3,2,1,0:T(8,128)S(1)}, f32[2,4,64,256]{3,2,1,0:T(8,128)S(1)}, u32[]{:S(2)}, u32[]{:S(2)}) collective-permute-start(f32[2,4,64,256]{3,2,1,0:T(8,128)S(1)} %inner.7.in4.other), channel_id=1, source_target_pairs={{0,1},{1,0},{2,3},{3,2},{4,5},{5,4},{6,7},{7,6},{8,9},{9,8},{10,11... | collective-permute-start | bytes 1572872 | tf_op jit(solution)/shard_map/ppermute | solution.py:451
  55.6 11.5 %collective-permute-start.9 = (f32[2,4,64,256]{3,2,1,0:T(8,128)S(1)}, f32[2,4,64,256]{3,2,1,0:T(8,128)S(1)}, u32[]{:S(2)}, u32[]{:S(2)}) collective-permute-start(f32[2,4,64,256]{3,2,1,0:T(8,128)S(1)} %finish.7.out4.half), channel_id=1, source_target_pairs={{1,2},{3,4},{5,6},{7,8},{9,10},{11,12},{13,14},{2,1},{4,3},{6,5},{... | collective-permute-start | bytes 1572872 | tf_op jit(solution)/shard_map/ppermute | solution.py:447

commit v6 on v5

--- a/solution.py
+++ b/solution.py
@@ -233,26 +233,29 @@
     )(*operands)
 
 
-def finish_kernel(halo, base, coef, wz, out, hi, lo):
+def finish_kernel(halo, base, coef, wz, out, hi, lo, dz):
     rows = halo.shape[2]
     sign = (1 - 2 * is_flipped(False)).astype(jnp.float32)
-    wx = [sign * w for w in mixed_w]
+    wx = [sign * w / SCALE for w in mixed_w]
     for f in range(2):
         for j in range(4):
             at_row = pl.ds((f * 4 + j) * rows, rows)
             hi[at_row], lo[at_row] = split(halo[f, j])
-    for f in range(2):
-        part = pl.ds(f * 4 * rows, 4 * rows)
-        dz = dot(hi[part], wz[1]) + dot(lo[part], wz[1])
-        for m in range(4):
-            hx = zx = None
-            for k in range(m + 1, 5):
-                j = k - m - 1
-                t = float(second_int[k]) * halo[f, j]
-                hx = t if hx is None else hx + t
-                t = wx[k - 1] * dz[j * rows : (j + 1) * rows]
-                zx = t if zx is None else zx + t
-            out[f, m] = base[f, m] + (1.0 / SCALE) * (coef[0, m] * hx - coef[2, m] * zx)
+    dz[...] = dot(hi[...], wz[1]) + dot(lo[...], wz[1])
+
+    for r in range(0, rows, CHUNK):
+        span = pl.ds(r, CHUNK)
+        for f in range(2):
+            h = [halo[f, j, span] for j in range(4)]
+            z = [dz[pl.ds((f * 4 + j) * rows + r, CHUNK)] for j in range(4)]
+            for m in range(4):
+                hx = zx = None
+                for k in range(m + 1, 5):
+                    t = second_w[k] * h[k - m - 1]
+                    hx = t if hx is None else hx + t
+                    t = wx[k - 1] * z[k - m - 1]
+                    zx = t if zx is None else zx + t
+                out[f, m, span] = base[f, m, span] + (coef[0, m, span] * hx - coef[2, m, span] * zx)
 
 
 def finish(halo, base, coef, wz):
@@ -262,7 +265,8 @@
         out_shape=jax.ShapeDtypeStruct(halo.shape, jnp.float32),
         in_specs=[VMEM] * 4,
         out_specs=VMEM,
-        scratch_shapes=[pltpu.VMEM((8 * rows, depth), jnp.bfloat16)] * 2,
+        scratch_shapes=[pltpu.VMEM((8 * rows, depth), jnp.bfloat16)] * 2
+        + [pltpu.VMEM((8 * rows, depth), jnp.float32)],
         cost_estimate=CHEAP,
         compiler_params=pltpu.CompilerParams(vmem_limit_bytes=8 * MIB),
         name="finish",

time: 68.8 us -> 68.6 us (level)
  no operation moved by 1% of the time
where the time goes in v6:
time: 68.6 us; the launch traced here: 68.2 us
  waiting for transfers between devices  24.7 us (36%)
  starting transfers between devices  23.2 us (34%)
  Pallas kernels  19.2 us (28%)
  between operations  0.96 us (1%)
    ppermute x5, waiting for transfers between devices, across_chips(): return lax.ppermute(value, 'blk', pairs + [(b, a) for a, b in pairs])  24.7 us
    ppermute x5, starting transfers between devices, across_chips(): return lax.ppermute(value, 'blk', pairs + [(b, a) for a, b in pairs])  22.4 us
    pallas_call x7, Pallas kernels, half_step(): pl.pallas_call(kernel, out_shape=jax.ShapeDtypeStruct(shape, jnp.float32)...  6.92 us
    pallas_call x1, Pallas kernels, image_main(): pl.pallas_call(image_main_kernel, out_shape=[jax.ShapeDtypeStruct(image_i...  3.14 us
    pallas_call x1, Pallas kernels, first(): pl.pallas_call(first_kernel, out_shape=[pair, three, three, pair], in_spe...  2.57 us
    pallas_call x2, Pallas kernels, gather(): pl.pallas_call(functools.partial(gather_kernel, plan, len(arrays)), out_s...  2.28 us
    pallas_call x4, Pallas kernels, finish(): pl.pallas_call(finish_kernel, out_shape=jax.ShapeDtypeStruct(halo.shape,...  1.56 us
    pallas_call x1, Pallas kernels, image_mid(): pl.pallas_call(image_mid_kernel, out_shape=jax.ShapeDtypeStruct(shape, jn...  1.42 us
  transfers between devices with their start and end apart: 10, of which 5 were waited for; matrix products, arithmetic and copies ran while one was open for 0% of the time, Pallas kernels for 25%

profile of v6, /device:TPU:1, one launch (start us, length us, event | category | flops | bytes accessed | tf_op | source)
XLA Modules:
  0.0 68.2 jit_solution(9762452666478117427)
XLA Ops:
  0.6 1.1 %gather.2.out.prev_out = f32[2,4,64,256]{3,2,1,0:T(8,128)S(1)} custom-call(f32[8,64,256]{2,1,0:T(8,128)} %bitcast.20, f32[8,64,256]{2,1,0:T(8,128)} %bitcast.22), custom_call_target="tpu_custom_call" | custom-call | flops 10000000000 | bytes 20000000 | tf_op jit(solution)/shard_map/gather/pallas_call | solution.py:94
  1.8 0.0 copy-start
  1.8 0.0 copy-start.1
  1.8 4.7 %collective-permute-start = (f32[2,4,64,256]{3,2,1,0:T(8,128)S(1)}, f32[2,4,64,256]{3,2,1,0:T(8,128)S(1)}, u32[]{:S(2)}, u32[]{:S(2)}) collective-permute-start(f32[2,4,64,256]{3,2,1,0:T(8,128)S(1)} %gather.2.out.prev_out), channel_id=1, source_target_pairs={{1,2},{3,4},{5,6},{7,8},{9,10},{11,12},{13,14},{2,1},{4,3},{6,5},{... | collective-permute-start | bytes 1572872 | tf_op jit(solution)/shard_map/ppermute | solution.py:451
  6.5 1.1 %gather.3.inn.prev_inn = f32[2,4,64,256]{3,2,1,0:T(8,128)S(1)} custom-call(f32[8,64,256]{2,1,0:T(8,128)} %bitcast.21, f32[8,64,256]{2,1,0:T(8,128)} %bitcast.23), custom_call_target="tpu_custom_call" | custom-call | flops 10000000000 | bytes 20000000 | tf_op jit(solution)/shard_map/gather/pallas_call | solution.py:94
  7.6 0.1 collective-permute-start.2
  7.7 0.0 copy-done
  7.7 0.0 copy-done.1
  7.7 2.6 %first.1 = (f32[2,4,64,256]{3,2,1,0:T(8,128)S(1)}, f32[3,4,64,256]{3,2,1,0:T(8,128)S(1)}, f32[3,4,64,256]{3,2,1,0:T(8,128)S(1)}, f32[2,4,64,256]{3,2,1,0:T(8,128)S(1)}) custom-call(f32[2,4,64,256]{3,2,1,0:T(8,128)S(1)} %gather.2.out.prev_out, f32[2,4,64,256]{3,2,1,0:T(8,128)S(1)} %gather.3.inn.prev_inn, bf16[2,256,256]{2,1,0:T(8,128)(2,1)S(1)} %copy-done, ...), custom_call_target="tpu_custom_call" | custom-call | flops 10000000000 | bytes 20000000 | tf_op jit(solution)/shard_map/first/pallas_call | solution.py:210
  10.3 0.0 collective-permute-done.2.near
  10.3 1.0 %inner.4.inn.prev_inn = f32[2,4,64,256]{3,2,1,0:T(8,128)S(1)} custom-call(f32[2,4,64,256]{3,2,1,0:T(8,128)S(1)} %gather.3.inn.prev_inn, f32[2,4,64,256]{3,2,1,0:T(8,128)S(1)} %gather.2.out.prev_out, f32[2,4,64,256]{3,2,1,0:T(8,128)S(1)} %collective-permute-done.2.near, f32[2,4,64,256]{3,2,1,0:T(8,128)S(1)} %get-tuple-element.13.prev_inn, ...), custom_call_target="tpu_custom_call" | custom-call | flops 1 | bytes 1 | tf_op jit(solution)/shard_map/inner/pallas_call | solution.py:224
  11.3 0.5 collective-permute-start.3
  11.8 6.4 %collective-permute-done.halo = f32[2,4,64,256]{3,2,1,0:T(8,128)S(1)} collective-permute-done((f32[2,4,64,256]{3,2,1,0:T(8,128)S(1)}, f32[2,4,64,256]{3,2,1,0:T(8,128)S(1)}, u32[]{:S(2)}, u32[]{:S(2)}) %collective-permute-start) | collective-permute-done | bytes 524320 | tf_op jit(solution)/shard_map/ppermute | solution.py:451
  18.2 0.4 finish.4.out.prev_out
  18.6 4.4 %collective-permute-start.1 = (f32[2,4,64,256]{3,2,1,0:T(8,128)S(1)}, f32[2,4,64,256]{3,2,1,0:T(8,128)S(1)}, u32[]{:S(2)}, u32[]{:S(2)}) collective-permute-start(f32[2,4,64,256]{3,2,1,0:T(8,128)S(1)} %finish.4.out.prev_out), channel_id=1, source_target_pairs={{1,2},{3,4},{5,6},{7,8},{9,10},{11,12},{13,14},{2,1},{4,3},{6,5},{... | collective-permute-start | bytes 1572872 | tf_op jit(solution)/shard_map/ppermute | solution.py:451
  23.0 0.8 %base.3 = f32[2,4,64,256]{3,2,1,0:T(8,128)S(1)} custom-call(f32[2,4,64,256]{3,2,1,0:T(8,128)S(1)} %finish.4.out.prev_out, f32[2,4,64,256]{3,2,1,0:T(8,128)S(1)} %inner.4.inn.prev_inn, f32[2,4,64,256]{3,2,1,0:T(8,128)S(1)} %gather.2.out.prev_out, f32[3,4,64,256]{3,2,1,0:T(8,128)S(1)} %get-tuple-element.12.coef.coef_out, bf16[2,256,256]{2,1,0:T(8,128)(2,1)S(1)} %copy-done, ...), custom_call_target="tpu_custom_call" | custom-call | flops 1 | bytes 1 | tf_op jit(solution)/shard_map/base/pallas_call | solution.py:224
  23.8 0.0 collective-permute-done.3.near
  23.9 1.0 %inner.5.other.inn.prev_inn.in2 = f32[2,4,64,256]{3,2,1,0:T(8,128)S(1)} custom-call(f32[2,4,64,256]{3,2,1,0:T(8,128)S(1)} %inner.4.inn.prev_inn, f32[2,4,64,256]{3,2,1,0:T(8,128)S(1)} %finish.4.out.prev_out, f32[2,4,64,256]{3,2,1,0:T(8,128)S(1)} %collective-permute-done.3.near, f32[2,4,64,256]{3,2,1,0:T(8,128)S(1)} %gather.3.inn.prev_inn, ...), custom_call_target="tpu_custom_call" | custom-call | flops 1 | bytes 1 | tf_op jit(solution)/shard_map/inner/pallas_call | solution.py:224
  24.8 0.1 collective-permute-start.5
  24.9 6.1 %collective-permute-done.1.halo = f32[2,4,64,256]{3,2,1,0:T(8,128)S(1)} collective-permute-done((f32[2,4,64,256]{3,2,1,0:T(8,128)S(1)}, f32[2,4,64,256]{3,2,1,0:T(8,128)S(1)}, u32[]{:S(2)}, u32[]{:S(2)}) %collective-permute-start.1) | collective-permute-done | bytes 524320 | tf_op jit(solution)/shard_map/ppermute | solution.py:451
  31.0 0.4 finish.5.half.out.prev_out.out2
  31.4 4.4 %collective-permute-start.4 = (f32[2,4,64,256]{3,2,1,0:T(8,128)S(1)}, f32[2,4,64,256]{3,2,1,0:T(8,128)S(1)}, u32[]{:S(2)}, u32[]{:S(2)}) collective-permute-start(f32[2,4,64,256]{3,2,1,0:T(8,128)S(1)} %finish.5.half.out.prev_out.out2), channel_id=1, source_target_pairs={{1,2},{3,4},{5,6},{7,8},{9,10},{11,12},{13,14},{2,1},{4,3},{6,5},{... | collective-permute-start | bytes 1572872 | tf_op jit(solution)/shard_map/ppermute | solution.py:451
  35.8 1.0 %base.4 = f32[2,4,64,256]{3,2,1,0:T(8,128)S(1)} custom-call(f32[2,4,64,256]{3,2,1,0:T(8,128)S(1)} %finish.5.half.out.prev_out.out2, f32[2,4,64,256]{3,2,1,0:T(8,128)S(1)} %inner.5.other.inn.prev_inn.in2, f32[2,4,64,256]{3,2,1,0:T(8,128)S(1)} %finish.4.out.prev_out, f32[3,4,64,256]{3,2,1,0:T(8,128)S(1)} %get-tuple-element.12.coef.coef_out, ...), custom_call_target="tpu_custom_call" | custom-call | flops 1 | bytes 1 | tf_op jit(solution)/shard_map/base/pallas_call | solution.py:224
  36.8 0.0 collective-permute-done.5.near.hal2
  36.8 0.0 slice-start
  36.9 1.2 %inner.6.inn = f32[2,4,64,256]{3,2,1,0:T(8,128)S(1)} custom-call(f32[2,4,64,256]{3,2,1,0:T(8,128)S(1)} %inner.5.other.inn.prev_inn.in2, f32[2,4,64,256]{3,2,1,0:T(8,128)S(1)} %finish.5.half.out.prev_out.out2, f32[2,4,64,256]{3,2,1,0:T(8,128)S(1)} %collective-permute-done.5.near.hal2, f32[2,4,64,256]{3,2,1,0:T(8,128)S(1)} %inner.4.inn.prev_inn, ...), custom_call_target="tpu_custom_call" | custom-call | flops 1 | bytes 1 | tf_op jit(solution)/shard_map/inner/pallas_call | solution.py:224
  38.1 0.1 collective-permute-start.6
  38.1 4.8 %collective-permute-done.4.halo = f32[2,4,64,256]{3,2,1,0:T(8,128)S(1)} collective-permute-done((f32[2,4,64,256]{3,2,1,0:T(8,128)S(1)}, f32[2,4,64,256]{3,2,1,0:T(8,128)S(1)}, u32[]{:S(2)}, u32[]{:S(2)}) %collective-permute-start.4) | collective-permute-done | bytes 524320 | tf_op jit(solution)/shard_map/ppermute | solution.py:451
  42.9 0.4 finish.6.out
  43.3 0.0 copy-start.3
  43.3 0.0 slice-start.1
  43.4 0.0 copy-start.2
  43.4 4.5 %collective-permute-start.7 = (f32[2,4,64,256]{3,2,1,0:T(8,128)S(1)}, f32[2,4,64,256]{3,2,1,0:T(8,128)S(1)}, u32[]{:S(2)}, u32[]{:S(2)}) collective-permute-start(f32[2,4,64,256]{3,2,1,0:T(8,128)S(1)} %finish.6.out), channel_id=1, source_target_pairs={{1,2},{3,4},{5,6},{7,8},{9,10},{11,12},{13,14},{2,1},{4,3},{6,5},{... | collective-permute-start | bytes 1572872 | tf_op jit(solution)/shard_map/ppermute | solution.py:451
  47.9 0.9 %base.5 = f32[2,4,64,256]{3,2,1,0:T(8,128)S(1)} custom-call(f32[2,4,64,256]{3,2,1,0:T(8,128)S(1)} %finish.6.out, f32[2,4,64,256]{3,2,1,0:T(8,128)S(1)} %inner.6.inn, f32[2,4,64,256]{3,2,1,0:T(8,128)S(1)} %finish.5.half.out.prev_out.out2, f32[3,4,64,256]{3,2,1,0:T(8,128)S(1)} %get-tuple-element.12.coef.coef_out, bf16[2,256,256]{2,1,0:T(8,128)(2,1)S(1)} %copy-done, ...), custom_call_target="tpu_custom_call" | custom-call | flops 1 | bytes 1 | tf_op jit(solution)/shard_map/base/pallas_call | solution.py:224
  48.8 0.0 collective-permute-done.6.near
  48.8 1.0 %inner.7.in4.other = f32[2,4,64,256]{3,2,1,0:T(8,128)S(1)} custom-call(f32[2,4,64,256]{3,2,1,0:T(8,128)S(1)} %inner.6.inn, f32[2,4,64,256]{3,2,1,0:T(8,128)S(1)} %finish.6.out, f32[2,4,64,256]{3,2,1,0:T(8,128)S(1)} %collective-permute-done.6.near, f32[2,4,64,256]{3,2,1,0:T(8,128)S(1)} %inner.5.other.inn.prev_inn.in2, ...), custom_call_target="tpu_custom_call" | custom-call | flops 1 | bytes 1 | tf_op jit(solution)/shard_map/inner/pallas_call | solution.py:224
  49.8 0.1 collective-permute-start.8
  49.9 5.1 %collective-permute-done.7.halo = f32[2,4,64,256]{3,2,1,0:T(8,128)S(1)} collective-permute-done((f32[2,4,64,256]{3,2,1,0:T(8,128)S(1)}, f32[2,4,64,256]{3,2,1,0:T(8,128)S(1)}, u32[]{:S(2)}, u32[]{:S(2)}) %collective-permute-start.7) | collective-permute-done | bytes 524320 | tf_op jit(solution)/shard_map/ppermute | solution.py:451
  55.0 0.4 finish.7.out4.half
  55.4 4.4 %collective-permute-start.9 = (f32[2,4,64,256]{3,2,1,0:T(8,128)S(1)}, f32[2,4,64,256]{3,2,1,0:T(8,128)S(1)}, u32[]{:S(2)}, u32[]{:S(2)}) collective-permute-start(f32[2,4,64,256]{3,2,1,0:T(8,128)S(1)} %finish.7.out4.half), channel_id=1, source_target_pairs={{1,2},{3,4},{5,6},{7,8},{9,10},{11,12},{13,14},{2,1},{4,3},{6,5},{... | collective-permute-start | bytes 1572872 | tf_op jit(solution)/shard_map/ppermute | solution.py:451
  59.8 0.0 copy-done.3
  59.8 0.1 fusion.mute
  59.9 0.0 slice-done
  59.9 0.0 slice-done.1
  60.0 0.0 copy-done.2
  60.0 1.4 %image_mid.1.part = f32[9,4,64,256]{3,2,1,0:T(8,128)S(1)} custom-call(f32[9,8,64,256]{3,2,1,0:T(8,128)S(1)} %bitcast.16, s32[9]{0:T(128)S(1)} %copy-done.2, f32[8,64,256]{2,1,0:T(8,128)S(1)} %fusion.mute, f32[2,4,64,256]{3,2,1,0:T(8,128)S(1)} %finish.5.half.out.prev_out.out2, f32[2,4,64,256]{3,2,1,0:T(8,128)S(1)} %inner.5.other.inn.prev_inn.in2, ...), custom_call_target="tpu_custom_call" | custom-call | flops 1 | bytes 1 | tf_op jit(solution)/shard_map/image_mid/pallas_call | solution.py:336
  61.4 0.0 collective-permute-done.8.hal4
  61.4 3.1 %image_main.1 = (f32[9,8,64,256]{3,2,1,0:T(8,128)}, f32[8,64,256]{2,1,0:T(8,128)}, f32[8,64,256]{2,1,0:T(8,128)}, s32[9,128]{1,0:T(8,128)S(1)}) custom-call(f32[9,8,64,256]{3,2,1,0:T(8,128)S(1)} %bitcast.17, f32[9,4,64,256]{3,2,1,0:T(8,128)S(1)} %image_mid.1.part, s32[9]{0:T(128)S(1)} %copy-done.2, f32[8,64,256]{2,1,0:T(8,128)S(1)} %fusion.mute, ...), custom_call_target="tpu_custom_call" | custom-call | flops 1 | bytes 1 | tf_op jit(solution)/shard_map/image_main/pallas_call | solution.py:397
  64.6 2.3 %collective-permute-done.9.halo = f32[2,4,64,256]{3,2,1,0:T(8,128)S(1)} collective-permute-done((f32[2,4,64,256]{3,2,1,0:T(8,128)S(1)}, f32[2,4,64,256]{3,2,1,0:T(8,128)S(1)}, u32[]{:S(2)}, u32[]{:S(2)}) %collective-permute-start.9) | collective-permute-done | bytes 524320 | tf_op jit(solution)/shard_map/ppermute | solution.py:451
  66.9 1.3 %image_last.1 = f32[9,8,64,256]{3,2,1,0:T(8,128)} custom-call(f32[9,8,64,256]{3,2,1,0:T(8,128)} %get-tuple-element.15.image_old, f32[9,4,64,256]{3,2,1,0:T(8,128)S(1)} %image_mid.1.part, s32[9,128]{1,0:T(8,128)S(1)} %get-tuple-element.16.table, f32[8,64,256]{2,1,0:T(8,128)S(1)} %fusion.mute, ...), custom_call_target="tpu_custom_call", output_to_operand_aliasing={{}: (0, {})} | custom-call | flops 1 | bytes 1 | tf_op jit(solution)/shard_map/image_last/pallas_call | solution.py:432
  (1 shorter events, 0.0 us)
Async XLA Ops:
  1.8 5.9 %copy-start = (bf16[2,256,256]{2,1,0:T(8,128)(2,1)S(1)}, bf16[2,256,256]{2,1,0:T(8,128)(2,1)}, u32[]{:S(2)}) copy-start(bf16[2,256,256]{2,1,0:T(8,128)(2,1)} %constant.4.clone.wz) | copy-start | bytes 786436
  1.8 5.9 %copy-start.1 = (bf16[256,256]{1,0:T(8,128)(2,1)S(1)}, bf16[256,256]{1,0:T(8,128)(2,1)}, u32[]{:S(2)}) copy-start(bf16[256,256]{1,0:T(8,128)(2,1)} %constant.5.clone.wy) | copy-start | bytes 393220
  1.8 16.4 %collective-permute-start = (f32[2,4,64,256]{3,2,1,0:T(8,128)S(1)}, f32[2,4,64,256]{3,2,1,0:T(8,128)S(1)}, u32[]{:S(2)}, u32[]{:S(2)}) collective-permute-start(f32[2,4,64,256]{3,2,1,0:T(8,128)S(1)} %gather.2.out.prev_out), channel_id=1, source_target_pairs={{1,2},{3,4},{5,6},{7,8},{9,10},{11,12},{13,14},{2,1},{4,3},{6,5},{... | collective-permute-start | bytes 1572872 | tf_op jit(solution)/shard_map/ppermute | solution.py:451
  7.6 2.7 %collective-permute-start.2 = (f32[2,4,64,256]{3,2,1,0:T(8,128)S(1)}, f32[2,4,64,256]{3,2,1,0:T(8,128)S(1)}, u32[]{:S(2)}, u32[]{:S(2)}) collective-permute-start(f32[2,4,64,256]{3,2,1,0:T(8,128)S(1)} %gather.3.inn.prev_inn), channel_id=1, source_target_pairs={{0,1},{1,0},{2,3},{3,2},{4,5},{5,4},{6,7},{7,6},{8,9},{9,8},{10,11... | collective-permute-start | bytes 1572872 | tf_op jit(solution)/shard_map/ppermute | solution.py:455
  11.3 12.5 %collective-permute-start.3 = (f32[2,4,64,256]{3,2,1,0:T(8,128)S(1)}, f32[2,4,64,256]{3,2,1,0:T(8,128)S(1)}, u32[]{:S(2)}, u32[]{:S(2)}) collective-permute-start(f32[2,4,64,256]{3,2,1,0:T(8,128)S(1)} %inner.4.inn.prev_inn), channel_id=1, source_target_pairs={{0,1},{1,0},{2,3},{3,2},{4,5},{5,4},{6,7},{7,6},{8,9},{9,8},{10,11... | collective-permute-start | bytes 1572872 | tf_op jit(solution)/shard_map/ppermute | solution.py:455
  18.6 12.4 %collective-permute-start.1 = (f32[2,4,64,256]{3,2,1,0:T(8,128)S(1)}, f32[2,4,64,256]{3,2,1,0:T(8,128)S(1)}, u32[]{:S(2)}, u32[]{:S(2)}) collective-permute-start(f32[2,4,64,256]{3,2,1,0:T(8,128)S(1)} %finish.4.out.prev_out), channel_id=1, source_target_pairs={{1,2},{3,4},{5,6},{7,8},{9,10},{11,12},{13,14},{2,1},{4,3},{6,5},{... | collective-permute-start | bytes 1572872 | tf_op jit(solution)/shard_map/ppermute | solution.py:451
  24.8 12.0 %collective-permute-start.5 = (f32[2,4,64,256]{3,2,1,0:T(8,128)S(1)}, f32[2,4,64,256]{3,2,1,0:T(8,128)S(1)}, u32[]{:S(2)}, u32[]{:S(2)}) collective-permute-start(f32[2,4,64,256]{3,2,1,0:T(8,128)S(1)} %inner.5.other.inn.prev_inn.in2), channel_id=1, source_target_pairs={{0,1},{1,0},{2,3},{3,2},{4,5},{5,4},{6,7},{7,6},{8,9},{9,8},{10,11... | collective-permute-start | bytes 1572872 | tf_op jit(solution)/shard_map/ppermute | solution.py:455
  31.4 11.5 %collective-permute-start.4 = (f32[2,4,64,256]{3,2,1,0:T(8,128)S(1)}, f32[2,4,64,256]{3,2,1,0:T(8,128)S(1)}, u32[]{:S(2)}, u32[]{:S(2)}) collective-permute-start(f32[2,4,64,256]{3,2,1,0:T(8,128)S(1)} %finish.5.half.out.prev_out.out2), channel_id=1, source_target_pairs={{1,2},{3,4},{5,6},{7,8},{9,10},{11,12},{13,14},{2,1},{4,3},{6,5},{... | collective-permute-start | bytes 1572872 | tf_op jit(solution)/shard_map/ppermute | solution.py:451
  36.8 23.1 %slice-start = ((s8[4718592]{0:T(1024)(128)(4,1)}), s8[4194304]{0:T(1024)(128)(4,1)S(1)}, s32[]{:S(2)}) async-start(s8[4718592]{0:T(1024)(128)(4,1)} %bitcast.14), calls=%async_computation | async-start | bytes 8388608
  38.1 10.7 %collective-permute-start.6 = (f32[2,4,64,256]{3,2,1,0:T(8,128)S(1)}, f32[2,4,64,256]{3,2,1,0:T(8,128)S(1)}, u32[]{:S(2)}, u32[]{:S(2)}) collective-permute-start(f32[2,4,64,256]{3,2,1,0:T(8,128)S(1)} %inner.6.inn), channel_id=1, source_target_pairs={{0,1},{1,0},{2,3},{3,2},{4,5},{5,4},{6,7},{7,6},{8,9},{9,8},{10,11... | collective-permute-start | bytes 1572872 | tf_op jit(solution)/shard_map/ppermute | solution.py:455
  43.3 16.5 %copy-start.3 = (s32[1,8,64]{2,1,0:T(8,128)S(1)}, s32[1,8,64]{2,1,0:T(8,128)}, u32[]{:S(2)}) copy-start(s32[1,8,64]{2,1,0:T(8,128)} %param.19) | copy-start | bytes 6148
  43.3 16.6 %slice-start.1 = ((s8[4718592]{0:T(1024)(128)(4,1)}), s8[524288]{0:T(1024)(128)(4,1)S(1)}, s32[]{:S(2)}) async-start(s8[4718592]{0:T(1024)(128)(4,1)} %bitcast.14), calls=%async_computation.1 | async-start | bytes 1048576
  43.4 16.6 %copy-start.2 = (s32[9]{0:T(128)S(1)}, s32[9]{0:T(128)}, u32[]{:S(2)}) copy-start(s32[9]{0:T(128)} %offsets.3) | copy-start | bytes 112
  43.4 11.6 %collective-permute-start.7 = (f32[2,4,64,256]{3,2,1,0:T(8,128)S(1)}, f32[2,4,64,256]{3,2,1,0:T(8,128)S(1)}, u32[]{:S(2)}, u32[]{:S(2)}) collective-permute-start(f32[2,4,64,256]{3,2,1,0:T(8,128)S(1)} %finish.6.out), channel_id=1, source_target_pairs={{1,2},{3,4},{5,6},{7,8},{9,10},{11,12},{13,14},{2,1},{4,3},{6,5},{... | collective-permute-start | bytes 1572872 | tf_op jit(solution)/shard_map/ppermute | solution.py:451
  49.8 11.6 %collective-permute-start.8 = (f32[2,4,64,256]{3,2,1,0:T(8,128)S(1)}, f32[2,4,64,256]{3,2,1,0:T(8,128)S(1)}, u32[]{:S(2)}, u32[]{:S(2)}) collective-permute-start(f32[2,4,64,256]{3,2,1,0:T(8,128)S(1)} %inner.7.in4.other), channel_id=1, source_target_pairs={{0,1},{1,0},{2,3},{3,2},{4,5},{5,4},{6,7},{7,6},{8,9},{9,8},{10,11... | collective-permute-start | bytes 1572872 | tf_op jit(solution)/shard_map/ppermute | solution.py:455
  55.4 11.5 %collective-permute-start.9 = (f32[2,4,64,256]{3,2,1,0:T(8,128)S(1)}, f32[2,4,64,256]{3,2,1,0:T(8,128)S(1)}, u32[]{:S(2)}, u32[]{:S(2)}) collective-permute-start(f32[2,4,64,256]{3,2,1,0:T(8,128)S(1)} %finish.7.out4.half), channel_id=1, source_target_pairs={{1,2},{3,4},{5,6},{7,8},{9,10},{11,12},{13,14},{2,1},{4,3},{6,5},{... | collective-permute-start | bytes 1572872 | tf_op jit(solution)/shard_map/ppermute | solution.py:451

commit v7 on v6

--- a/solution.py
+++ b/solution.py
@@ -285,7 +285,7 @@
 BY_REACH = (-4, 4, -3, 3, -2, 2, -1, 1, 0)
 
 
-def add_terms(old, new, slots, planes, mute, snaps, inner):
+def add_terms(old, new, slots, planes, mute, snaps, inner, straight=False):
     flip = is_flipped(inner)
     rows = old.shape[2]
     chunk = CHUNK
@@ -293,7 +293,7 @@
         chunk *= 2
 
     def body(i, carry):
-        span = pl.ds(pl.multiple_of(i * chunk, chunk), chunk)
+        span = pl.ds(i * chunk if straight else pl.multiple_of(i * chunk, chunk), chunk)
         for m in planes:
             local = m + flip * (3 - 2 * m)
             mask = mute[natural(m, flip), span]
@@ -305,7 +305,11 @@
                 new[slot, local, span] = old[slot, local, span] + mask * total
         return carry
 
-    lax.fori_loop(0, rows // chunk, body, 0)
+    if straight:
+        for i in range(rows // chunk):
+            body(i, 0)
+    else:
+        lax.fori_loop(0, rows // chunk, body, 0)
 
 
 def store_planes(buffer, image, slot, first, count, inner, sem):
@@ -418,9 +422,10 @@
 def image_last_kernel(image_old, part, table, mute, half, other, halo, image, done, sem):
     del image_old
     stores = []
+    slot = {h: table[h + HMAX, 0] for h in range(-HMAX, HMAX + 1)}
     for reach in range(HMAX, 0, -1):
-        pair = {h: table[h + HMAX, 0] for h in (-reach, reach)}
-        add_terms(part, done, pair, range(reach), mute, [(half, other, halo)], False)
+        pair = {h: slot[h] for h in (-reach, reach)}
+        add_terms(part, done, pair, range(reach), mute, [(half, other, halo)], False, True)
         for k in pair.values():
             stores.append(store_planes(done, image, k, 0, reach, False, sem.at[len(stores)]))
             stores[-1].start()

time: 68.6 us -> 68.5 us (level)
  no operation moved by 1% of the time
where the time goes in v7:
time: 68.5 us; the launch traced here: 68.1 us
  waiting for transfers between devices  24.7 us (36%)
  starting transfers between devices  23.2 us (34%)
  Pallas kernels  19.1 us (28%)
  between operations  0.96 us (1%)
    ppermute x5, waiting for transfers between devices, across_chips(): return lax.ppermute(value, 'blk', pairs + [(b, a) for a, b in pairs])  24.7 us
    ppermute x5, starting transfers between devices, across_chips(): return lax.ppermute(value, 'blk', pairs + [(b, a) for a, b in pairs])  22.4 us
    pallas_call x7, Pallas kernels, half_step(): pl.pallas_call(kernel, out_shape=jax.ShapeDtypeStruct(shape, jnp.float32)...  6.92 us
    pallas_call x1, Pallas kernels, image_main(): pl.pallas_call(image_main_kernel, out_shape=[jax.ShapeDtypeStruct(image_i...  3.14 us
    pallas_call x1, Pallas kernels, first(): pl.pallas_call(first_kernel, out_shape=[pair, three, three, pair], in_spe...  2.57 us
    pallas_call x2, Pallas kernels, gather(): pl.pallas_call(functools.partial(gather_kernel, plan, len(arrays)), out_s...  2.28 us
    pallas_call x4, Pallas kernels, finish(): pl.pallas_call(finish_kernel, out_shape=jax.ShapeDtypeStruct(halo.shape,...  1.56 us
    pallas_call x1, Pallas kernels, image_mid(): pl.pallas_call(image_mid_kernel, out_shape=jax.ShapeDtypeStruct(shape, jn...  1.42 us
  transfers between devices with their start and end apart: 10, of which 5 were waited for; matrix products, arithmetic and copies ran while one was open for 0% of the time, Pallas kernels for 25%

profile of v7, /device:TPU:1, one launch (start us, length us, event | category | flops | bytes accessed | tf_op | source)
XLA Modules:
  0.0 68.1 jit_solution(17777693181393259295)
XLA Ops:
  0.6 1.1 %gather.2.out.prev_out = f32[2,4,64,256]{3,2,1,0:T(8,128)S(1)} custom-call(f32[8,64,256]{2,1,0:T(8,128)} %bitcast.20, f32[8,64,256]{2,1,0:T(8,128)} %bitcast.22), custom_call_target="tpu_custom_call" | custom-call | flops 10000000000 | bytes 20000000 | tf_op jit(solution)/shard_map/gather/pallas_call | solution.py:94
  1.8 0.0 copy-start
  1.8 0.0 copy-start.1
  1.8 4.7 %collective-permute-start = (f32[2,4,64,256]{3,2,1,0:T(8,128)S(1)}, f32[2,4,64,256]{3,2,1,0:T(8,128)S(1)}, u32[]{:S(2)}, u32[]{:S(2)}) collective-permute-start(f32[2,4,64,256]{3,2,1,0:T(8,128)S(1)} %gather.2.out.prev_out), channel_id=1, source_target_pairs={{1,2},{3,4},{5,6},{7,8},{9,10},{11,12},{13,14},{2,1},{4,3},{6,5},{... | collective-permute-start | bytes 1572872 | tf_op jit(solution)/shard_map/ppermute | solution.py:456
  6.5 1.1 %gather.3.inn.prev_inn = f32[2,4,64,256]{3,2,1,0:T(8,128)S(1)} custom-call(f32[8,64,256]{2,1,0:T(8,128)} %bitcast.21, f32[8,64,256]{2,1,0:T(8,128)} %bitcast.23), custom_call_target="tpu_custom_call" | custom-call | flops 10000000000 | bytes 20000000 | tf_op jit(solution)/shard_map/gather/pallas_call | solution.py:94
  7.6 0.1 collective-permute-start.2
  7.7 0.0 copy-done
  7.7 0.0 copy-done.1
  7.7 2.6 %first.1 = (f32[2,4,64,256]{3,2,1,0:T(8,128)S(1)}, f32[3,4,64,256]{3,2,1,0:T(8,128)S(1)}, f32[3,4,64,256]{3,2,1,0:T(8,128)S(1)}, f32[2,4,64,256]{3,2,1,0:T(8,128)S(1)}) custom-call(f32[2,4,64,256]{3,2,1,0:T(8,128)S(1)} %gather.2.out.prev_out, f32[2,4,64,256]{3,2,1,0:T(8,128)S(1)} %gather.3.inn.prev_inn, bf16[2,256,256]{2,1,0:T(8,128)(2,1)S(1)} %copy-done, ...), custom_call_target="tpu_custom_call" | custom-call | flops 10000000000 | bytes 20000000 | tf_op jit(solution)/shard_map/first/pallas_call | solution.py:210
  10.3 0.0 collective-permute-done.2.near
  10.3 1.0 %inner.4.inn.prev_inn = f32[2,4,64,256]{3,2,1,0:T(8,128)S(1)} custom-call(f32[2,4,64,256]{3,2,1,0:T(8,128)S(1)} %gather.3.inn.prev_inn, f32[2,4,64,256]{3,2,1,0:T(8,128)S(1)} %gather.2.out.prev_out, f32[2,4,64,256]{3,2,1,0:T(8,128)S(1)} %collective-permute-done.2.near, f32[2,4,64,256]{3,2,1,0:T(8,128)S(1)} %get-tuple-element.13.prev_inn, ...), custom_call_target="tpu_custom_call" | custom-call | flops 1 | bytes 1 | tf_op jit(solution)/shard_map/inner/pallas_call | solution.py:224
  11.3 0.5 collective-permute-start.3
  11.8 6.4 %collective-permute-done.halo = f32[2,4,64,256]{3,2,1,0:T(8,128)S(1)} collective-permute-done((f32[2,4,64,256]{3,2,1,0:T(8,128)S(1)}, f32[2,4,64,256]{3,2,1,0:T(8,128)S(1)}, u32[]{:S(2)}, u32[]{:S(2)}) %collective-permute-start) | collective-permute-done | bytes 524320 | tf_op jit(solution)/shard_map/ppermute | solution.py:456
  18.2 0.4 finish.4.out.prev_out
  18.6 4.4 %collective-permute-start.1 = (f32[2,4,64,256]{3,2,1,0:T(8,128)S(1)}, f32[2,4,64,256]{3,2,1,0:T(8,128)S(1)}, u32[]{:S(2)}, u32[]{:S(2)}) collective-permute-start(f32[2,4,64,256]{3,2,1,0:T(8,128)S(1)} %finish.4.out.prev_out), channel_id=1, source_target_pairs={{1,2},{3,4},{5,6},{7,8},{9,10},{11,12},{13,14},{2,1},{4,3},{6,5},{... | collective-permute-start | bytes 1572872 | tf_op jit(solution)/shard_map/ppermute | solution.py:456
  23.0 0.8 %base.3 = f32[2,4,64,256]{3,2,1,0:T(8,128)S(1)} custom-call(f32[2,4,64,256]{3,2,1,0:T(8,128)S(1)} %finish.4.out.prev_out, f32[2,4,64,256]{3,2,1,0:T(8,128)S(1)} %inner.4.inn.prev_inn, f32[2,4,64,256]{3,2,1,0:T(8,128)S(1)} %gather.2.out.prev_out, f32[3,4,64,256]{3,2,1,0:T(8,128)S(1)} %get-tuple-element.12.coef.coef_out, bf16[2,256,256]{2,1,0:T(8,128)(2,1)S(1)} %copy-done, ...), custom_call_target="tpu_custom_call" | custom-call | flops 1 | bytes 1 | tf_op jit(solution)/shard_map/base/pallas_call | solution.py:224
  23.8 0.0 collective-permute-done.3.near
  23.9 1.0 %inner.5.other.inn.prev_inn.in2 = f32[2,4,64,256]{3,2,1,0:T(8,128)S(1)} custom-call(f32[2,4,64,256]{3,2,1,0:T(8,128)S(1)} %inner.4.inn.prev_inn, f32[2,4,64,256]{3,2,1,0:T(8,128)S(1)} %finish.4.out.prev_out, f32[2,4,64,256]{3,2,1,0:T(8,128)S(1)} %collective-permute-done.3.near, f32[2,4,64,256]{3,2,1,0:T(8,128)S(1)} %gather.3.inn.prev_inn, ...), custom_call_target="tpu_custom_call" | custom-call | flops 1 | bytes 1 | tf_op jit(solution)/shard_map/inner/pallas_call | solution.py:224
  24.8 0.1 collective-permute-start.5
  24.9 6.1 %collective-permute-done.1.halo = f32[2,4,64,256]{3,2,1,0:T(8,128)S(1)} collective-permute-done((f32[2,4,64,256]{3,2,1,0:T(8,128)S(1)}, f32[2,4,64,256]{3,2,1,0:T(8,128)S(1)}, u32[]{:S(2)}, u32[]{:S(2)}) %collective-permute-start.1) | collective-permute-done | bytes 524320 | tf_op jit(solution)/shard_map/ppermute | solution.py:456
  31.0 0.4 finish.5.half.out.prev_out.out2
  31.4 4.4 %collective-permute-start.4 = (f32[2,4,64,256]{3,2,1,0:T(8,128)S(1)}, f32[2,4,64,256]{3,2,1,0:T(8,128)S(1)}, u32[]{:S(2)}, u32[]{:S(2)}) collective-permute-start(f32[2,4,64,256]{3,2,1,0:T(8,128)S(1)} %finish.5.half.out.prev_out.out2), channel_id=1, source_target_pairs={{1,2},{3,4},{5,6},{7,8},{9,10},{11,12},{13,14},{2,1},{4,3},{6,5},{... | collective-permute-start | bytes 1572872 | tf_op jit(solution)/shard_map/ppermute | solution.py:456
  35.8 1.0 %base.4 = f32[2,4,64,256]{3,2,1,0:T(8,128)S(1)} custom-call(f32[2,4,64,256]{3,2,1,0:T(8,128)S(1)} %finish.5.half.out.prev_out.out2, f32[2,4,64,256]{3,2,1,0:T(8,128)S(1)} %inner.5.other.inn.prev_inn.in2, f32[2,4,64,256]{3,2,1,0:T(8,128)S(1)} %finish.4.out.prev_out, f32[3,4,64,256]{3,2,1,0:T(8,128)S(1)} %get-tuple-element.12.coef.coef_out, ...), custom_call_target="tpu_custom_call" | custom-call | flops 1 | bytes 1 | tf_op jit(solution)/shard_map/base/pallas_call | solution.py:224
  36.8 0.0 collective-permute-done.5.near.hal2
  36.8 0.0 slice-start
  36.9 1.2 %inner.6.inn = f32[2,4,64,256]{3,2,1,0:T(8,128)S(1)} custom-call(f32[2,4,64,256]{3,2,1,0:T(8,128)S(1)} %inner.5.other.inn.prev_inn.in2, f32[2,4,64,256]{3,2,1,0:T(8,128)S(1)} %finish.5.half.out.prev_out.out2, f32[2,4,64,256]{3,2,1,0:T(8,128)S(1)} %collective-permute-done.5.near.hal2, f32[2,4,64,256]{3,2,1,0:T(8,128)S(1)} %inner.4.inn.prev_inn, ...), custom_call_target="tpu_custom_call" | custom-call | flops 1 | bytes 1 | tf_op jit(solution)/shard_map/inner/pallas_call | solution.py:224
  38.1 0.1 collective-permute-start.6
  38.1 4.8 %collective-permute-done.4.halo = f32[2,4,64,256]{3,2,1,0:T(8,128)S(1)} collective-permute-done((f32[2,4,64,256]{3,2,1,0:T(8,128)S(1)}, f32[2,4,64,256]{3,2,1,0:T(8,128)S(1)}, u32[]{:S(2)}, u32[]{:S(2)}) %collective-permute-start.4) | collective-permute-done | bytes 524320 | tf_op jit(solution)/shard_map/ppermute | solution.py:456
  42.9 0.4 finish.6.out
  43.3 0.0 copy-start.3
  43.3 0.0 slice-start.1
  43.4 0.0 copy-start.2
  43.4 4.5 %collective-permute-start.7 = (f32[2,4,64,256]{3,2,1,0:T(8,128)S(1)}, f32[2,4,64,256]{3,2,1,0:T(8,128)S(1)}, u32[]{:S(2)}, u32[]{:S(2)}) collective-permute-start(f32[2,4,64,256]{3,2,1,0:T(8,128)S(1)} %finish.6.out), channel_id=1, source_target_pairs={{1,2},{3,4},{5,6},{7,8},{9,10},{11,12},{13,14},{2,1},{4,3},{6,5},{... | collective-permute-start | bytes 1572872 | tf_op jit(solution)/shard_map/ppermute | solution.py:456
  47.9 0.9 %base.5 = f32[2,4,64,256]{3,2,1,0:T(8,128)S(1)} custom-call(f32[2,4,64,256]{3,2,1,0:T(8,128)S(1)} %finish.6.out, f32[2,4,64,256]{3,2,1,0:T(8,128)S(1)} %inner.6.inn, f32[2,4,64,256]{3,2,1,0:T(8,128)S(1)} %finish.5.half.out.prev_out.out2, f32[3,4,64,256]{3,2,1,0:T(8,128)S(1)} %get-tuple-element.12.coef.coef_out, bf16[2,256,256]{2,1,0:T(8,128)(2,1)S(1)} %copy-done, ...), custom_call_target="tpu_custom_call" | custom-call | flops 1 | bytes 1 | tf_op jit(solution)/shard_map/base/pallas_call | solution.py:224
  48.8 0.0 collective-permute-done.6.near
  48.8 1.0 %inner.7.in4.other = f32[2,4,64,256]{3,2,1,0:T(8,128)S(1)} custom-call(f32[2,4,64,256]{3,2,1,0:T(8,128)S(1)} %inner.6.inn, f32[2,4,64,256]{3,2,1,0:T(8,128)S(1)} %finish.6.out, f32[2,4,64,256]{3,2,1,0:T(8,128)S(1)} %collective-permute-done.6.near, f32[2,4,64,256]{3,2,1,0:T(8,128)S(1)} %inner.5.other.inn.prev_inn.in2, ...), custom_call_target="tpu_custom_call" | custom-call | flops 1 | bytes 1 | tf_op jit(solution)/shard_map/inner/pallas_call | solution.py:224
  49.8 0.1 collective-permute-start.8
  49.9 5.1 %collective-permute-done.7.halo = f32[2,4,64,256]{3,2,1,0:T(8,128)S(1)} collective-permute-done((f32[2,4,64,256]{3,2,1,0:T(8,128)S(1)}, f32[2,4,64,256]{3,2,1,0:T(8,128)S(1)}, u32[]{:S(2)}, u32[]{:S(2)}) %collective-permute-start.7) | collective-permute-done | bytes 524320 | tf_op jit(solution)/shard_map/ppermute | solution.py:456
  55.0 0.4 finish.7.out4.half
  55.4 4.4 %collective-permute-start.9 = (f32[2,4,64,256]{3,2,1,0:T(8,128)S(1)}, f32[2,4,64,256]{3,2,1,0:T(8,128)S(1)}, u32[]{:S(2)}, u32[]{:S(2)}) collective-permute-start(f32[2,4,64,256]{3,2,1,0:T(8,128)S(1)} %finish.7.out4.half), channel_id=1, source_target_pairs={{1,2},{3,4},{5,6},{7,8},{9,10},{11,12},{13,14},{2,1},{4,3},{6,5},{... | collective-permute-start | bytes 1572872 | tf_op jit(solution)/shard_map/ppermute | solution.py:456
  59.8 0.0 copy-done.3
  59.8 0.1 fusion.mute
  59.9 0.0 slice-done
  59.9 0.0 slice-done.1
  60.0 0.0 copy-done.2
  60.0 1.4 %image_mid.1.part = f32[9,4,64,256]{3,2,1,0:T(8,128)S(1)} custom-call(f32[9,8,64,256]{3,2,1,0:T(8,128)S(1)} %bitcast.16, s32[9]{0:T(128)S(1)} %copy-done.2, f32[8,64,256]{2,1,0:T(8,128)S(1)} %fusion.mute, f32[2,4,64,256]{3,2,1,0:T(8,128)S(1)} %finish.5.half.out.prev_out.out2, f32[2,4,64,256]{3,2,1,0:T(8,128)S(1)} %inner.5.other.inn.prev_inn.in2, ...), custom_call_target="tpu_custom_call" | custom-call | flops 1 | bytes 1 | tf_op jit(solution)/shard_map/image_mid/pallas_call | solution.py:340
  61.4 0.0 collective-permute-done.8.hal4
  61.4 3.1 %image_main.1 = (f32[9,8,64,256]{3,2,1,0:T(8,128)}, f32[8,64,256]{2,1,0:T(8,128)}, f32[8,64,256]{2,1,0:T(8,128)}, s32[9,128]{1,0:T(8,128)S(1)}) custom-call(f32[9,8,64,256]{3,2,1,0:T(8,128)S(1)} %bitcast.17, f32[9,4,64,256]{3,2,1,0:T(8,128)S(1)} %image_mid.1.part, s32[9]{0:T(128)S(1)} %copy-done.2, f32[8,64,256]{2,1,0:T(8,128)S(1)} %fusion.mute, ...), custom_call_target="tpu_custom_call" | custom-call | flops 1 | bytes 1 | tf_op jit(solution)/shard_map/image_main/pallas_call | solution.py:401
  64.6 2.3 %collective-permute-done.9.halo = f32[2,4,64,256]{3,2,1,0:T(8,128)S(1)} collective-permute-done((f32[2,4,64,256]{3,2,1,0:T(8,128)S(1)}, f32[2,4,64,256]{3,2,1,0:T(8,128)S(1)}, u32[]{:S(2)}, u32[]{:S(2)}) %collective-permute-start.9) | collective-permute-done | bytes 524320 | tf_op jit(solution)/shard_map/ppermute | solution.py:456
  66.9 1.2 %image_last.1 = f32[9,8,64,256]{3,2,1,0:T(8,128)} custom-call(f32[9,8,64,256]{3,2,1,0:T(8,128)} %get-tuple-element.15.image_old, f32[9,4,64,256]{3,2,1,0:T(8,128)S(1)} %image_mid.1.part, s32[9,128]{1,0:T(8,128)S(1)} %get-tuple-element.16.table, f32[8,64,256]{2,1,0:T(8,128)S(1)} %fusion.mute, ...), custom_call_target="tpu_custom_call", output_to_operand_aliasing={{}: (0, {})} | custom-call | flops 1 | bytes 1 | tf_op jit(solution)/shard_map/image_last/pallas_call | solution.py:437
  (1 shorter events, 0.0 us)
Async XLA Ops:
  1.8 5.9 %copy-start = (bf16[2,256,256]{2,1,0:T(8,128)(2,1)S(1)}, bf16[2,256,256]{2,1,0:T(8,128)(2,1)}, u32[]{:S(2)}) copy-start(bf16[2,256,256]{2,1,0:T(8,128)(2,1)} %constant.4.clone.wz) | copy-start | bytes 786436
  1.8 5.9 %copy-start.1 = (bf16[256,256]{1,0:T(8,128)(2,1)S(1)}, bf16[256,256]{1,0:T(8,128)(2,1)}, u32[]{:S(2)}) copy-start(bf16[256,256]{1,0:T(8,128)(2,1)} %constant.5.clone.wy) | copy-start | bytes 393220
  1.8 16.4 %collective-permute-start = (f32[2,4,64,256]{3,2,1,0:T(8,128)S(1)}, f32[2,4,64,256]{3,2,1,0:T(8,128)S(1)}, u32[]{:S(2)}, u32[]{:S(2)}) collective-permute-start(f32[2,4,64,256]{3,2,1,0:T(8,128)S(1)} %gather.2.out.prev_out), channel_id=1, source_target_pairs={{1,2},{3,4},{5,6},{7,8},{9,10},{11,12},{13,14},{2,1},{4,3},{6,5},{... | collective-permute-start | bytes 1572872 | tf_op jit(solution)/shard_map/ppermute | solution.py:456
  7.6 2.7 %collective-permute-start.2 = (f32[2,4,64,256]{3,2,1,0:T(8,128)S(1)}, f32[2,4,64,256]{3,2,1,0:T(8,128)S(1)}, u32[]{:S(2)}, u32[]{:S(2)}) collective-permute-start(f32[2,4,64,256]{3,2,1,0:T(8,128)S(1)} %gather.3.inn.prev_inn), channel_id=1, source_target_pairs={{0,1},{1,0},{2,3},{3,2},{4,5},{5,4},{6,7},{7,6},{8,9},{9,8},{10,11... | collective-permute-start | bytes 1572872 | tf_op jit(solution)/shard_map/ppermute | solution.py:460
  11.3 12.5 %collective-permute-start.3 = (f32[2,4,64,256]{3,2,1,0:T(8,128)S(1)}, f32[2,4,64,256]{3,2,1,0:T(8,128)S(1)}, u32[]{:S(2)}, u32[]{:S(2)}) collective-permute-start(f32[2,4,64,256]{3,2,1,0:T(8,128)S(1)} %inner.4.inn.prev_inn), channel_id=1, source_target_pairs={{0,1},{1,0},{2,3},{3,2},{4,5},{5,4},{6,7},{7,6},{8,9},{9,8},{10,11... | collective-permute-start | bytes 1572872 | tf_op jit(solution)/shard_map/ppermute | solution.py:460
  18.6 12.4 %collective-permute-start.1 = (f32[2,4,64,256]{3,2,1,0:T(8,128)S(1)}, f32[2,4,64,256]{3,2,1,0:T(8,128)S(1)}, u32[]{:S(2)}, u32[]{:S(2)}) collective-permute-start(f32[2,4,64,256]{3,2,1,0:T(8,128)S(1)} %finish.4.out.prev_out), channel_id=1, source_target_pairs={{1,2},{3,4},{5,6},{7,8},{9,10},{11,12},{13,14},{2,1},{4,3},{6,5},{... | collective-permute-start | bytes 1572872 | tf_op jit(solution)/shard_map/ppermute | solution.py:456
  24.8 12.0 %collective-permute-start.5 = (f32[2,4,64,256]{3,2,1,0:T(8,128)S(1)}, f32[2,4,64,256]{3,2,1,0:T(8,128)S(1)}, u32[]{:S(2)}, u32[]{:S(2)}) collective-permute-start(f32[2,4,64,256]{3,2,1,0:T(8,128)S(1)} %inner.5.other.inn.prev_inn.in2), channel_id=1, source_target_pairs={{0,1},{1,0},{2,3},{3,2},{4,5},{5,4},{6,7},{7,6},{8,9},{9,8},{10,11... | collective-permute-start | bytes 1572872 | tf_op jit(solution)/shard_map/ppermute | solution.py:460
  31.4 11.5 %collective-permute-start.4 = (f32[2,4,64,256]{3,2,1,0:T(8,128)S(1)}, f32[2,4,64,256]{3,2,1,0:T(8,128)S(1)}, u32[]{:S(2)}, u32[]{:S(2)}) collective-permute-start(f32[2,4,64,256]{3,2,1,0:T(8,128)S(1)} %finish.5.half.out.prev_out.out2), channel_id=1, source_target_pairs={{1,2},{3,4},{5,6},{7,8},{9,10},{11,12},{13,14},{2,1},{4,3},{6,5},{... | collective-permute-start | bytes 1572872 | tf_op jit(solution)/shard_map/ppermute | solution.py:456
  36.8 23.1 %slice-start = ((s8[4718592]{0:T(1024)(128)(4,1)}), s8[4194304]{0:T(1024)(128)(4,1)S(1)}, s32[]{:S(2)}) async-start(s8[4718592]{0:T(1024)(128)(4,1)} %bitcast.14), calls=%async_computation | async-start | bytes 8388608
  38.1 10.7 %collective-permute-start.6 = (f32[2,4,64,256]{3,2,1,0:T(8,128)S(1)}, f32[2,4,64,256]{3,2,1,0:T(8,128)S(1)}, u32[]{:S(2)}, u32[]{:S(2)}) collective-permute-start(f32[2,4,64,256]{3,2,1,0:T(8,128)S(1)} %inner.6.inn), channel_id=1, source_target_pairs={{0,1},{1,0},{2,3},{3,2},{4,5},{5,4},{6,7},{7,6},{8,9},{9,8},{10,11... | collective-permute-start | bytes 1572872 | tf_op jit(solution)/shard_map/ppermute | solution.py:460
  43.3 16.5 %copy-start.3 = (s32[1,8,64]{2,1,0:T(8,128)S(1)}, s32[1,8,64]{2,1,0:T(8,128)}, u32[]{:S(2)}) copy-start(s32[1,8,64]{2,1,0:T(8,128)} %param.19) | copy-start | bytes 6148
  43.3 16.6 %slice-start.1 = ((s8[4718592]{0:T(1024)(128)(4,1)}), s8[524288]{0:T(1024)(128)(4,1)S(1)}, s32[]{:S(2)}) async-start(s8[4718592]{0:T(1024)(128)(4,1)} %bitcast.14), calls=%async_computation.1 | async-start | bytes 1048576
  43.4 16.6 %copy-start.2 = (s32[9]{0:T(128)S(1)}, s32[9]{0:T(128)}, u32[]{:S(2)}) copy-start(s32[9]{0:T(128)} %offsets.3) | copy-start | bytes 112
  43.4 11.6 %collective-permute-start.7 = (f32[2,4,64,256]{3,2,1,0:T(8,128)S(1)}, f32[2,4,64,256]{3,2,1,0:T(8,128)S(1)}, u32[]{:S(2)}, u32[]{:S(2)}) collective-permute-start(f32[2,4,64,256]{3,2,1,0:T(8,128)S(1)} %finish.6.out), channel_id=1, source_target_pairs={{1,2},{3,4},{5,6},{7,8},{9,10},{11,12},{13,14},{2,1},{4,3},{6,5},{... | collective-permute-start | bytes 1572872 | tf_op jit(solution)/shard_map/ppermute | solution.py:456
  49.8 11.6 %collective-permute-start.8 = (f32[2,4,64,256]{3,2,1,0:T(8,128)S(1)}, f32[2,4,64,256]{3,2,1,0:T(8,128)S(1)}, u32[]{:S(2)}, u32[]{:S(2)}) collective-permute-start(f32[2,4,64,256]{3,2,1,0:T(8,128)S(1)} %inner.7.in4.other), channel_id=1, source_target_pairs={{0,1},{1,0},{2,3},{3,2},{4,5},{5,4},{6,7},{7,6},{8,9},{9,8},{10,11... | collective-permute-start | bytes 1572872 | tf_op jit(solution)/shard_map/ppermute | solution.py:460
  55.4 11.5 %collective-permute-start.9 = (f32[2,4,64,256]{3,2,1,0:T(8,128)S(1)}, f32[2,4,64,256]{3,2,1,0:T(8,128)S(1)}, u32[]{:S(2)}, u32[]{:S(2)}) collective-permute-start(f32[2,4,64,256]{3,2,1,0:T(8,128)S(1)} %finish.7.out4.half), channel_id=1, source_target_pairs={{1,2},{3,4},{5,6},{7,8},{9,10},{11,12},{13,14},{2,1},{4,3},{6,5},{... | collective-permute-start | bytes 1572872 | tf_op jit(solution)/shard_map/ppermute | solution.py:456
